TPU v7x, 128 devices: a whole 4x4x4 slice. The times are simulated.
128 devices in a mesh: row: 16 (over z, y_hi, core), col: 8 (over y_lo, x).
Axes of the slice: x: 4, y: 4 (y_hi: 2, y_lo: 2; y = y_hi * 2 + y_lo), z: 4, core: 2. Of those that a mesh axis runs over, the one named last changes fastest.
Arguments:
- layer_input: bfloat16 [2, 8192, 1024], P(None, 'row', 'col'), may hold values from -96 to 96
- out_grad: bfloat16 [2, 8192, 1024], P(None, 'row', 'col'), may hold values from -6 to 6
- token_route: int32 [2, 8192], P(None, 'row'), may hold values from 0 to 8191, as said below
- seq_lengths: int32 [2, 16, 4], P(None, 'row'), may hold values from 0 to 512, as said below
- positions: int32 [2, 8192], P(None, 'row'), may hold values from 0 to 3580, as said below
- attn_gain: bfloat16 [1024], replicated, may hold values from 0.099609375 to 1.8984375
- query_weight: bfloat16 [1024, 2048], P('row', 'col'), may hold values from -0.1875 to 0.1875
- key_weight: bfloat16 [1024, 1024], P('row', 'col'), may hold values from -0.1875 to 0.1875
- value_weight: bfloat16 [1024, 1024], P('row', 'col'), may hold values from -0.1875 to 0.1875
- query_gain: bfloat16 [128], replicated, may hold values from 0.099609375 to 1.8984375
- key_gain: bfloat16 [128], replicated, may hold values from 0.099609375 to 1.8984375
- out_weight: bfloat16 [2048, 1024], P('col', 'row'), may hold values from -0.5 to 0.5
- mlp_gain: bfloat16 [1024], replicated, may hold values from 0.099609375 to 1.8984375
- gate_weight: bfloat16 [1024, 3072], P('row', 'col'), may hold values from -0.1875 to 0.1875
- up_weight: bfloat16 [1024, 3072], P('row', 'col'), may hold values from -0.1875 to 0.1875
- down_weight: bfloat16 [3072, 1024], P('col', 'row'), may hold values from -0.109375 to 0.109375
Outputs:
- layer_output: bfloat16 [2, 8192, 1024], P(None, 'row', 'col')
- input_grad: bfloat16 [2, 8192, 1024], P(None, 'row', 'col')
- attn_gain_grad: float32 [1024], replicated
- query_grad: float32 [1024, 2048], P('row', 'col')
- key_grad: float32 [1024, 1024], P('row', 'col')
- value_grad: float32 [1024, 1024], P('row', 'col')
- query_gain_grad: float32 [128], replicated
- key_gain_grad: float32 [128], replicated
- out_proj_grad: float32 [2048, 1024], P('col', 'row')
- mlp_gain_grad: float32 [1024], replicated
- gate_grad: float32 [1024, 3072], P('row', 'col')
- up_grad: float32 [1024, 3072], P('row', 'col')
- down_grad: float32 [3072, 1024], P('col', 'row')
Inputs may be any that keep to these rules, and one draw needn't show every extreme that they name: Each row of token_route holds every number from 0 to 8191 once. Each aligned block of 512 entries holds the same number of entries of every group (g * 512 to (g + 1) * 512 - 1). `seq_lengths`: each row of 4 lengths sums to 512; nonzero lengths come first and zeros mark unused slots. Some row holds a single sequence of 512 tokens. Within each sequence of the group layout, positions rise by 1 to 3 from one token to the next.
All inputs are finite; a program needn't handle non-finite values.
Results may differ from a plain program's by a relative error of at most 0.018.
Values may be sent and summed in bfloat16 or wider, within the bound.
No kernel may reach another device: no remote copies, remote signals or barrier semaphores. Data moves between devices by JAX's collectives and lax.ppermute only.
A program may use at most 128 MiB of HBM per device.

v0:
```python
import functools
import math

import jax
import jax.numpy as jnp
from jax import lax
from jax.experimental import pallas as pl
from jax.experimental.pallas import tpu as pltpu
from jax.sharding import PartitionSpec as P

D = 1024
HEAD_SIZE = 128
EPSILON = 1e-06
ROPE_BASE = 1000000.0
NEGATIVE = -1e30
BOTH = ("row", "col")
ROWS = 16
TOK = 512
TILE = 256
SENT = 40
BF = jnp.bfloat16
F32 = jnp.float32
SCALE = 1.0 / math.sqrt(HEAD_SIZE)


def flat(row, col):
    return row * 8 + col


def spot(z, y, core, x):
    return flat(z * 4 + (y // 2) * 2 + core, (y % 2) * 4 + x)


SQUAD = [
    [flat(2 * k + core, 4 * y_lo + x) for k in range(8) for y_lo in range(2) for core in range(2)]
    for x in range(4)
]
SAME_X = [[flat(row, 4 * y_lo + x) for x in range(4)] for row in range(ROWS) for y_lo in range(2)]
TEAM = [[flat(row, 4 * y_lo + x) for y_lo in range(2) for row in range(ROWS)] for x in range(4)]


def moves(dz=0, dy=0, dcore=0, dx=0):
    return [
        (spot(z, y, core, x), spot((z + dz) % 4, (y + dy) % 4, core ^ dcore, (x + dx) % 4))
        for z in range(4)
        for y in range(4)
        for core in range(2)
        for x in range(4)
    ]


def shift(value, **step):
    return lax.ppermute(value, BOTH, moves(**step))


def dot(a, b, dims):
    return lax.dot_general(a, b, (dims, ((), ())), preferred_element_type=F32)


def nn(a, b):
    return dot(a, b, ((1,), (0,)))


def nt(a, b):
    return dot(a, b, ((1,), (1,)))


def tn(a, b):
    return dot(a, b, ((0,), (0,)))


def call(body, ins, outs, scratch, copies, flops, traffic, *args, limit=60):
    spaces = {"s": pltpu.SMEM, "v": pltpu.VMEM, "h": pl.ANY}
    return pl.pallas_call(
        body,
        out_shape=[jax.ShapeDtypeStruct(s, t) for _, s, t in outs],
        in_specs=[pl.BlockSpec(memory_space=spaces[k]) for k in ins],
        out_specs=[pl.BlockSpec(memory_space=spaces[k]) for k, _, _ in outs],
        scratch_shapes=[pltpu.VMEM(s, t) for s, t in scratch] + [pltpu.SemaphoreType.DMA((copies,))],
        compiler_params=pltpu.CompilerParams(vmem_limit_bytes=limit * 1024 * 1024),
        cost_estimate=pl.CostEstimate(flops=flops >> 6, bytes_accessed=traffic >> 6, transcendentals=0),
    )(*args)


class Mover:
    def __init__(self, sems):
        self.sems = sems
        self.used = 0

    def start(self, source, target):
        copy = pltpu.make_async_copy(source, target, self.sems.at[self.used])
        self.used += 1
        copy.start()
        return copy


def wait(copies):
    for copy in copies:
        copy.wait()


def ranks(row):
    column = jnp.transpose(jnp.broadcast_to(row, (8, TOK)))[:, 0:1]
    across = jnp.sum((column < row).astype(F32), axis=0, keepdims=True)
    down = jnp.sum((row < column).astype(F32), axis=1, keepdims=True)
    return column, across, down


def sort_body(route_ref, x_hbm, g_hbm, out_ref, x_ref, g_ref, sems):
    mover = Mover(sems)
    loads = [mover.start(x_hbm, x_ref), mover.start(g_hbm, g_ref)]
    for m in range(2):
        column, across, down = ranks(route_ref[m : m + 1, :].astype(F32))
        place = lax.broadcasted_iota(jnp.int32, (TOK, TOK), 0).astype(F32)
        pick = (place == across).astype(BF)
        slot = column - jnp.floor(column * (1.0 / TOK)) * TOK
        high = jnp.floor(slot * (1.0 / 16))
        low = slot - high * 16
        group = jnp.floor(down * (1.0 / 32))
        inner = down - group * 32
        lane = lax.broadcasted_iota(jnp.int32, (TOK, 128), 1).astype(F32)
        spread = jnp.where(lane == inner, high, jnp.where(lane == inner + 32, low, 0.0)).astype(BF)
        owner = jnp.floor(across * (1.0 / 32))
        member = (lax.broadcasted_iota(jnp.int32, (ROWS, TOK), 0).astype(F32) == owner).astype(BF)
        codes = nn(member, spread).astype(BF)
        out_ref[m, :, 64:72, :] = jnp.broadcast_to(codes[:, None, :], (ROWS, 8, 128))
        if m == 0:
            wait(loads)
        out_ref[m, :, 0:32, :] = nn(pick, x_ref[m]).astype(BF).reshape(ROWS, 32, 128)
        out_ref[m, :, 32:64, :] = nn(pick, g_ref[m]).astype(BF).reshape(ROWS, 32, 128)


def unsort_body(route_ref, home_hbm, y_ref, dx_ref, home_ref, sems):
    mover = Mover(sems)
    loads = [mover.start(home_hbm.at[:, m], home_ref.at[m]) for m in range(2)]
    for m in range(2):
        _, _, down = ranks(route_ref[m : m + 1, :].astype(F32))
        lane = lax.broadcasted_iota(jnp.int32, (TOK, TOK), 1).astype(F32)
        pick = (lane == down).astype(BF)
        loads[m].wait()
        total = home_ref[m, :, 0, 0:32, :].astype(F32)
        for x in range(1, 4):
            total = total + home_ref[m, :, x, 0:32, :].astype(F32)
        dx_ref[m] = nn(pick, total.astype(BF).reshape(TOK, 128)).astype(BF)
        output = home_ref[m, :, :, 32:40, :].astype(F32).reshape(TOK, 128).astype(BF)
        y_ref[m] = nn(pick, output).astype(BF)


def features_of(mover, blocks, x, full_ref):
    return [
        mover.start(block.at[y], full_ref.at[:, mine(lax.rem(x + 4 - k, 4), y)])
        for k, block in enumerate(blocks)
        for y in range(2)
    ]


def features_in_order(mover, blocks, full_ref):
    return [
        mover.start(blocks.at[k, y], full_ref.at[:, pl.ds(y * 512 + k * 128, 128)])
        for k in range(4)
        for y in range(2)
    ]


def weight(w_ref, y, lanes):
    value = w_ref[(slice(None),) * (len(w_ref.shape) - 4) + (y, slice(None), slice(None), lanes)]
    return value.reshape(D, value.shape[-1])


def mine(x, y):
    return pl.ds(pl.multiple_of(y * 512 + x * 128, 128), 128)


def split_features(part_ref, rows, send_ref):
    for k in range(4):
        for y in range(2):
            lanes = slice(y * 512 + k * 128, y * 512 + k * 128 + 128)
            send_ref[k, y, rows, :] = part_ref[:, lanes].astype(BF)


def merge_body(got_ref, base_ref, total_ref, wide_ref, sems):
    for y in range(2):
        total = base_ref[y].astype(F32)
        for k in range(4):
            total = total + got_ref[k, y].astype(F32)
        total_ref[y] = total
        for k in range(4):
            wide_ref[k, y] = total.astype(BF)


def sent_tiles(send_ref, send_hbm, sems):
    return [
        pltpu.make_async_copy(
            send_ref.at[:, :, pl.ds(i * TILE, TILE)], send_hbm.at[:, :, pl.ds(i * TILE, TILE)], sems.at[SENT + i]
        )
        for i in range(TOK // TILE)
    ]


def norm_rope(proj, gain, cosine, sine):
    inv = lax.rsqrt(jnp.mean(proj * proj, axis=-1, keepdims=True) + EPSILON)
    normed = proj * inv * gain
    return normed * cosine + pltpu.roll(normed, 64, 1) * sine


def bias_of(table_ref, bias_ref):
    columns = jnp.transpose(table_ref[...])
    slot_row = table_ref[0:1, :]
    allowed = (slot_row <= columns[:, 0:1]) & (slot_row >= columns[:, 1:2])
    bias_ref[...] = jnp.where(allowed, 0.0, NEGATIVE)


def tile(i):
    return pl.ds(pl.multiple_of(i * TILE, TILE), TILE)


def attend_body(
    x_hbm, w_hbm, table_hbm, rope_hbm, gain_hbm,
    send_hbm, full_hbm, n_hbm, proj_hbm, q_hbm, k_hbm, v_hbm, a_hbm, lse_hbm,
    full_ref, w_ref, table_ref, rope_ref, gain_ref, bias_ref, part_ref, n_ref, proj_ref, q_ref, k_ref, v_ref, a_ref,
    lse_ref, send_ref, sems,
):
    mover = Mover(sems)
    cut = pl.ds(0, 512)
    rest = pl.ds(512, 256)
    first = features_in_order(mover, x_hbm, full_ref) + [mover.start(gain_hbm, gain_ref)]
    load_table = mover.start(table_hbm, table_ref)
    loads = [
        mover.start(w_hbm.at[:, :, :, :, cut], w_ref.at[:, :, :, :, cut]),
        mover.start(rope_hbm, rope_ref),
    ]
    load_rest = mover.start(w_hbm.at[:, :, :, :, rest], w_ref.at[:, :, :, :, rest])
    load_table.wait()
    bias_of(table_ref, bias_ref)
    wait(first)
    stores = [mover.start(full_ref, full_hbm)]

    def norm(i, carry):
        rows = tile(i)
        value = full_ref[rows, :].astype(F32)
        inv = lax.rsqrt(jnp.mean(value * value, axis=-1, keepdims=True) + EPSILON)
        n_ref[rows, :] = (value * inv * gain_ref[0:1, :]).astype(BF)
        return carry

    lax.fori_loop(0, TOK // TILE, norm, 0)
    stores.append(mover.start(n_ref, n_hbm))
    wait(loads)

    def project(i, carry):
        rows = tile(i)
        cosine, sine = rope_ref[rows, 0:128], rope_ref[rows, 128:256]
        for y in range(2):
            out = nn(n_ref[rows, :], weight(w_ref, y, slice(0, 512)))
            proj_ref[y, rows, :] = out[:, 0:384]
            for h in range(2):
                lanes = slice(h * 128, h * 128 + 128)
                q_ref[y, rows, lanes] = norm_rope(
                    out[:, lanes], gain_ref[2:3, 0:128], cosine, sine
                ).astype(BF)
            k_ref[y, rows, :] = norm_rope(
                out[:, 256:384], gain_ref[2:3, 128:256], cosine, sine
            ).astype(BF)
            v_ref[y, rows, :] = out[:, 384:512].astype(BF)
        return carry

    lax.fori_loop(0, TOK // TILE, project, 0)
    stores += [
        mover.start(proj_ref, proj_hbm),
        mover.start(q_ref, q_hbm),
        mover.start(k_ref, k_hbm),
        mover.start(v_ref, v_hbm),
    ]
    load_rest.wait()

    def attend(i, carry):
        rows = tile(i)
        bias = bias_ref[rows, :]
        lane = lax.broadcasted_iota(jnp.int32, (TILE, 128), 1)
        logs = jnp.zeros((TILE, 128), F32)
        for y in range(2):
            for h in range(2):
                lanes = slice(h * 128, h * 128 + 128)
                scores = nt(q_ref[y, rows, lanes], k_ref[y]) * SCALE + bias
                top = jnp.max(scores, axis=-1, keepdims=True)
                power = jnp.exp(scores - top)
                total = jnp.sum(power, axis=-1, keepdims=True)
                weights = (power * (1.0 / total)).astype(BF)
                a_ref[y, rows, lanes] = nn(weights, v_ref[y]).astype(BF)
                logs = jnp.where(lane == y * 2 + h, top + jnp.log(total), logs)
        lse_ref[rows, :] = logs
        return carry

    lax.fori_loop(0, TOK // TILE, attend, 0)
    stores += [mover.start(a_ref, a_hbm), mover.start(lse_ref, lse_hbm)]

    def leave(i, carry):
        rows = tile(i)
        part_ref[...] = nt(a_ref[0, rows, :], weight(w_ref, 0, slice(512, 768))) + nt(
            a_ref[1, rows, :], weight(w_ref, 1, slice(512, 768))
        )
        split_features(part_ref, rows, send_ref)
        pltpu.make_async_copy(send_ref.at[:, :, rows], send_hbm.at[:, :, rows], sems.at[SENT + i]).start()
        return carry

    lax.fori_loop(0, TOK // TILE, leave, 0)
    wait(stores + sent_tiles(send_ref, send_hbm, sems))


def feed_body(
    where_ref, h_hbm, g0, g1, g2, g3, w_hbm, gain_hbm,
    send_hbm, dy_hbm, n_hbm, hid_hbm, dgu_hbm, sum_ref,
    full_ref, w_ref, part_ref, gain_ref, dy_ref, n_ref, hid_ref, dgu_ref, send_ref, sems,
):
    mover = Mover(sems)
    cut = pl.ds(0, 768)
    rest = pl.ds(768, 384)
    loads = features_in_order(mover, h_hbm, full_ref)
    loads.append(mover.start(gain_hbm, gain_ref))
    loads.append(mover.start(w_hbm.at[:, :, :, :, cut], w_ref.at[:, :, :, :, cut]))
    later = features_of(mover, (g0, g1, g2, g3), where_ref[0], dy_ref)
    later.append(mover.start(w_hbm.at[:, :, :, :, rest], w_ref.at[:, :, :, :, rest]))
    sum_ref[...] = jnp.zeros_like(sum_ref)
    wait(loads + later)
    stores = [mover.start(dy_ref, dy_hbm)]

    def step(i, carry):
        rows = tile(i)
        gain = gain_ref[1:2, :]
        value = full_ref[rows, :].astype(F32)
        inv = lax.rsqrt(jnp.mean(value * value, axis=-1, keepdims=True) + EPSILON)
        hat = value * inv
        normed = (hat * gain).astype(BF)
        n_ref[rows, :] = normed
        delta = dy_ref[rows, :]
        for y in range(2):
            gate = nn(normed, weight(w_ref, y, slice(0, 384)))
            up = nn(normed, weight(w_ref, y, slice(384, 768)))
            down = nn(delta, weight(w_ref, y, slice(768, 1152)))
            sigma = jax.nn.sigmoid(gate)
            act = gate * sigma
            hid_ref[y, rows, :] = (act * up).astype(BF)
            dgu_ref[y, rows, 0:384] = (down * up * sigma * (1.0 + gate * (1.0 - sigma))).astype(BF)
            dgu_ref[y, rows, 384:768] = (down * act).astype(BF)
            out = nt(dgu_ref[y, rows, :], weight(w_ref, y, slice(0, 768)))
            if y == 0:
                part_ref[...] = out
            else:
                out = part_ref[...] + out
                sum_ref[0:1, :] += jnp.sum(out * hat, axis=0, keepdims=True)
                scaled = out * gain
                inner = jnp.mean(scaled * hat, axis=-1, keepdims=True)
                part_ref[...] = inv * (scaled - hat * inner)
        split_features(part_ref, rows, send_ref)
        pltpu.make_async_copy(send_ref.at[:, :, rows], send_hbm.at[:, :, rows], sems.at[SENT + i]).start()
        pltpu.make_async_copy(n_ref.at[rows], n_hbm.at[rows], sems.at[SENT + 2 + i]).start()
        pltpu.make_async_copy(hid_ref.at[:, rows], hid_hbm.at[:, rows], sems.at[SENT + 4 + i]).start()
        pltpu.make_async_copy(dgu_ref.at[:, rows], dgu_hbm.at[:, rows], sems.at[SENT + 6 + i]).start()
        return carry

    lax.fori_loop(0, TOK // TILE, step, 0)
    for i in range(TOK // TILE):
        rows = pl.ds(i * TILE, TILE)
        stores.append(pltpu.make_async_copy(n_ref.at[rows], n_hbm.at[rows], sems.at[SENT + 2 + i]))
        stores.append(pltpu.make_async_copy(hid_ref.at[:, rows], hid_hbm.at[:, rows], sems.at[SENT + 4 + i]))
        stores.append(pltpu.make_async_copy(dgu_ref.at[:, rows], dgu_hbm.at[:, rows], sems.at[SENT + 6 + i]))
    wait(stores + sent_tiles(send_ref, send_hbm, sems))


def store_grad(value_ref, core, chunk, y, lanes, keep_ref, give_ref):
    for k in range(2):
        kept = pl.multiple_of((k * 2 + core) * 64, 64)
        given = pl.multiple_of((k * 2 + 1 - core) * 64, 64)
        keep_ref[(chunk * 2 + k) * 2 + y, 0:64, lanes] = value_ref[pl.ds(kept, 64), :]
        give_ref[(chunk * 2 + k) * 2 + y, 0:64, lanes] = value_ref[pl.ds(given, 64), :]


def feed_grad_body(
    where_ref, hid_hbm, dgu_hbm, n_hbm, dy_hbm, w_hbm, resid_hbm,
    quarter_hbm, keep_hbm, give_hbm,
    hid_ref, dgu_ref, n_ref, dy_ref, w_ref, resid_ref, part_ref, wide_ref, thin_ref, stage_ref, quarter_ref, keep_ref,
    give_ref, sems,
):
    x, core = where_ref[0], where_ref[3]
    mover = Mover(sems)
    first = [
        mover.start(hid_hbm, hid_ref),
        mover.start(w_hbm.at[:, :, :, :, pl.ds(768, 384)], w_ref),
        mover.start(resid_hbm, resid_ref),
    ]
    loads = [
        mover.start(n_hbm, n_ref),
        mover.start(dgu_hbm, dgu_ref),
        mover.start(dy_hbm, dy_ref),
    ]
    wait(first)

    def step(i, carry):
        rows = tile(i)
        part_ref[...] = nt(hid_ref[0, rows, :], weight(w_ref, 0, slice(0, 384))) + nt(
            hid_ref[1, rows, :], weight(w_ref, 1, slice(0, 384))
        )
        for y in range(2):
            part_ref[:, mine(x, y)] += resid_ref[y, rows, :]
        places = pl.ds(pl.multiple_of(i * (TILE // 32), TILE // 32), TILE // 32)
        stage_ref[places] = part_ref[...].reshape(TILE // 32, 4, 8, D)
        return carry

    lax.fori_loop(0, TOK // TILE, step, 0)
    for k in range(4):
        quarter_ref[k] = stage_ref[:, k].reshape(128, D).astype(BF)
    stores = [mover.start(quarter_ref, quarter_hbm)]
    wait(loads)
    for j in range(4):
        lanes = slice(j * 256, j * 256 + 256)
        normed = jnp.transpose(n_ref[:, lanes])
        delta = jnp.transpose(dy_ref[:, lanes])
        for y in range(2):
            wide_ref[...] = nn(normed, dgu_ref[y]).astype(BF)
            store_grad(wide_ref, core, j, y, slice(0, 768), keep_ref, give_ref)
            thin_ref[...] = nn(delta, hid_ref[y]).astype(BF)
            store_grad(thin_ref, core, j, y, slice(768, 1152), keep_ref, give_ref)
        done = pl.ds(j * 4, 4)
        stores.append(mover.start(give_ref.at[done], give_hbm.at[done]))
        stores.append(mover.start(keep_ref.at[done], keep_hbm.at[done]))
    wait(stores)


def attend_back_body(
    where_ref, d_hbm, w_hbm, proj_hbm, q_hbm, k_hbm, v_hbm, lse_hbm, table_hbm,
    rope_hbm, gain_hbm, full_hbm, resid_hbm,
    back_hbm, dproj_hbm, delta_hbm, head_ref, sum_ref,
    delta_ref, w_ref, proj_ref, q_ref, k_ref, v_ref, lse_ref, table_ref, rope_ref, gain_ref, bias_ref, dk_ref, dv_ref,
    da_ref, dproj_ref, full_ref, resid_ref, part_ref, back_ref, sems,
):
    x = where_ref[0]
    mover = Mover(sems)
    loads = [
        mover.start(table_hbm, table_ref),
        mover.start(lse_hbm, lse_ref),
        mover.start(q_hbm, q_ref),
        mover.start(k_hbm, k_ref),
        mover.start(v_hbm, v_ref),
    ]
    loads += features_in_order(mover, d_hbm, delta_ref)
    loads.append(mover.start(w_hbm.at[:, :, :, :, pl.ds(512, 256)], w_ref.at[:, :, :, :, pl.ds(512, 256)]))
    loads += [
        mover.start(proj_hbm, proj_ref),
        mover.start(rope_hbm, rope_ref),
        mover.start(gain_hbm, gain_ref),
    ]
    more = [
        mover.start(w_hbm.at[:, :, :, :, pl.ds(0, 512)], w_ref.at[:, :, :, :, pl.ds(0, 512)]),
        mover.start(full_hbm, full_ref),
        mover.start(resid_hbm, resid_ref),
    ]
    head_ref[...] = jnp.zeros_like(head_ref)
    sum_ref[...] = jnp.zeros_like(sum_ref)
    dk_ref[...] = jnp.zeros_like(dk_ref)
    dv_ref[...] = jnp.zeros_like(dv_ref)
    loads[0].wait()
    bias_of(table_ref, bias_ref)
    wait(loads[1:])
    stores = [mover.start(delta_ref, delta_hbm)]

    def back(rotated, proj, gain, rows, at):
        turned = rotated * rope_ref[rows, 0:128] - pltpu.roll(rotated, 64, 1) * rope_ref[rows, 128:256]
        inv = lax.rsqrt(jnp.mean(proj * proj, axis=-1, keepdims=True) + EPSILON)
        hat = proj * inv
        head_ref[at : at + 1, :] += jnp.sum(turned * hat, axis=0, keepdims=True)
        scaled = turned * gain
        return (inv * (scaled - hat * jnp.mean(scaled * hat, axis=-1, keepdims=True))).astype(BF)

    def attend(i, carry):
        rows = tile(i)
        bias = bias_ref[rows, :]
        logs = lse_ref[rows, :]
        for y in range(2):
            da_ref[...] = nn(delta_ref[rows, :], weight(w_ref, y, slice(512, 768))).astype(BF)
            for h in range(2):
                lanes = slice(h * 128, h * 128 + 128)
                query = q_ref[y, rows, lanes]
                da = da_ref[:, lanes]
                scores = nt(query, k_ref[y]) * SCALE + bias
                soft = jnp.exp(scores - logs[:, y * 2 + h : y * 2 + h + 1])
                dp = nt(da, v_ref[y])
                dv_ref[y] += tn(da, soft.astype(BF))
                ds = (soft * (dp - jnp.sum(dp * soft, axis=-1, keepdims=True))).astype(BF)
                dk_ref[y] += tn(query, ds)
                dq = nn(ds, k_ref[y]) * SCALE
                dproj_ref[y, rows, lanes] = back(
                    dq, proj_ref[y, rows, lanes], gain_ref[2:3, 0:128], rows, 0
                )
        return carry

    lax.fori_loop(0, TOK // TILE, attend, 0)

    for i in range(TOK // TILE):
        rows = pl.ds(i * TILE, TILE)
        for y in range(2):
            dproj_ref[y, rows, 256:384] = back(
                jnp.transpose(dk_ref[y, :, rows]) * SCALE, proj_ref[y, rows, 256:384], gain_ref[2:3, 128:256], rows, 1
            )
            dproj_ref[y, rows, 384:512] = jnp.transpose(dv_ref[y, :, rows]).astype(BF)
    stores.append(mover.start(dproj_ref, dproj_hbm))
    wait(more)
    for i in range(TOK // TILE):
        rows = pl.ds(i * TILE, TILE)
        value = full_ref[rows, :].astype(F32)
        inv = lax.rsqrt(jnp.mean(value * value, axis=-1, keepdims=True) + EPSILON)
        hat = value * inv
        out = nt(dproj_ref[0, rows, :], weight(w_ref, 0, slice(0, 512))) + nt(
            dproj_ref[1, rows, :], weight(w_ref, 1, slice(0, 512))
        )
        sum_ref[0:1, :] += jnp.sum(out * hat, axis=0, keepdims=True)
        scaled = out * gain_ref[0:1, :]
        inner = jnp.mean(scaled * hat, axis=-1, keepdims=True)
        part_ref[...] = inv * (scaled - hat * inner)
        for y in range(2):
            part_ref[:, mine(x, y)] += resid_ref[y, rows, :]
        places = pl.ds(i * (TILE // 32), TILE // 32)
        for c in range(8):
            back_ref[places, c] = (
                part_ref[:, c * 128 : c * 128 + 128].astype(BF).reshape(TILE // 32, 32, 128)
            )
        stores.append(mover.start(back_ref.at[places], back_hbm.at[places, :, pl.ds(0, 32)]))
    wait(stores)


def attend_grad_body(
    where_ref, dproj_hbm, n_hbm, delta_hbm, a_hbm,
    keep_hbm, give_hbm,
    dproj_ref, n_ref, delta_ref, a_ref, wide_ref, thin_ref, keep_ref, give_ref, sems,
):
    core = where_ref[3]
    mover = Mover(sems)
    wait(
        [
            mover.start(n_hbm, n_ref),
            mover.start(dproj_hbm, dproj_ref),
            mover.start(a_hbm, a_ref),
            mover.start(delta_hbm, delta_ref),
        ]
    )
    stores = []
    for j in range(4):
        lanes = slice(j * 256, j * 256 + 256)
        normed = jnp.transpose(n_ref[:, lanes])
        delta = jnp.transpose(delta_ref[:, lanes])
        for y in range(2):
            wide_ref[...] = nn(normed, dproj_ref[y]).astype(BF)
            store_grad(wide_ref, core, j, y, slice(0, 512), keep_ref, give_ref)
            thin_ref[...] = nn(delta, a_ref[y]).astype(BF)
            store_grad(thin_ref, core, j, y, slice(512, 768), keep_ref, give_ref)
        done = pl.ds(j * 4, 4)
        stores.append(mover.start(give_ref.at[done], give_hbm.at[done]))
        stores.append(mover.start(keep_ref.at[done], keep_hbm.at[done]))
    wait(stores)


def spread(value):
    return [value] + [shift(value, dx=k) for k in (1, 2, 3)]


def collect(sends):
    return [shift(sends[k - 1], dx=k) for k in (1, 2, 3)]


def repeat(value):
    return jnp.broadcast_to(value[None], (4,) + value.shape)


def collect_weight(parts):
    shard = jnp.concatenate(parts, axis=1)
    full = lax.all_gather(shard, BOTH, axis=0, tiled=False, axis_index_groups=SQUAD)
    return full.reshape(8, 2, 2, 64, shard.shape[1])


def merge(got, base):
    return call(
        merge_body, "vv", [("v", FEATURES, F32), ("v", WIDE, BF)], [], 1, 1 << 20, 4 << 20, got, base, limit=16
    )


def add_up(own, parts):
    return own.astype(F32) + (
        parts[0].astype(F32) + parts[1].astype(F32) + parts[2].astype(F32)
    )


def exchange(blocks, groups):
    return lax.all_to_all(blocks, BOTH, 0, 0, axis_index_groups=groups, tiled=True)


FEATURES = (2, TOK, 128)
EARLY = (8, 2, 2, 64)
WIDE = (4, 2, TOK, 128)
LATE = (8, 2, 2, 64)


fence = lax.optimization_barrier


def take(blocks, at):
    return lax.dynamic_index_in_dim(blocks, at % 4, 0, keepdims=False)


def blocks_z(where, keep, other, gains=None):
    shape = (4, 4) + keep.shape[1:]
    keep, other = keep.reshape(shape), other.reshape(shape)

    def block(k):
        total = take(keep, where[1] + k).astype(F32) + take(other, where[1] + k).astype(F32)
        if gains is None:
            return total if k == 0 else total.astype(BF)
        rows = jnp.broadcast_to(gains[None], (4,) + gains.shape)
        return jnp.concatenate([total.astype(BF), rows], axis=1)

    own, *sends = [block(k) for k in range(4)]
    return own, sends


def reduce_y(where, total):
    return add_up(
        take(total, where[2]), [shift(take(total, where[2] + k).astype(BF), dy=k) for k in (1, 2, 3)]
    )


def body(
    layer_input,
    out_grad,
    token_route,
    seq_lengths,
    positions,
    attn_gain,
    query_weight,
    key_weight,
    value_weight,
    query_gain,
    key_gain,
    out_weight,
    mlp_gain,
    gate_weight,
    up_weight,
    down_weight,
):
    row = lax.axis_index("row")
    col = lax.axis_index("col")
    y_lo = col // 4
    x = col % 4
    where = jnp.stack([x, row // 4, ((row // 2) % 2) * 2 + y_lo, row % 2]).astype(jnp.int32)
    places = jnp.arange(TOK, dtype=jnp.int32)
    heads = jnp.concatenate([query_gain, key_gain, jnp.zeros((D - 256,), BF)])
    all_gains = jnp.stack([attn_gain, mlp_gain, heads] + [jnp.zeros((D,), BF)] * 5).astype(F32)

    early = collect_weight([query_weight, key_weight, value_weight, out_weight.T])
    late = collect_weight([gate_weight, up_weight, down_weight.T])

    (sorted_rows,) = call(
        sort_body,
        "vhh",
        [("v", (2, ROWS, 72, 128), BF)],
        [((2, TOK, 128), BF)] * 2,
        2,
        2 * 2 * 2 * TOK * TOK * 128,
        4 << 20,
        token_route,
        layer_input,
        out_grad,
        limit=60,
    )
    arrived = exchange(sorted_rows.reshape(32, 72, 128), TEAM).reshape(2, ROWS, 72, 128)
    my_input = arrived[:, :, 0:32, :].reshape(FEATURES)
    inputs = exchange(repeat(my_input), SAME_X)
    grads = spread(arrived[:, :, 32:64, :].reshape(FEATURES))
    codes = arrived[0, :, 64, 0:64].astype(F32)
    slots = (codes[:, 0:32] * 16 + codes[:, 32:64]).astype(jnp.int32).reshape(TOK)

    lengths = lax.dynamic_index_in_dim(seq_lengths, y_lo, 0, keepdims=False)[0]
    bound_one = lengths[0]
    bound_two = bound_one + lengths[1]
    bound_three = bound_two + lengths[2]
    first = jnp.where(slots >= bound_one, bound_one, 0)
    first = jnp.where(slots >= bound_two, bound_two, first)
    first = jnp.where(slots >= bound_three, bound_three, first)
    table = jnp.concatenate(
        [slots.astype(F32)[None], first.astype(F32)[None], jnp.zeros((6, TOK), F32)], axis=0
    )
    my_positions = lax.dynamic_index_in_dim(positions, y_lo, 0, keepdims=False)
    position = jnp.sum(
        jnp.where(slots[:, None] == places[None, :], my_positions[None, :], 0), axis=1
    )
    freq_steps = jnp.arange(0, HEAD_SIZE, 2).astype(F32) / HEAD_SIZE
    frequency = 1.0 / ROPE_BASE**freq_steps
    angles = position.astype(F32)[:, None] * frequency[None, :]
    cosine = jnp.cos(angles)
    sine = jnp.sin(angles)
    rope = jnp.concatenate([cosine, cosine, -sine, sine], axis=-1)
    inputs, table, rope = fence((inputs, table, rope))

    sent = [("h", WIDE, BF)]
    send, full, normed_one, proj, q_rows, k_rows, v_rows, attended, lse = call(
        attend_body,
        "hhhhh",
        sent + [("h", (TOK, D), BF), ("h", (TOK, D), BF), ("h", (2, TOK, 384), F32), ("h", (2, TOK, 256), BF),
                ("h", FEATURES, BF), ("h", FEATURES, BF), ("h", (2, TOK, 256), BF), ("h", (TOK, 128), F32)],
        [((TOK, D), BF), (EARLY + (768,), BF), ((8, TOK), F32), ((TOK, 256), F32), ((8, D), F32), ((TOK, TOK), F32),
         ((TILE, D), F32), ((TOK, D), BF), ((2, TOK, 384), F32), ((2, TOK, 256), BF), (FEATURES, BF), (FEATURES, BF),
         ((2, TOK, 256), BF), ((TOK, 128), F32), (WIDE, BF)],
        SENT + 2,
        3 << 30,
        16 << 20,
        inputs, early, table, rope, all_gains,
    )
    send, grads = fence((send, grads))
    resid, wide = merge(exchange(send, SAME_X), my_input)
    wide = exchange(wide, SAME_X)

    send, delta_out, normed_two, hidden, dgu, mlp_sum = call(
        feed_body,
        "s" + "h" * 7,
        sent + [("h", (TOK, D), BF)] * 2 + [("h", (2, TOK, 384), BF), ("h", (2, TOK, 768), BF), ("v", (8, D), F32)],
        [((TOK, D), BF), (LATE + (1152,), BF), ((TILE, D), F32), ((8, D), F32), ((TOK, D), BF), ((TOK, D), BF),
         ((2, TOK, 384), BF), ((2, TOK, 768), BF), (WIDE, BF)],
        SENT + 8,
        5 << 30,
        16 << 20,
        where, wide, *grads, late, all_gains,
    )
    parts = exchange(send, SAME_X)
    quarters, keep, give = call(
        feed_grad_body,
        "s" + "h" * 6,
        [("h", (4, 128, D), BF)] + [("h", (16, 64, 1152), BF)] * 2,
        [((2, TOK, 384), BF), ((2, TOK, 768), BF), ((TOK, D), BF), ((TOK, D), BF), (LATE + (384,), BF), (FEATURES, F32),
         ((TILE, D), F32), ((256, 768), BF), ((256, 384), BF), ((ROWS, 4, 8, D), F32), ((4, 128, D), BF)]
        + [((16, 64, 1152), BF)] * 2,
        20,
        4 << 30,
        16 << 20,
        where, hidden, dgu, normed_two, delta_out, late, resid,
    )
    parts, quarters, keep, give = fence((parts, quarters, keep, give))
    resid_delta, wide = merge(parts, grads[0])
    wide = exchange(wide, SAME_X)
    output_mine = lax.psum_scatter(
        quarters.reshape(TOK, D), BOTH, scatter_dimension=0, tiled=True, axis_index_groups=SAME_X
    ).reshape(ROWS, 8, 8, 128)
    late_own, late_sends = blocks_z(where, keep, shift(give, dcore=1))
    late_parts = [shift(late_sends[k - 1], dz=k) for k in (1, 2, 3)]
    wide, _ = fence((wide, late_sends))

    back, dproj, delta_wide, head_sum, attn_sum = call(
        attend_back_body,
        "s" + "h" * 12,
        [("h", (ROWS, 8, 40, 128), BF), ("h", (2, TOK, 512), BF), ("h", (TOK, D), BF), ("v", (8, 128), F32),
         ("v", (8, D), F32)],
        [((TOK, D), BF), (EARLY + (768,), BF), ((2, TOK, 384), F32), ((2, TOK, 256), BF), (FEATURES, BF), (FEATURES, BF),
         ((TOK, 128), F32), ((8, TOK), F32), ((TOK, 256), F32), ((8, D), F32), ((TOK, TOK), F32), ((2, 128, TOK), F32),
         ((2, 128, TOK), F32), ((TILE, 256), BF), ((2, TOK, 512), BF), ((TOK, D), BF), (FEATURES, F32), ((TILE, D), F32),
         ((ROWS, 8, 32, 128), BF)],
        40,
        7 << 30,
        32 << 20,
        where, wide, early, proj, q_rows, k_rows, v_rows, lse, table, rope, all_gains, full, resid_delta,
    )
    back, dproj, delta_wide, head_sum, attn_sum, late_parts = fence(
        (back, dproj, delta_wide, head_sum, attn_sum, late_parts)
    )
    back = back.at[:, :, 32:40, :].set(jnp.transpose(output_mine, (0, 2, 1, 3)))
    gains = jnp.concatenate([attn_sum[0], mlp_sum[0], head_sum[0], head_sum[1]]).reshape(3, 768)
    gains = jnp.concatenate([gains, jnp.zeros((5, 768), F32)], axis=0)
    gain_parts = [shift(gains, dx=k) for k in (1, 2, 3)]
    keep, give = call(
        attend_grad_body,
        "shhhh",
        [("h", (16, 64, 768), BF)] * 2,
        [((2, TOK, 512), BF), ((TOK, D), BF), ((TOK, D), BF), ((2, TOK, 256), BF), ((256, 512), BF), ((256, 256), BF)]
        + [((16, 64, 768), BF)] * 2,
        20,
        2 << 30,
        8 << 20,
        where, dproj, normed_one, delta_wide, attended,
        limit=60,
    )
    keep, give, gain_parts = fence((keep, give, gain_parts))
    gains = add_up(gains, gain_parts)
    gains = (gains + shift(gains, dcore=1)).astype(BF)
    own, sends = blocks_z(where, keep, shift(give, dcore=1), gains)
    home = exchange(back.reshape(128, 40, 128), None)
    early_parts = [shift(sends[k - 1], dz=k) for k in (1, 2, 3)]
    early_parts[0], late_own, late_parts = fence((early_parts[0], late_own, late_parts))
    late_total = add_up(late_own, late_parts)
    late_parts = [shift(take(late_total, where[2] + k).astype(BF), dy=k) for k in (1, 2, 3)]
    early_parts, late_parts = fence((early_parts, late_parts))
    late_total = add_up(take(late_total, where[2]), late_parts)
    early_total = add_up(own, early_parts)
    early_total = reduce_y(where, early_total)
    layer_output, input_grad = call(
        unsort_body,
        "vh",
        [("v", (2, TOK, 128), BF)] * 2,
        [((2, ROWS, 4, 40, 128), BF)],
        2,
        4 * 2 * TOK * TOK * 128,
        2 << 20,
        token_route,
        home.reshape(ROWS, 2, 4, 40, 128),
        limit=60,
    )
    gains = early_total[64:67].reshape(3 * 768)
    early_total = early_total[0:64]
    return (
        layer_output,
        input_grad,
        gains[0:D],
        early_total[:, 0:256],
        early_total[:, 256:384],
        early_total[:, 384:512],
        gains[2 * D : 2 * D + 128],
        gains[2 * D + 128 :],
        early_total[:, 512:768].T,
        gains[D : 2 * D],
        late_total[:, 0:384],
        late_total[:, 384:768],
        late_total[:, 768:1152].T,
    )


def solution(mesh):
    in_specs = (
        P(None, "row", "col"),
        P(None, "row", "col"),
        P(None, "row"),
        P(None, "row", None),
        P(None, "row"),
        P(),
        P("row", "col"),
        P("row", "col"),
        P("row", "col"),
        P(),
        P(),
        P("col", "row"),
        P(),
        P("row", "col"),
        P("row", "col"),
        P("col", "row"),
    )
    out_specs = (
        P(None, "row", "col"),
        P(None, "row", "col"),
        P(),
        P("row", "col"),
        P("row", "col"),
        P("row", "col"),
        P(),
        P(),
        P("col", "row"),
        P(),
        P("row", "col"),
        P("row", "col"),
        P("col", "row"),
    )
    return jax.shard_map(body, mesh=mesh, in_specs=in_specs, out_specs=out_specs, check_vma=False)
```

profile of v0, /device:TPU:2, one launch (start us, length us, event | category | flops | bytes accessed | tf_op | source)
XLA Modules:
  0.0 272.4 jit_solution(9352698566365054203)
XLA Ops:
  10.4 3.7 %shard_map.255 = bf16[2,16,72,128]{3,2,1,0:T(8,128)(2,1)} custom-call(s32[2,512]{1,0:T(2,128)} %route_ref.3, bf16[2,512,128]{2,1,0:T(8,128)(2,1)} %x_hbm.1, bf16[2,512,128]{2,1,0:T(8,128)(2,1)} %g_hbm.1), custom_call_target="tpu_custom_call" | custom-call | flops 4194304 | bytes 65536 | tf_op jit(solution)/shard_map/pallas_call | solution.py:74
  14.1 8.3 %all-to-all-start = ((bf16[32,72,128]{2,1,0:T(8,128)(2,1)}), bf16[32,72,128]{2,1,0:T(8,128)(2,1)S(1)}, u32[]{:S(2)}, u32[]{:S(2)}) async-start(bf16[32,72,128]{2,1,0:T(8,128)(2,1)} %bitcast.82), calls=%async_computation | async-start | bytes 1179648 | tf_op jit(solution)/shard_map/all_to_all | solution.py:591
  25.9 9.9 %all-to-all-done = bf16[32,72,128]{2,1,0:T(8,128)(2,1)S(1)} async-done(((bf16[32,72,128]{2,1,0:T(8,128)(2,1)}), bf16[32,72,128]{2,1,0:T(8,128)(2,1)S(1)}, u32[]{:S(2)}, u32[]{:S(2)}) %all-to-all-start) | async-done | bytes 589856 | tf_op jit(solution)/shard_map/all_to_all | solution.py:591
  42.2 3.8 %all-to-all-start.1 = ((bf16[4,2,512,128]{3,2,1,0:T(8,128)(2,1)}), bf16[4,2,512,128]{3,2,1,0:T(8,128)(2,1)S(1)}, u32[]{:S(2)}, u32[]{:S(2)}) async-start(bf16[4,2,512,128]{3,2,1,0:T(8,128)(2,1)} %broadcast_in_dim.34), calls=%async_computation.1 | async-start | bytes 2097152 | tf_op jit(solution)/shard_map/all_to_all | solution.py:591
  49.6 12.6 %all-to-all-done.1.x_hbm = bf16[4,2,512,128]{3,2,1,0:T(8,128)(2,1)S(1)} async-done(((bf16[4,2,512,128]{3,2,1,0:T(8,128)(2,1)}), bf16[4,2,512,128]{3,2,1,0:T(8,128)(2,1)S(1)}, u32[]{:S(2)}, u32[]{:S(2)}) %all-to-all-start.1) | async-done | bytes 1048608 | tf_op jit(solution)/shard_map/all_to_all | solution.py:591
  63.2 10.0 %shard_map.256 = (bf16[4,2,512,128]{3,2,1,0:T(8,128)(2,1)}, bf16[512,1024]{1,0:T(8,128)(2,1)}, bf16[512,1024]{1,0:T(8,128)(2,1)}, f32[2,512,384]{2,1,0:T(8,128)}...) custom-call(bf16[4,2,512,128]{3,2,1,0:T(8,128)(2,1)} %copy-done.8, ...), custom_call_target="tpu_custom_call" | custom-call | flops 50331648 | bytes 262144 | tf_op jit(solution)/shard_map/pallas_call | solution.py:74
  73.2 20.3 %all_to_all.35.got_ref = bf16[4,2,512,128]{3,2,1,0:T(8,128)(2,1)S(1)} all-to-all(bf16[4,2,512,128]{3,2,1,0:T(8,128)(2,1)} %get-tuple-element.97), channel_id=1, replica_groups={{0,1,2,3},{4,5,6,7},{8,9,10,11},{12,13,14,15},{16,17,18,19},{20,21,22,2..., dimensions={0} | all-to-all | bytes 2097152 | tf_op jit(solution)/shard_map/all_to_all | solution.py:591
  95.6 4.9 %all-to-all-start.3 = ((bf16[4,2,512,128]{3,2,1,0:T(8,128)(2,1)}), bf16[4,2,512,128]{3,2,1,0:T(8,128)(2,1)S(1)}, u32[]{:S(2)}, u32[]{:S(2)}) async-start(bf16[4,2,512,128]{3,2,1,0:T(8,128)(2,1)} %get-tuple-element.98), calls=%async_computation.3 | async-start | bytes 2097152 | tf_op jit(solution)/shard_map/all_to_all | solution.py:591
  101.1 11.4 %all-to-all-done.3.h_hbm = bf16[4,2,512,128]{3,2,1,0:T(8,128)(2,1)S(1)} async-done(((bf16[4,2,512,128]{3,2,1,0:T(8,128)(2,1)}), bf16[4,2,512,128]{3,2,1,0:T(8,128)(2,1)S(1)}, u32[]{:S(2)}, u32[]{:S(2)}) %all-to-all-start.3) | async-done | bytes 1048608 | tf_op jit(solution)/shard_map/all_to_all | solution.py:591
  113.5 12.7 %shard_map.258 = (bf16[4,2,512,128]{3,2,1,0:T(8,128)(2,1)}, bf16[512,1024]{1,0:T(8,128)(2,1)}, bf16[512,1024]{1,0:T(8,128)(2,1)}, bf16[2,512,384]{2,1,0:T(8,128)...) custom-call(s32[4]{0:T(128)} %pad_add_fusion.where_ref, bf16[4,2,512,128]{3,2,1,0:T(8,128)(2,1)} %copy-done.7, ...), custom_call_target="tpu_custom_call" | custom-call | flops 83886080 | bytes 262144 | tf_op jit(solution)/shard_map/pallas_call | solution.py:74
  126.2 5.0 %all-to-all-start.4 = ((bf16[4,2,512,128]{3,2,1,0:T(8,128)(2,1)}), bf16[4,2,512,128]{3,2,1,0:T(8,128)(2,1)S(1)}, u32[]{:S(2)}, u32[]{:S(2)}) async-start(bf16[4,2,512,128]{3,2,1,0:T(8,128)(2,1)} %get-tuple-element.103), calls=%async_computation.4 | async-start | bytes 2097152 | tf_op jit(solution)/shard_map/all_to_all | solution.py:591
  131.2 8.7 %shard_map.259 = (bf16[4,128,1024]{2,1,0:T(8,128)(2,1)}, bf16[16,64,1152]{2,1,0:T(8,128)(2,1)}, bf16[16,64,1152]{2,1,0:T(8,128)(2,1)}) custom-call(s32[4]{0:T(128)} %pad_add_fusion.where_ref, bf16[2,512,384]{2,1,0:T(8,128)(2,1)} %get-tuple-element.104.hid_hbm, bf16[2,512,768]{2,1,0:T(8,128)(2,1)} %get-tuple-element.105.dgu_hbm, ...), custom_call_target="tpu_custom_call" | custom-call | flops 67108864 | bytes 262144 | tf_op jit(solution)/shard_map/pallas_call | solution.py:74
  144.0 4.9 %all-to-all-start.5 = ((bf16[4,2,512,128]{3,2,1,0:T(8,128)(2,1)}), bf16[4,2,512,128]{3,2,1,0:T(8,128)(2,1)S(1)}, u32[]{:S(2)}, u32[]{:S(2)}) async-start(bf16[4,2,512,128]{3,2,1,0:T(8,128)(2,1)} %get-tuple-element.113), calls=%async_computation.5 | async-start | bytes 2097152 | tf_op jit(solution)/shard_map/all_to_all | solution.py:591
  149.0 3.8 %add_bitcast_fusion = (f32[4,64,1152]{2,1,0:T(8,128)S(1)}, bf16[4,64,1152]{2,1,0:T(8,128)(2,1)}, bf16[4,64,1152]{2,1,0:T(8,128)(2,1)S(1)}, bf16[4,64,1152]{2,1,0:T(8,128)(2,1)S(1)}) fusion(bf16[4,4,64,1152]{3,2,1,0:T(8,128)(2,1)} %bitcast.18, s32[]{:T(128)S(6)} %select_n.199, bf16[4,4,64,1152]{3,2,1,0:T(8,128)(2,1)} %bitcast.83, s32[]{:T(128)S(6)} %select_n.197, ...), kind=kLoop, calls=%fused_computation.1 | loop fusion | flops 4423680 | bytes 7667728 | tf_op jit(solution)/shard_map/add | solution.py:612
  156.3 7.3 %all-to-all-done.5.d_hbm = bf16[4,2,512,128]{3,2,1,0:T(8,128)(2,1)S(1)} async-done(((bf16[4,2,512,128]{3,2,1,0:T(8,128)(2,1)}), bf16[4,2,512,128]{3,2,1,0:T(8,128)(2,1)S(1)}, u32[]{:S(2)}, u32[]{:S(2)}) %all-to-all-start.5) | async-done | bytes 1048608 | tf_op jit(solution)/shard_map/all_to_all | solution.py:591
  164.5 14.3 %shard_map.261 = (bf16[16,8,40,128]{3,2,1,0:T(8,128)(2,1)}, bf16[2,512,512]{2,1,0:T(8,128)(2,1)}, bf16[512,1024]{1,0:T(8,128)(2,1)}, f32[8,128]{1,0:T(8,128)}, f32[8,1024]{1,0:T(8,128)}) custom-call(s32[4]{0:T(128)} %pad_add_fusion.where_ref, bf16[4,2,512,128]{3,2,1,0:T(8,128)(2,1)} %copy-done.6, bf16[8,2,2,64,768]{4,3,2,1,0:T(8,128)(2,1)} %bitcast.80, ...), custom_call_target="tpu_custom_call" | custom-call | flops 117440512 | bytes 524288 | tf_op jit(solution)/shard_map/pallas_call | solution.py:74
  180.6 3.5 %collective-permute-done.4 = bf16[4,64,1152]{2,1,0:T(8,128)(2,1)} collective-permute-done((bf16[4,64,1152]{2,1,0:T(8,128)(2,1)S(1)}, bf16[4,64,1152]{2,1,0:T(8,128)(2,1)}, u32[]{:S(2)}, u32[]{:S(2)}) %collective-permute-start.4) | collective-permute-done | bytes 589856 | tf_op jit(solution)/shard_map/ppermute | solution.py:53
  190.4 5.7 %shard_map.263 = (bf16[16,64,768]{2,1,0:T(8,128)(2,1)}, bf16[16,64,768]{2,1,0:T(8,128)(2,1)}) custom-call(s32[4]{0:T(128)} %pad_add_fusion.where_ref, bf16[2,512,512]{2,1,0:T(8,128)(2,1)} %get-tuple-element.133.dproj_hbm, bf16[512,1024]{1,0:T(8,128)(2,1)} %get-tuple-element.134.n_hbm, bf16[512,1024]{1,0:T(8,128)(2,1)} %get-tuple-element.135.delta_hbm, ...), custom_call_target="tpu_custom_call" | custom-call | flops 33554432 | bytes 131072 | tf_op jit(solution)/shard_map/pallas_call | solution.py:74
  204.3 7.0 %all-to-all-start.6 = ((bf16[128,40,128]{2,1,0:T(8,128)(2,1)}), bf16[128,40,128]{2,1,0:T(8,128)(2,1)S(1)}, u32[]{:S(2)}, u32[]{:S(2)}) async-start(bf16[128,40,128]{2,1,0:T(8,128)(2,1)} %bitcast.88), calls=%async_computation.7 | async-start | bytes 2621440 | tf_op jit(solution)/shard_map/all_to_all | solution.py:591
  211.4 3.4 %collective-permute-start.14 = (bf16[4,72,768]{2,1,0:T(8,128)(2,1)}, bf16[4,72,768]{2,1,0:T(8,128)(2,1)}, u32[]{:S(2)}, u32[]{:S(2)}) collective-permute-start(bf16[4,72,768]{2,1,0:T(8,128)(2,1)} %get-tuple-element.186), channel_id=1, source_target_pairs={{0,96},{1,97},{2,98},{3,99},{8,104},{9,105},{10,106},{11,107},{4,1... | collective-permute-start | bytes 1327112 | tf_op jit(solution)/shard_map/ppermute | solution.py:53
  215.2 24.5 %collective-permute-done.12 = bf16[4,72,768]{2,1,0:T(8,128)(2,1)} collective-permute-done((bf16[4,72,768]{2,1,0:T(8,128)(2,1)}, bf16[4,72,768]{2,1,0:T(8,128)(2,1)}, u32[]{:S(2)}, u32[]{:S(2)}) %collective-permute-start.12) | collective-permute-done | bytes 442400 | tf_op jit(solution)/shard_map/ppermute | solution.py:53
  245.9 3.5 %shard_map.262 = (bf16[2,512,128]{2,1,0:T(8,128)(2,1)}, bf16[2,512,128]{2,1,0:T(8,128)(2,1)}) custom-call(s32[2,512]{1,0:T(2,128)} %route_ref.3, bf16[16,2,4,40,128]{4,3,2,1,0:T(8,128)(2,1)} %bitcast.81), custom_call_target="tpu_custom_call" | custom-call | flops 4194304 | bytes 32768 | tf_op jit(solution)/shard_map/pallas_call | solution.py:74
  254.0 3.2 %collective-permute-start.20 = (bf16[72,768]{1,0:T(8,128)(2,1)S(1)}, bf16[72,768]{1,0:T(8,128)(2,1)S(1)}, u32[]{:S(2)}, u32[]{:S(2)}) collective-permute-start(bf16[72,768]{1,0:T(8,128)(2,1)S(1)} %get-tuple-element.175), channel_id=1, source_target_pairs={{0,20},{1,21},{2,22},{3,23},{8,28},{9,29},{10,30},{11,31},{4,0},{5... | collective-permute-start | bytes 331784 | tf_op jit(solution)/shard_map/ppermute | solution.py:53
  260.7 2.8 %collective-permute-done.19 = bf16[72,768]{1,0:T(8,128)(2,1)S(1)} collective-permute-done((bf16[72,768]{1,0:T(8,128)(2,1)S(1)}, bf16[72,768]{1,0:T(8,128)(2,1)S(1)}, u32[]{:S(2)}, u32[]{:S(2)}) %collective-permute-start.19) | collective-permute-done | bytes 110624 | tf_op jit(solution)/shard_map/ppermute | solution.py:53
  (142 shorter events, 61.0 us)
Async XLA Ops:
  7.2 55.0 %all-gather.5.cloned.1.call-start = ((), (), s32[]{:S(2)}) async-start(), calls=%async_computation.9 | async-start | bytes 3244032 | tf_op jit(solution)/shard_map/all_gather | solution.py:574
  8.7 103.8 %all-gather.7.cloned.1.call-start = ((), (), s32[]{:S(2)}) async-start(), calls=%async_computation.10 | async-start | bytes 4866048 | tf_op jit(solution)/shard_map/all_gather | solution.py:574
  14.1 21.7 %all-to-all-start = ((bf16[32,72,128]{2,1,0:T(8,128)(2,1)}), bf16[32,72,128]{2,1,0:T(8,128)(2,1)S(1)}, u32[]{:S(2)}, u32[]{:S(2)}) async-start(bf16[32,72,128]{2,1,0:T(8,128)(2,1)} %bitcast.82), calls=%async_computation | async-start | bytes 1179648 | tf_op jit(solution)/shard_map/all_to_all | solution.py:591
  35.8 37.3 %collective-permute-start.2 = (bf16[2,512,128]{2,1,0:T(8,128)(2,1)S(1)}, bf16[2,512,128]{2,1,0:T(8,128)(2,1)S(1)}, u32[]{:S(2)}, u32[]{:S(2)}) collective-permute-start(bf16[2,512,128]{2,1,0:T(8,128)(2,1)S(1)} %bitcast.70), channel_id=1, source_target_pairs={{0,3},{1,0},{2,1},{3,2},{8,11},{9,8},{10,9},{11,10},{4,7},{5,4},{6... | collective-permute-start | bytes 786440 | tf_op jit(solution)/shard_map/ppermute | solution.py:53
  36.4 36.8 %collective-permute-start.1 = (bf16[2,512,128]{2,1,0:T(8,128)(2,1)S(1)}, bf16[2,512,128]{2,1,0:T(8,128)(2,1)S(1)}, u32[]{:S(2)}, u32[]{:S(2)}) collective-permute-start(bf16[2,512,128]{2,1,0:T(8,128)(2,1)S(1)} %bitcast.71), channel_id=1, source_target_pairs={{0,2},{1,3},{2,0},{3,1},{8,10},{9,11},{10,8},{11,9},{4,6},{5,7},{6... | collective-permute-start | bytes 786440 | tf_op jit(solution)/shard_map/ppermute | solution.py:53
  38.8 34.3 %collective-permute-start = (bf16[2,512,128]{2,1,0:T(8,128)(2,1)S(1)}, bf16[2,512,128]{2,1,0:T(8,128)(2,1)S(1)}, u32[]{:S(2)}, u32[]{:S(2)}) collective-permute-start(bf16[2,512,128]{2,1,0:T(8,128)(2,1)S(1)} %bitcast.72), channel_id=1, source_target_pairs={{0,1},{1,2},{2,3},{3,0},{8,9},{9,10},{10,11},{11,8},{4,5},{5,6},{6... | collective-permute-start | bytes 786440 | tf_op jit(solution)/shard_map/ppermute | solution.py:53
  42.2 20.0 %all-to-all-start.1 = ((bf16[4,2,512,128]{3,2,1,0:T(8,128)(2,1)}), bf16[4,2,512,128]{3,2,1,0:T(8,128)(2,1)S(1)}, u32[]{:S(2)}, u32[]{:S(2)}) async-start(bf16[4,2,512,128]{3,2,1,0:T(8,128)(2,1)} %broadcast_in_dim.34), calls=%async_computation.1 | async-start | bytes 2097152 | tf_op jit(solution)/shard_map/all_to_all | solution.py:591
  95.6 16.9 %all-to-all-start.3 = ((bf16[4,2,512,128]{3,2,1,0:T(8,128)(2,1)}), bf16[4,2,512,128]{3,2,1,0:T(8,128)(2,1)S(1)}, u32[]{:S(2)}, u32[]{:S(2)}) async-start(bf16[4,2,512,128]{3,2,1,0:T(8,128)(2,1)} %get-tuple-element.98), calls=%async_computation.3 | async-start | bytes 2097152 | tf_op jit(solution)/shard_map/all_to_all | solution.py:591
  126.2 15.7 %all-to-all-start.4 = ((bf16[4,2,512,128]{3,2,1,0:T(8,128)(2,1)}), bf16[4,2,512,128]{3,2,1,0:T(8,128)(2,1)S(1)}, u32[]{:S(2)}, u32[]{:S(2)}) async-start(bf16[4,2,512,128]{3,2,1,0:T(8,128)(2,1)} %get-tuple-element.103), calls=%async_computation.4 | async-start | bytes 2097152 | tf_op jit(solution)/shard_map/all_to_all | solution.py:591
  142.0 7.0 %collective-permute-start.3 = (bf16[16,64,1152]{2,1,0:T(8,128)(2,1)}, bf16[16,64,1152]{2,1,0:T(8,128)(2,1)}, u32[]{:S(2)}, u32[]{:S(2)}) collective-permute-start(bf16[16,64,1152]{2,1,0:T(8,128)(2,1)} %get-tuple-element.115), channel_id=1, source_target_pairs={{0,8},{1,9},{2,10},{3,11},{8,0},{9,1},{10,2},{11,3},{4,12},{5,13},... | collective-permute-start | bytes 7077896 | tf_op jit(solution)/shard_map/ppermute | solution.py:53
  144.0 19.5 %all-to-all-start.5 = ((bf16[4,2,512,128]{3,2,1,0:T(8,128)(2,1)}), bf16[4,2,512,128]{3,2,1,0:T(8,128)(2,1)S(1)}, u32[]{:S(2)}, u32[]{:S(2)}) async-start(bf16[4,2,512,128]{3,2,1,0:T(8,128)(2,1)} %get-tuple-element.113), calls=%async_computation.5 | async-start | bytes 2097152 | tf_op jit(solution)/shard_map/all_to_all | solution.py:591
  148.9 53.7 %reduce-scatter.2.cloned.1.call-start = ((), (), s32[]{:S(2)}) async-start(), calls=%async_computation.8 | async-start | bytes 1310720 | tf_op jit(solution)/shard_map/reduce_scatter | solution.py:745
  152.7 27.9 %collective-permute-start.6 = (bf16[4,64,1152]{2,1,0:T(8,128)(2,1)}, bf16[4,64,1152]{2,1,0:T(8,128)(2,1)}, u32[]{:S(2)}, u32[]{:S(2)}) collective-permute-start(bf16[4,64,1152]{2,1,0:T(8,128)(2,1)} %get-tuple-element.164), channel_id=1, source_target_pairs={{0,96},{1,97},{2,98},{3,99},{8,104},{9,105},{10,106},{11,107},{4,1... | collective-permute-start | bytes 1769480 | tf_op jit(solution)/shard_map/ppermute | solution.py:53
  154.6 26.0 %collective-permute-start.5 = (bf16[4,64,1152]{2,1,0:T(8,128)(2,1)S(1)}, bf16[4,64,1152]{2,1,0:T(8,128)(2,1)}, u32[]{:S(2)}, u32[]{:S(2)}) collective-permute-start(bf16[4,64,1152]{2,1,0:T(8,128)(2,1)S(1)} %get-tuple-element.165), channel_id=1, source_target_pairs={{0,64},{1,65},{2,66},{3,67},{8,72},{9,73},{10,74},{11,75},{4,68},{... | collective-permute-start | bytes 1769480 | tf_op jit(solution)/shard_map/ppermute | solution.py:53
  155.5 28.6 %collective-permute-start.4 = (bf16[4,64,1152]{2,1,0:T(8,128)(2,1)S(1)}, bf16[4,64,1152]{2,1,0:T(8,128)(2,1)}, u32[]{:S(2)}, u32[]{:S(2)}) collective-permute-start(bf16[4,64,1152]{2,1,0:T(8,128)(2,1)S(1)} %get-tuple-element.166), channel_id=1, source_target_pairs={{0,32},{1,33},{2,34},{3,35},{8,40},{9,41},{10,42},{11,43},{4,36},{... | collective-permute-start | bytes 1769480 | tf_op jit(solution)/shard_map/ppermute | solution.py:53
  185.6 10.4 %collective-permute-start.9 = (f32[8,768]{1,0:T(8,128)S(1)}, f32[8,768]{1,0:T(8,128)S(1)}, u32[]{:S(2)}, u32[]{:S(2)}) collective-permute-start(f32[8,768]{1,0:T(8,128)S(1)} %concatenate.41), channel_id=1, source_target_pairs={{0,3},{1,0},{2,1},{3,2},{8,11},{9,8},{10,9},{11,10},{4,7},{5,4},{6... | collective-permute-start | bytes 73736 | tf_op jit(solution)/shard_map/ppermute | solution.py:53
  186.1 10.0 %collective-permute-start.8 = (f32[8,768]{1,0:T(8,128)S(1)}, f32[8,768]{1,0:T(8,128)S(1)}, u32[]{:S(2)}, u32[]{:S(2)}) collective-permute-start(f32[8,768]{1,0:T(8,128)S(1)} %concatenate.41), channel_id=1, source_target_pairs={{0,2},{1,3},{2,0},{3,1},{8,10},{9,11},{10,8},{11,9},{4,6},{5,7},{6... | collective-permute-start | bytes 73736 | tf_op jit(solution)/shard_map/ppermute | solution.py:53
  188.6 7.5 %collective-permute-start.7 = (f32[8,768]{1,0:T(8,128)S(1)}, f32[8,768]{1,0:T(8,128)S(1)}, u32[]{:S(2)}, u32[]{:S(2)}) collective-permute-start(f32[8,768]{1,0:T(8,128)S(1)} %concatenate.41), channel_id=1, source_target_pairs={{0,1},{1,2},{2,3},{3,0},{8,9},{9,10},{10,11},{11,8},{4,5},{5,6},{6... | collective-permute-start | bytes 73736 | tf_op jit(solution)/shard_map/ppermute | solution.py:53
  202.6 37.0 %collective-permute-start.12 = (bf16[4,72,768]{2,1,0:T(8,128)(2,1)}, bf16[4,72,768]{2,1,0:T(8,128)(2,1)}, u32[]{:S(2)}, u32[]{:S(2)}) collective-permute-start(bf16[4,72,768]{2,1,0:T(8,128)(2,1)} %get-tuple-element.187), channel_id=1, source_target_pairs={{0,32},{1,33},{2,34},{3,35},{8,40},{9,41},{10,42},{11,43},{4,36},{... | collective-permute-start | bytes 1327112 | tf_op jit(solution)/shard_map/ppermute | solution.py:53
  204.3 40.5 %all-to-all-start.6 = ((bf16[128,40,128]{2,1,0:T(8,128)(2,1)}), bf16[128,40,128]{2,1,0:T(8,128)(2,1)S(1)}, u32[]{:S(2)}, u32[]{:S(2)}) async-start(bf16[128,40,128]{2,1,0:T(8,128)(2,1)} %bitcast.88), calls=%async_computation.7 | async-start | bytes 2621440 | tf_op jit(solution)/shard_map/all_to_all | solution.py:591
  211.4 38.0 %collective-permute-start.14 = (bf16[4,72,768]{2,1,0:T(8,128)(2,1)}, bf16[4,72,768]{2,1,0:T(8,128)(2,1)}, u32[]{:S(2)}, u32[]{:S(2)}) collective-permute-start(bf16[4,72,768]{2,1,0:T(8,128)(2,1)} %get-tuple-element.186), channel_id=1, source_target_pairs={{0,96},{1,97},{2,98},{3,99},{8,104},{9,105},{10,106},{11,107},{4,1... | collective-permute-start | bytes 1327112 | tf_op jit(solution)/shard_map/ppermute | solution.py:53
  214.8 34.6 %collective-permute-start.13 = (bf16[4,72,768]{2,1,0:T(8,128)(2,1)S(1)}, bf16[4,72,768]{2,1,0:T(8,128)(2,1)}, u32[]{:S(2)}, u32[]{:S(2)}) collective-permute-start(bf16[4,72,768]{2,1,0:T(8,128)(2,1)S(1)} %get-tuple-element.188), channel_id=1, source_target_pairs={{0,64},{1,65},{2,66},{3,67},{8,72},{9,73},{10,74},{11,75},{4,68},{... | collective-permute-start | bytes 1327112 | tf_op jit(solution)/shard_map/ppermute | solution.py:53
  242.5 7.0 %collective-permute-start.17 = (bf16[64,1152]{1,0:T(8,128)(2,1)S(1)}, bf16[64,1152]{1,0:T(8,128)(2,1)S(1)}, u32[]{:S(2)}, u32[]{:S(2)}) collective-permute-start(bf16[64,1152]{1,0:T(8,128)(2,1)S(1)} %get-tuple-element.171), channel_id=1, source_target_pairs={{0,20},{1,21},{2,22},{3,23},{8,28},{9,29},{10,30},{11,31},{4,0},{5... | collective-permute-start | bytes 442376 | tf_op jit(solution)/shard_map/ppermute | solution.py:53
  242.9 9.4 %collective-permute-start.15 = (bf16[64,1152]{1,0:T(8,128)(2,1)S(1)}, bf16[64,1152]{1,0:T(8,128)(2,1)S(1)}, u32[]{:S(2)}, u32[]{:S(2)}) collective-permute-start(bf16[64,1152]{1,0:T(8,128)(2,1)S(1)} %get-tuple-element.173), channel_id=1, source_target_pairs={{0,4},{1,5},{2,6},{3,7},{8,12},{9,13},{10,14},{11,15},{4,16},{5,17... | collective-permute-start | bytes 442376 | tf_op jit(solution)/shard_map/ppermute | solution.py:53
  (24 other events, 201.4 us)
Sparse Core Ops, SparseCore 0:
  10.9 50.4 all-gather.4
  63.6 46.2 all-gather.6
  156.4 21.5 reduce-scatter.1
where the time goes:
time: 274 us; the launch traced here: 272 us
  waiting for transfers between devices  83.4 us (30%)
  Pallas kernels  60.8 us (22%)
  starting transfers between devices  56.6 us (21%)
  blocking collectives  20.3 us (7%)
  other arithmetic  18.8 us (7%)
  between operations  16.3 us (6%)
  local copies, waits for them, and re-layouts  16.2 us (6%)
    pallas_call x9, Pallas kernels, call(): pl.pallas_call(body, out_shape=[jax.ShapeDtypeStruct(s, t) for _, s, t in...  60.8 us
    all_to_all x6, waiting for transfers between devices, exchange(): lax.all_to_all(blocks, BOTH, 0, 0, axis_index_groups=groups, tiled=True)  43.3 us
    ppermute x21, waiting for transfers between devices, shift(): return lax.ppermute(value, BOTH, moves(**step))  40 us
    all_to_all x6, starting transfers between devices, exchange(): lax.all_to_all(blocks, BOTH, 0, 0, axis_index_groups=groups, tiled=True)  34 us
    ppermute x21, starting transfers between devices, shift(): return lax.ppermute(value, BOTH, moves(**step))  22.5 us
    all_to_all x1, blocking collectives, exchange(): lax.all_to_all(blocks, BOTH, 0, 0, axis_index_groups=groups, tiled=True)  20.3 us
    unnamed x36, local copies, waits for them, and re-layouts  6.79 us
  transfers between devices with their start and end apart: 30, of which 15 were waited for; matrix products, arithmetic and copies ran while one was open for 8% of the time, Pallas kernels for 18%

commit v1 on v0

--- a/solution.py
+++ b/solution.py
@@ -132,18 +132,15 @@
 
 def unsort_body(route_ref, home_hbm, y_ref, dx_ref, home_ref, sems):
     mover = Mover(sems)
-    loads = [mover.start(home_hbm.at[:, m], home_ref.at[m]) for m in range(2)]
+    loads = [mover.start(home_hbm.at[m], home_ref.at[m]) for m in range(2)]
     for m in range(2):
         _, _, down = ranks(route_ref[m : m + 1, :].astype(F32))
         lane = lax.broadcasted_iota(jnp.int32, (TOK, TOK), 1).astype(F32)
         pick = (lane == down).astype(BF)
         loads[m].wait()
-        total = home_ref[m, :, 0, 0:32, :].astype(F32)
-        for x in range(1, 4):
-            total = total + home_ref[m, :, x, 0:32, :].astype(F32)
-        dx_ref[m] = nn(pick, total.astype(BF).reshape(TOK, 128)).astype(BF)
-        output = home_ref[m, :, :, 32:40, :].astype(F32).reshape(TOK, 128).astype(BF)
-        y_ref[m] = nn(pick, output).astype(BF)
+        for at, target_ref in ((0, dx_ref), (32, y_ref)):
+            rows = home_ref[m, :, at : at + 32, :].reshape(TOK, 128)
+            target_ref[m] = nn(pick, rows).astype(BF)
 
 
 def features_of(mover, blocks, x, full_ref):
@@ -178,12 +175,11 @@
             send_ref[k, y, rows, :] = part_ref[:, lanes].astype(BF)
 
 
-def merge_body(got_ref, base_ref, total_ref, wide_ref, sems):
+def merge_body(got_ref, base_ref, wide_ref, sems):
     for y in range(2):
         total = base_ref[y].astype(F32)
         for k in range(4):
             total = total + got_ref[k, y].astype(F32)
-        total_ref[y] = total
         for k in range(4):
             wide_ref[k, y] = total.astype(BF)
 
@@ -370,14 +366,14 @@
     for k in range(2):
         kept = pl.multiple_of((k * 2 + core) * 64, 64)
         given = pl.multiple_of((k * 2 + 1 - core) * 64, 64)
-        keep_ref[(chunk * 2 + k) * 2 + y, 0:64, lanes] = value_ref[pl.ds(kept, 64), :]
-        give_ref[(chunk * 2 + k) * 2 + y, 0:64, lanes] = value_ref[pl.ds(given, 64), :]
+        keep_ref[(chunk * 2 + k) * 2 + y, :, lanes] = value_ref[pl.ds(kept, 64), :]
+        give_ref[(chunk * 2 + k) * 2 + y, :, lanes] = value_ref[pl.ds(given, 64), :]
 
 
 def feed_grad_body(
-    where_ref, hid_hbm, dgu_hbm, n_hbm, dy_hbm, w_hbm, resid_hbm,
-    quarter_hbm, keep_hbm, give_hbm,
-    hid_ref, dgu_ref, n_ref, dy_ref, w_ref, resid_ref, part_ref, wide_ref, thin_ref, stage_ref, quarter_ref, keep_ref,
+    where_ref, hid_hbm, dgu_hbm, n_hbm, dy_hbm, w_hbm, h_hbm,
+    out_hbm, keep_hbm, give_hbm,
+    hid_ref, dgu_ref, n_ref, dy_ref, w_ref, resid_ref, part_ref, wide_ref, thin_ref, out_ref, keep_ref,
     give_ref, sems,
 ):
     x, core = where_ref[0], where_ref[3]
@@ -385,7 +381,7 @@
     first = [
         mover.start(hid_hbm, hid_ref),
         mover.start(w_hbm.at[:, :, :, :, pl.ds(768, 384)], w_ref),
-        mover.start(resid_hbm, resid_ref),
+        mover.start(h_hbm.at[x], resid_ref),
     ]
     loads = [
         mover.start(n_hbm, n_ref),
@@ -400,15 +396,12 @@
             hid_ref[1, rows, :], weight(w_ref, 1, slice(0, 384))
         )
         for y in range(2):
-            part_ref[:, mine(x, y)] += resid_ref[y, rows, :]
-        places = pl.ds(pl.multiple_of(i * (TILE // 32), TILE // 32), TILE // 32)
-        stage_ref[places] = part_ref[...].reshape(TILE // 32, 4, 8, D)
+            part_ref[:, mine(x, y)] += resid_ref[y, rows, :].astype(F32)
+        split_features(part_ref, rows, out_ref)
         return carry
 
     lax.fori_loop(0, TOK // TILE, step, 0)
-    for k in range(4):
-        quarter_ref[k] = stage_ref[:, k].reshape(128, D).astype(BF)
-    stores = [mover.start(quarter_ref, quarter_hbm)]
+    stores = [mover.start(out_ref, out_hbm)]
     wait(loads)
     for j in range(4):
         lanes = slice(j * 256, j * 256 + 256)
@@ -427,12 +420,13 @@
 
 def attend_back_body(
     where_ref, d_hbm, w_hbm, proj_hbm, q_hbm, k_hbm, v_hbm, lse_hbm, table_hbm,
-    rope_hbm, gain_hbm, full_hbm, resid_hbm,
-    back_hbm, dproj_hbm, delta_hbm, head_ref, sum_ref,
+    rope_hbm, gain_hbm, full_hbm, n_hbm, a_hbm, mlp_sum_hbm,
+    own_hbm, send1, send2, send3, keep_hbm, give_hbm,
     delta_ref, w_ref, proj_ref, q_ref, k_ref, v_ref, lse_ref, table_ref, rope_ref, gain_ref, bias_ref, dk_ref, dv_ref,
-    da_ref, dproj_ref, full_ref, resid_ref, part_ref, back_ref, sems,
+    da_ref, dproj_ref, full_ref, part_ref, own_ref, back_ref, n_ref, a_ref, wide_ref, thin_ref, keep_ref, give_ref,
+    head_ref, sum_ref, mlp_sum_ref, rows_ref, sems,
 ):
-    x = where_ref[0]
+    x, core = where_ref[0], where_ref[3]
     mover = Mover(sems)
     loads = [
         mover.start(table_hbm, table_ref),
@@ -447,12 +441,13 @@
         mover.start(proj_hbm, proj_ref),
         mover.start(rope_hbm, rope_ref),
         mover.start(gain_hbm, gain_ref),
+        mover.start(mlp_sum_hbm, mlp_sum_ref),
     ]
     more = [
         mover.start(w_hbm.at[:, :, :, :, pl.ds(0, 512)], w_ref.at[:, :, :, :, pl.ds(0, 512)]),
         mover.start(full_hbm, full_ref),
-        mover.start(resid_hbm, resid_ref),
-    ]
+    ]
+    much = [mover.start(n_hbm, n_ref), mover.start(a_hbm, a_ref)]
     head_ref[...] = jnp.zeros_like(head_ref)
     sum_ref[...] = jnp.zeros_like(sum_ref)
     dk_ref[...] = jnp.zeros_like(dk_ref)
@@ -460,7 +455,7 @@
     loads[0].wait()
     bias_of(table_ref, bias_ref)
     wait(loads[1:])
-    stores = [mover.start(delta_ref, delta_hbm)]
+    stores = []
 
     def back(rotated, proj, gain, rows, at):
         turned = rotated * rope_ref[rows, 0:128] - pltpu.roll(rotated, 64, 1) * rope_ref[rows, 128:256]
@@ -501,7 +496,19 @@
                 jnp.transpose(dk_ref[y, :, rows]) * SCALE, proj_ref[y, rows, 256:384], gain_ref[2:3, 128:256], rows, 1
             )
             dproj_ref[y, rows, 384:512] = jnp.transpose(dv_ref[y, :, rows]).astype(BF)
-    stores.append(mover.start(dproj_ref, dproj_hbm))
+    wait(much)
+    for j in range(4):
+        lanes = slice(j * 256, j * 256 + 256)
+        normed = jnp.transpose(n_ref[:, lanes])
+        delta = jnp.transpose(delta_ref[:, lanes])
+        for y in range(2):
+            wide_ref[...] = nn(normed, dproj_ref[y]).astype(BF)
+            store_grad(wide_ref, core, j, y, slice(0, 512), keep_ref, give_ref)
+            thin_ref[...] = nn(delta, a_ref[y]).astype(BF)
+            store_grad(thin_ref, core, j, y, slice(512, 768), keep_ref, give_ref)
+        done = pl.ds(j * 4, 4)
+        stores.append(mover.start(give_ref.at[done], give_hbm.at[done, pl.ds(0, 64)]))
+        stores.append(mover.start(keep_ref.at[done], keep_hbm.at[done, pl.ds(0, 64)]))
     wait(more)
     for i in range(TOK // TILE):
         rows = pl.ds(i * TILE, TILE)
@@ -516,44 +523,27 @@
         inner = jnp.mean(scaled * hat, axis=-1, keepdims=True)
         part_ref[...] = inv * (scaled - hat * inner)
         for y in range(2):
-            part_ref[:, mine(x, y)] += resid_ref[y, rows, :]
-        places = pl.ds(i * (TILE // 32), TILE // 32)
-        for c in range(8):
-            back_ref[places, c] = (
-                part_ref[:, c * 128 : c * 128 + 128].astype(BF).reshape(TILE // 32, 32, 128)
-            )
-        stores.append(mover.start(back_ref.at[places], back_hbm.at[places, :, pl.ds(0, 32)]))
-    wait(stores)
-
-
-def attend_grad_body(
-    where_ref, dproj_hbm, n_hbm, delta_hbm, a_hbm,
-    keep_hbm, give_hbm,
-    dproj_ref, n_ref, delta_ref, a_ref, wide_ref, thin_ref, keep_ref, give_ref, sems,
-):
-    core = where_ref[3]
-    mover = Mover(sems)
-    wait(
+            part_ref[:, mine(x, y)] += delta_ref[rows, mine(x, y)].astype(F32)
+        for y in range(2):
+            own_ref[y, rows, :] = part_ref[:, mine(x, y)]
+            for k in range(3):
+                back_ref[k, y, rows, :] = part_ref[:, mine(lax.rem(x + k + 1, 4), y)].astype(BF)
+        stores.append(mover.start(own_ref.at[:, rows], own_hbm.at[:, rows]))
+        for k, send in enumerate((send1, send2, send3)):
+            stores.append(mover.start(back_ref.at[k, :, rows], send.at[:, rows]))
+    attn_sum, mlp_sum = sum_ref[0:1, :], mlp_sum_ref[0:1, :]
+    gains = jnp.concatenate(
         [
-            mover.start(n_hbm, n_ref),
-            mover.start(dproj_hbm, dproj_ref),
-            mover.start(a_hbm, a_ref),
-            mover.start(delta_hbm, delta_ref),
-        ]
-    )
-    stores = []
-    for j in range(4):
-        lanes = slice(j * 256, j * 256 + 256)
-        normed = jnp.transpose(n_ref[:, lanes])
-        delta = jnp.transpose(delta_ref[:, lanes])
-        for y in range(2):
-            wide_ref[...] = nn(normed, dproj_ref[y]).astype(BF)
-            store_grad(wide_ref, core, j, y, slice(0, 512), keep_ref, give_ref)
-            thin_ref[...] = nn(delta, a_ref[y]).astype(BF)
-            store_grad(thin_ref, core, j, y, slice(512, 768), keep_ref, give_ref)
-        done = pl.ds(j * 4, 4)
-        stores.append(mover.start(give_ref.at[done], give_hbm.at[done]))
-        stores.append(mover.start(keep_ref.at[done], keep_hbm.at[done]))
+            attn_sum[:, 0:768],
+            jnp.concatenate([attn_sum[:, 768:1024], mlp_sum[:, 0:512]], axis=1),
+            jnp.concatenate([mlp_sum[:, 512:1024], head_ref[0:1, :], head_ref[1:2, :]], axis=1),
+            jnp.zeros((5, 768), F32),
+        ],
+        axis=0,
+    )
+    rows_ref[...] = jnp.broadcast_to(gains[None], (16, 8, 768)).astype(BF)
+    stores.append(mover.start(rows_ref, keep_hbm.at[:, pl.ds(64, 8)]))
+    stores.append(mover.start(rows_ref, give_hbm.at[:, pl.ds(64, 8)]))
     wait(stores)
 
 
@@ -577,8 +567,8 @@
 
 def merge(got, base):
     return call(
-        merge_body, "vv", [("v", FEATURES, F32), ("v", WIDE, BF)], [], 1, 1 << 20, 4 << 20, got, base, limit=16
-    )
+        merge_body, "vv", [("v", WIDE, BF)], [], 1, 1 << 20, 4 << 20, got, base, limit=16
+    )[0]
 
 
 def add_up(own, parts):
@@ -604,19 +594,14 @@
     return lax.dynamic_index_in_dim(blocks, at % 4, 0, keepdims=False)
 
 
-def blocks_z(where, keep, other, gains=None):
+def blocks_z(where, keep, other):
     shape = (4, 4) + keep.shape[1:]
     keep, other = keep.reshape(shape), other.reshape(shape)
 
     def block(k):
-        total = take(keep, where[1] + k).astype(F32) + take(other, where[1] + k).astype(F32)
-        if gains is None:
-            return total if k == 0 else total.astype(BF)
-        rows = jnp.broadcast_to(gains[None], (4,) + gains.shape)
-        return jnp.concatenate([total.astype(BF), rows], axis=1)
-
-    own, *sends = [block(k) for k in range(4)]
-    return own, sends
+        return take(keep, where[1] + k).astype(F32) + take(other, where[1] + k).astype(F32)
+
+    return block(0), [block(k).astype(BF) for k in (1, 2, 3)]
 
 
 def reduce_y(where, total):
@@ -712,7 +697,7 @@
         inputs, early, table, rope, all_gains,
     )
     send, grads = fence((send, grads))
-    resid, wide = merge(exchange(send, SAME_X), my_input)
+    wide = merge(exchange(send, SAME_X), my_input)
     wide = exchange(wide, SAME_X)
 
     send, delta_out, normed_two, hidden, dgu, mlp_sum = call(
@@ -727,87 +712,74 @@
         where, wide, *grads, late, all_gains,
     )
     parts = exchange(send, SAME_X)
-    quarters, keep, give = call(
+    out_home, keep, give = call(
         feed_grad_body,
         "s" + "h" * 6,
-        [("h", (4, 128, D), BF)] + [("h", (16, 64, 1152), BF)] * 2,
-        [((2, TOK, 384), BF), ((2, TOK, 768), BF), ((TOK, D), BF), ((TOK, D), BF), (LATE + (384,), BF), (FEATURES, F32),
-         ((TILE, D), F32), ((256, 768), BF), ((256, 384), BF), ((ROWS, 4, 8, D), F32), ((4, 128, D), BF)]
+        [("h", WIDE, BF)] + [("h", (16, 64, 1152), BF)] * 2,
+        [((2, TOK, 384), BF), ((2, TOK, 768), BF), ((TOK, D), BF), ((TOK, D), BF), (LATE + (384,), BF), (FEATURES, BF),
+         ((TILE, D), F32), ((256, 768), BF), ((256, 384), BF), (WIDE, BF)]
         + [((16, 64, 1152), BF)] * 2,
         20,
         4 << 30,
         16 << 20,
-        where, hidden, dgu, normed_two, delta_out, late, resid,
-    )
-    parts, quarters, keep, give = fence((parts, quarters, keep, give))
-    resid_delta, wide = merge(parts, grads[0])
+        where, hidden, dgu, normed_two, delta_out, late, wide,
+    )
+    parts, out_home, keep, give = fence((parts, out_home, keep, give))
+    wide = merge(parts, grads[0])
     wide = exchange(wide, SAME_X)
-    output_mine = lax.psum_scatter(
-        quarters.reshape(TOK, D), BOTH, scatter_dimension=0, tiled=True, axis_index_groups=SAME_X
-    ).reshape(ROWS, 8, 8, 128)
     late_own, late_sends = blocks_z(where, keep, shift(give, dcore=1))
     late_parts = [shift(late_sends[k - 1], dz=k) for k in (1, 2, 3)]
     wide, _ = fence((wide, late_sends))
 
-    back, dproj, delta_wide, head_sum, attn_sum = call(
+    mine_delta, *delta_sends, keep, give = call(
         attend_back_body,
-        "s" + "h" * 12,
-        [("h", (ROWS, 8, 40, 128), BF), ("h", (2, TOK, 512), BF), ("h", (TOK, D), BF), ("v", (8, 128), F32),
-         ("v", (8, D), F32)],
+        "s" + "h" * 14,
+        [("h", FEATURES, F32)] + [("h", FEATURES, BF)] * 3 + [("h", (16, 72, 768), BF)] * 2,
         [((TOK, D), BF), (EARLY + (768,), BF), ((2, TOK, 384), F32), ((2, TOK, 256), BF), (FEATURES, BF), (FEATURES, BF),
          ((TOK, 128), F32), ((8, TOK), F32), ((TOK, 256), F32), ((8, D), F32), ((TOK, TOK), F32), ((2, 128, TOK), F32),
-         ((2, 128, TOK), F32), ((TILE, 256), BF), ((2, TOK, 512), BF), ((TOK, D), BF), (FEATURES, F32), ((TILE, D), F32),
-         ((ROWS, 8, 32, 128), BF)],
-        40,
+         ((2, 128, TOK), F32), ((TILE, 256), BF), ((2, TOK, 512), BF), ((TOK, D), BF), ((TILE, D), F32),
+         (FEATURES, F32), ((3,) + FEATURES, BF), ((TOK, D), BF), ((2, TOK, 256), BF), ((256, 512), BF), ((256, 256), BF)]
+        + [((16, 64, 768), BF)] * 2
+        + [((8, 128), F32), ((8, D), F32), ((8, D), F32), ((16, 8, 768), BF)],
+        52,
         7 << 30,
         32 << 20,
-        where, wide, early, proj, q_rows, k_rows, v_rows, lse, table, rope, all_gains, full, resid_delta,
-    )
-    back, dproj, delta_wide, head_sum, attn_sum, late_parts = fence(
-        (back, dproj, delta_wide, head_sum, attn_sum, late_parts)
-    )
-    back = back.at[:, :, 32:40, :].set(jnp.transpose(output_mine, (0, 2, 1, 3)))
-    gains = jnp.concatenate([attn_sum[0], mlp_sum[0], head_sum[0], head_sum[1]]).reshape(3, 768)
-    gains = jnp.concatenate([gains, jnp.zeros((5, 768), F32)], axis=0)
-    gain_parts = [shift(gains, dx=k) for k in (1, 2, 3)]
-    keep, give = call(
-        attend_grad_body,
-        "shhhh",
-        [("h", (16, 64, 768), BF)] * 2,
-        [((2, TOK, 512), BF), ((TOK, D), BF), ((TOK, D), BF), ((2, TOK, 256), BF), ((256, 512), BF), ((256, 256), BF)]
-        + [((16, 64, 768), BF)] * 2,
-        20,
-        2 << 30,
-        8 << 20,
-        where, dproj, normed_one, delta_wide, attended,
-        limit=60,
-    )
-    keep, give, gain_parts = fence((keep, give, gain_parts))
-    gains = add_up(gains, gain_parts)
-    gains = (gains + shift(gains, dcore=1)).astype(BF)
-    own, sends = blocks_z(where, keep, shift(give, dcore=1), gains)
-    home = exchange(back.reshape(128, 40, 128), None)
+        where, wide, early, proj, q_rows, k_rows, v_rows, lse, table, rope, all_gains, full, normed_one, attended, mlp_sum,
+    )
+    mine_delta, delta_sends, keep, give, late_parts = fence(
+        (mine_delta, delta_sends, keep, give, late_parts)
+    )
+    own, sends = blocks_z(where, keep, shift(give, dcore=1))
+    sends, delta_sends = fence((sends, delta_sends))
     early_parts = [shift(sends[k - 1], dz=k) for k in (1, 2, 3)]
-    early_parts[0], late_own, late_parts = fence((early_parts[0], late_own, late_parts))
+    delta_mine = add_up(mine_delta, collect(delta_sends)).astype(BF)
+    output_mine = lax.psum_scatter(
+        out_home, BOTH, scatter_dimension=0, tiled=True, axis_index_groups=SAME_X
+    )
+    back = jnp.concatenate(
+        [delta_mine.reshape(2, ROWS, 32, 128), output_mine.reshape(2, ROWS, 32, 128)], axis=2
+    )
+    home = exchange(back.reshape(32, 64, 128), TEAM).reshape(2, ROWS, 64, 128)
+    late_own, late_parts = fence((late_own, late_parts))
     late_total = add_up(late_own, late_parts)
     late_parts = [shift(take(late_total, where[2] + k).astype(BF), dy=k) for k in (1, 2, 3)]
     early_parts, late_parts = fence((early_parts, late_parts))
     late_total = add_up(take(late_total, where[2]), late_parts)
-    early_total = add_up(own, early_parts)
-    early_total = reduce_y(where, early_total)
+    early_total = reduce_y(where, add_up(own, early_parts))
     layer_output, input_grad = call(
         unsort_body,
         "vh",
         [("v", (2, TOK, 128), BF)] * 2,
-        [((2, ROWS, 4, 40, 128), BF)],
+        [((2, ROWS, 64, 128), BF)],
         2,
         4 * 2 * TOK * TOK * 128,
         2 << 20,
         token_route,
-        home.reshape(ROWS, 2, 4, 40, 128),
+        home,
         limit=60,
     )
-    gains = early_total[64:67].reshape(3 * 768)
+    gains = early_total[64:72]
+    gains = add_up(gains, [shift(gains, dx=k) for k in (1, 2, 3)])[0:3].reshape(3 * 768)
     early_total = early_total[0:64]
     return (
         layer_output,

time: 274 us -> 258 us (0.942)
  waiting for transfers between devices: 83.4 us -> 67.5 us
  starting transfers between devices: 56.6 us -> 67.4 us
  local copies, waits for them, and re-layouts: 16.2 us -> 10.7 us
  Pallas kernels: 60.8 us -> 56.7 us
  blocking collectives: 20.3 us -> 17 us
  other arithmetic: 18.8 us -> 21.9 us
    ppermute x21 -> x23, waiting for transfers between devices: 40 us -> 22.3 us  [shift(): return lax.ppermute(value, BOTH, moves(**step))]
    ppermute x21 -> x23, starting transfers between devices: 22.5 us -> 34.5 us  [shift(): return lax.ppermute(value, BOTH, moves(**step))]
    pallas_call x9 -> x8, Pallas kernels: 60.8 us -> 56.7 us  [call(): pl.pallas_call(body, out_shape=[jax.ShapeDtypeStruct(s, t) for _, s, t in...]
    all_to_all x1, blocking collectives: 20.3 us -> 17 us  [exchange(): lax.all_to_all(blocks, BOTH, 0, 0, axis_index_groups=groups, tiled=True)]
    unnamed x36 -> x42, local copies, waits for them, and re-layouts: 6.79 us -> 4.59 us
  transfers between devices with their start and end apart: 30 -> 32, of which waited for: 15 -> 13; matrix products, arithmetic and copies ran while one was open for 8% -> 10% of each run, Pallas kernels for 18% -> 16%
where the time goes in v1:
time: 258 us; the launch traced here: 257 us
  waiting for transfers between devices  67.5 us (26%)
  starting transfers between devices  67.4 us (26%)
  Pallas kernels  56.7 us (22%)
  other arithmetic  21.9 us (8%)
  blocking collectives  17 us (7%)
  between operations  16.3 us (6%)
  local copies, waits for them, and re-layouts  10.7 us (4%)
    pallas_call x8, Pallas kernels, call(): pl.pallas_call(body, out_shape=[jax.ShapeDtypeStruct(s, t) for _, s, t in...  56.7 us
    all_to_all x6, waiting for transfers between devices, exchange(): lax.all_to_all(blocks, BOTH, 0, 0, axis_index_groups=groups, tiled=True)  45.1 us
    ppermute x23, starting transfers between devices, shift(): return lax.ppermute(value, BOTH, moves(**step))  34.5 us
    all_to_all x6, starting transfers between devices, exchange(): lax.all_to_all(blocks, BOTH, 0, 0, axis_index_groups=groups, tiled=True)  32.9 us
    ppermute x23, waiting for transfers between devices, shift(): return lax.ppermute(value, BOTH, moves(**step))  22.3 us
    all_to_all x1, blocking collectives, exchange(): lax.all_to_all(blocks, BOTH, 0, 0, axis_index_groups=groups, tiled=True)  17 us
  transfers between devices with their start and end apart: 32, of which 13 were waited for; matrix products, arithmetic and copies ran while one was open for 10% of the time, Pallas kernels for 16%

profile of v1, /device:TPU:2, one launch (start us, length us, event | category | flops | bytes accessed | tf_op | source)
XLA Modules:
  0.0 257.4 jit_solution(5513656481138200752)
XLA Ops:
  10.4 3.7 %shard_map.255 = bf16[2,16,72,128]{3,2,1,0:T(8,128)(2,1)} custom-call(s32[2,512]{1,0:T(2,128)} %route_ref.3, bf16[2,512,128]{2,1,0:T(8,128)(2,1)} %x_hbm.1, bf16[2,512,128]{2,1,0:T(8,128)(2,1)} %g_hbm.1), custom_call_target="tpu_custom_call" | custom-call | flops 4194304 | bytes 65536 | tf_op jit(solution)/shard_map/pallas_call | solution.py:74
  14.1 8.3 %all-to-all-start = ((bf16[32,72,128]{2,1,0:T(8,128)(2,1)}), bf16[32,72,128]{2,1,0:T(8,128)(2,1)S(1)}, u32[]{:S(2)}, u32[]{:S(2)}) async-start(bf16[32,72,128]{2,1,0:T(8,128)(2,1)} %bitcast.71), calls=%async_computation | async-start | bytes 1179648 | tf_op jit(solution)/shard_map/all_to_all | solution.py:581
  25.9 9.9 %all-to-all-done = bf16[32,72,128]{2,1,0:T(8,128)(2,1)S(1)} async-done(((bf16[32,72,128]{2,1,0:T(8,128)(2,1)}), bf16[32,72,128]{2,1,0:T(8,128)(2,1)S(1)}, u32[]{:S(2)}, u32[]{:S(2)}) %all-to-all-start) | async-done | bytes 589856 | tf_op jit(solution)/shard_map/all_to_all | solution.py:581
  42.2 4.9 %all-to-all-start.1 = ((bf16[4,2,512,128]{3,2,1,0:T(8,128)(2,1)}), bf16[4,2,512,128]{3,2,1,0:T(8,128)(2,1)S(1)}, u32[]{:S(2)}, u32[]{:S(2)}) async-start(bf16[4,2,512,128]{3,2,1,0:T(8,128)(2,1)} %broadcast_in_dim.43), calls=%async_computation.1 | async-start | bytes 2097152 | tf_op jit(solution)/shard_map/all_to_all | solution.py:581
  50.8 13.2 %all-to-all-done.1.x_hbm = bf16[4,2,512,128]{3,2,1,0:T(8,128)(2,1)S(1)} async-done(((bf16[4,2,512,128]{3,2,1,0:T(8,128)(2,1)}), bf16[4,2,512,128]{3,2,1,0:T(8,128)(2,1)S(1)}, u32[]{:S(2)}, u32[]{:S(2)}) %all-to-all-start.1) | async-done | bytes 1048608 | tf_op jit(solution)/shard_map/all_to_all | solution.py:581
  65.0 10.0 %shard_map.256 = (bf16[4,2,512,128]{3,2,1,0:T(8,128)(2,1)}, bf16[512,1024]{1,0:T(8,128)(2,1)}, bf16[512,1024]{1,0:T(8,128)(2,1)}, f32[2,512,384]{2,1,0:T(8,128)}...) custom-call(bf16[4,2,512,128]{3,2,1,0:T(8,128)(2,1)} %copy-done.4, ...), custom_call_target="tpu_custom_call" | custom-call | flops 50331648 | bytes 262144 | tf_op jit(solution)/shard_map/pallas_call | solution.py:74
  75.0 17.0 %all_to_all.35.got_ref = bf16[4,2,512,128]{3,2,1,0:T(8,128)(2,1)S(1)} all-to-all(bf16[4,2,512,128]{3,2,1,0:T(8,128)(2,1)} %get-tuple-element.81), channel_id=1, replica_groups={{0,1,2,3},{4,5,6,7},{8,9,10,11},{12,13,14,15},{16,17,18,19},{20,21,22,2..., dimensions={0} | all-to-all | bytes 2097152 | tf_op jit(solution)/shard_map/all_to_all | solution.py:581
  93.2 5.0 %all-to-all-start.3 = ((bf16[4,2,512,128]{3,2,1,0:T(8,128)(2,1)}), bf16[4,2,512,128]{3,2,1,0:T(8,128)(2,1)S(1)}, u32[]{:S(2)}, u32[]{:S(2)}) async-start(bf16[4,2,512,128]{3,2,1,0:T(8,128)(2,1)} %shard_map.257), calls=%async_computation.3 | async-start | bytes 2097152 | tf_op jit(solution)/shard_map/all_to_all | solution.py:581
  98.8 11.9 %all-to-all-done.3.h_hbm = bf16[4,2,512,128]{3,2,1,0:T(8,128)(2,1)S(1)} async-done(((bf16[4,2,512,128]{3,2,1,0:T(8,128)(2,1)}), bf16[4,2,512,128]{3,2,1,0:T(8,128)(2,1)S(1)}, u32[]{:S(2)}, u32[]{:S(2)}) %all-to-all-start.3) | async-done | bytes 1048608 | tf_op jit(solution)/shard_map/all_to_all | solution.py:581
  111.7 12.7 %shard_map.258 = (bf16[4,2,512,128]{3,2,1,0:T(8,128)(2,1)}, bf16[512,1024]{1,0:T(8,128)(2,1)}, bf16[512,1024]{1,0:T(8,128)(2,1)}, bf16[2,512,384]{2,1,0:T(8,128)...) custom-call(s32[4]{0:T(128)} %pad_add_fusion.where_ref, bf16[4,2,512,128]{3,2,1,0:T(8,128)(2,1)} %copy-done.3, ...), custom_call_target="tpu_custom_call" | custom-call | flops 83886080 | bytes 262144 | tf_op jit(solution)/shard_map/pallas_call | solution.py:74
  124.4 4.9 %all-to-all-start.4 = ((bf16[4,2,512,128]{3,2,1,0:T(8,128)(2,1)}), bf16[4,2,512,128]{3,2,1,0:T(8,128)(2,1)S(1)}, u32[]{:S(2)}, u32[]{:S(2)}) async-start(bf16[4,2,512,128]{3,2,1,0:T(8,128)(2,1)} %get-tuple-element.86), calls=%async_computation.4 | async-start | bytes 2097152 | tf_op jit(solution)/shard_map/all_to_all | solution.py:581
  129.4 8.5 %shard_map.259 = (bf16[4,2,512,128]{3,2,1,0:T(8,128)(2,1)}, bf16[16,64,1152]{2,1,0:T(8,128)(2,1)}, bf16[16,64,1152]{2,1,0:T(8,128)(2,1)}) custom-call(s32[4]{0:T(128)} %pad_add_fusion.where_ref, bf16[2,512,384]{2,1,0:T(8,128)(2,1)} %get-tuple-element.87.hid_hbm, bf16[2,512,768]{2,1,0:T(8,128)(2,1)} %get-tuple-element.88.dgu_hbm, ...), custom_call_target="tpu_custom_call" | custom-call | flops 67108864 | bytes 262144 | tf_op jit(solution)/shard_map/pallas_call | solution.py:74
  137.9 3.6 %all-to-all-done.4.got_ref = bf16[4,2,512,128]{3,2,1,0:T(8,128)(2,1)S(1)} async-done(((bf16[4,2,512,128]{3,2,1,0:T(8,128)(2,1)}), bf16[4,2,512,128]{3,2,1,0:T(8,128)(2,1)S(1)}, u32[]{:S(2)}, u32[]{:S(2)}) %all-to-all-start.4) | async-done | bytes 1048608 | tf_op jit(solution)/shard_map/all_to_all | solution.py:581
  142.6 5.0 %all-to-all-start.5 = ((bf16[4,2,512,128]{3,2,1,0:T(8,128)(2,1)}), bf16[4,2,512,128]{3,2,1,0:T(8,128)(2,1)S(1)}, u32[]{:S(2)}, u32[]{:S(2)}) async-start(bf16[4,2,512,128]{3,2,1,0:T(8,128)(2,1)} %shard_map.260), calls=%async_computation.5 | async-start | bytes 2097152 | tf_op jit(solution)/shard_map/all_to_all | solution.py:581
  147.6 3.8 %add_bitcast_fusion = (f32[4,64,1152]{2,1,0:T(8,128)S(1)}, bf16[4,64,1152]{2,1,0:T(8,128)(2,1)S(1)}, bf16[4,64,1152]{2,1,0:T(8,128)(2,1)S(1)}, bf16[4,64,1152]{2,1,0:T(8,128)(2,1)}) fusion(bf16[4,4,64,1152]{3,2,1,0:T(8,128)(2,1)} %bitcast.18, s32[]{:T(128)S(6)} %select_n.199, bf16[4,4,64,1152]{3,2,1,0:T(8,128)(2,1)} %bitcast.72, s32[]{:T(128)S(6)} %select_n.197, ...), kind=kLoop, calls=%fused_computation.1 | loop fusion | flops 4423680 | bytes 7667728 | tf_op jit(solution)/shard_map/add | solution.py:602
  155.8 6.4 %all-to-all-done.5.d_hbm = bf16[4,2,512,128]{3,2,1,0:T(8,128)(2,1)S(1)} async-done(((bf16[4,2,512,128]{3,2,1,0:T(8,128)(2,1)}), bf16[4,2,512,128]{3,2,1,0:T(8,128)(2,1)S(1)}, u32[]{:S(2)}, u32[]{:S(2)}) %all-to-all-start.5) | async-done | bytes 1048608 | tf_op jit(solution)/shard_map/all_to_all | solution.py:581
  163.2 16.1 %shard_map.261 = (f32[2,512,128]{2,1,0:T(8,128)}, bf16[2,512,128]{2,1,0:T(8,128)(2,1)}, bf16[2,512,128]{2,1,0:T(8,128)(2,1)}, bf16[2,512,128]{2,1,0:T(8,128)(2,1...) custom-call(s32[4]{0:T(128)} %pad_add_fusion.where_ref, bf16[4,2,512,128]{3,2,1,0:T(8,128)(2,1)} %copy-done.5, ...), custom_call_target="tpu_custom_call" | custom-call | flops 117440512 | bytes 524288 | tf_op jit(solution)/shard_map/pallas_call | solution.py:74
  190.1 3.3 %collective-permute-start.9 = (bf16[2,512,128]{2,1,0:T(8,128)(2,1)}, bf16[2,512,128]{2,1,0:T(8,128)(2,1)S(1)}, u32[]{:S(2)}, u32[]{:S(2)}) collective-permute-start(bf16[2,512,128]{2,1,0:T(8,128)(2,1)} %get-tuple-element.120), channel_id=1, source_target_pairs={{0,2},{1,3},{2,0},{3,1},{8,10},{9,11},{10,8},{11,9},{4,6},{5,7},{6... | collective-permute-start | bytes 786440 | tf_op jit(solution)/shard_map/ppermute | solution.py:53
  195.9 4.6 %collective-permute-done.14 = bf16[64,1152]{1,0:T(8,128)(2,1)S(1)} collective-permute-done((bf16[64,1152]{1,0:T(8,128)(2,1)S(1)}, bf16[64,1152]{1,0:T(8,128)(2,1)S(1)}, u32[]{:S(2)}, u32[]{:S(2)}) %collective-permute-start.14) | collective-permute-done | bytes 147488 | tf_op jit(solution)/shard_map/ppermute | solution.py:53
  205.5 5.8 %collective-permute-done.9 = bf16[2,512,128]{2,1,0:T(8,128)(2,1)S(1)} collective-permute-done((bf16[2,512,128]{2,1,0:T(8,128)(2,1)}, bf16[2,512,128]{2,1,0:T(8,128)(2,1)S(1)}, u32[]{:S(2)}, u32[]{:S(2)}) %collective-permute-start.9) | collective-permute-done | bytes 262176 | tf_op jit(solution)/shard_map/ppermute | solution.py:53
  216.8 4.8 %all-to-all-start.6 = ((bf16[32,64,128]{2,1,0:T(8,128)(2,1)}), bf16[32,64,128]{2,1,0:T(8,128)(2,1)S(1)}, u32[]{:S(2)}, u32[]{:S(2)}) async-start(bf16[32,64,128]{2,1,0:T(8,128)(2,1)} %pad_maximum_fusion.1), calls=%async_computation.7 | async-start | bytes 1048576 | tf_op jit(solution)/shard_map/all_to_all | solution.py:581
  225.3 2.7 %collective-permute-start.18 = (bf16[72,768]{1,0:T(8,128)(2,1)S(1)}, bf16[72,768]{1,0:T(8,128)(2,1)S(1)}, u32[]{:S(2)}, u32[]{:S(2)}) collective-permute-start(bf16[72,768]{1,0:T(8,128)(2,1)S(1)} %get-tuple-element.155), channel_id=1, source_target_pairs={{0,16},{1,17},{2,18},{3,19},{8,24},{9,25},{10,26},{11,27},{4,20},{... | collective-permute-start | bytes 331784 | tf_op jit(solution)/shard_map/ppermute | solution.py:53
  238.9 2.8 %collective-permute-start.21 = (f32[8,768]{1,0:T(8,128)S(1)}, f32[8,768]{1,0:T(8,128)S(1)}, u32[]{:S(2)}, u32[]{:S(2)}) collective-permute-start(f32[8,768]{1,0:T(8,128)S(1)} %slice.97), channel_id=1, source_target_pairs={{0,2},{1,3},{2,0},{3,1},{8,10},{9,11},{10,8},{11,9},{4,6},{5,7},{6... | collective-permute-start | bytes 73736 | tf_op jit(solution)/shard_map/ppermute | solution.py:53
  247.4 3.4 %shard_map.262 = (bf16[2,512,128]{2,1,0:T(8,128)(2,1)}, bf16[2,512,128]{2,1,0:T(8,128)(2,1)}) custom-call(s32[2,512]{1,0:T(2,128)} %route_ref.3, bf16[2,16,64,128]{3,2,1,0:T(8,128)(2,1)} %bitcast.75), custom_call_target="tpu_custom_call" | custom-call | flops 4194304 | bytes 32768 | tf_op jit(solution)/shard_map/pallas_call | solution.py:74
  (143 shorter events, 69.0 us)
Async XLA Ops:
  7.2 56.8 %all-gather.5.cloned.1.call-start = ((), (), s32[]{:S(2)}) async-start(), calls=%async_computation.9 | async-start | bytes 3244032 | tf_op jit(solution)/shard_map/all_gather | solution.py:564
  8.7 102.0 %all-gather.7.cloned.1.call-start = ((), (), s32[]{:S(2)}) async-start(), calls=%async_computation.10 | async-start | bytes 4866048 | tf_op jit(solution)/shard_map/all_gather | solution.py:564
  14.1 21.7 %all-to-all-start = ((bf16[32,72,128]{2,1,0:T(8,128)(2,1)}), bf16[32,72,128]{2,1,0:T(8,128)(2,1)S(1)}, u32[]{:S(2)}, u32[]{:S(2)}) async-start(bf16[32,72,128]{2,1,0:T(8,128)(2,1)} %bitcast.71), calls=%async_computation | async-start | bytes 1179648 | tf_op jit(solution)/shard_map/all_to_all | solution.py:581
  35.8 39.1 %collective-permute-start = (bf16[2,512,128]{2,1,0:T(8,128)(2,1)S(1)}, bf16[2,512,128]{2,1,0:T(8,128)(2,1)S(1)}, u32[]{:S(2)}, u32[]{:S(2)}) collective-permute-start(bf16[2,512,128]{2,1,0:T(8,128)(2,1)S(1)} %bitcast.60), channel_id=1, source_target_pairs={{0,1},{1,2},{2,3},{3,0},{8,9},{9,10},{10,11},{11,8},{4,5},{5,6},{6... | collective-permute-start | bytes 786440 | tf_op jit(solution)/shard_map/ppermute | solution.py:53
  37.4 37.6 %collective-permute-start.1 = (bf16[2,512,128]{2,1,0:T(8,128)(2,1)S(1)}, bf16[2,512,128]{2,1,0:T(8,128)(2,1)S(1)}, u32[]{:S(2)}, u32[]{:S(2)}) collective-permute-start(bf16[2,512,128]{2,1,0:T(8,128)(2,1)S(1)} %bitcast.61), channel_id=1, source_target_pairs={{0,2},{1,3},{2,0},{3,1},{8,10},{9,11},{10,8},{11,9},{4,6},{5,7},{6... | collective-permute-start | bytes 786440 | tf_op jit(solution)/shard_map/ppermute | solution.py:53
  38.5 36.5 %collective-permute-start.2 = (bf16[2,512,128]{2,1,0:T(8,128)(2,1)S(1)}, bf16[2,512,128]{2,1,0:T(8,128)(2,1)S(1)}, u32[]{:S(2)}, u32[]{:S(2)}) collective-permute-start(bf16[2,512,128]{2,1,0:T(8,128)(2,1)S(1)} %bitcast.62), channel_id=1, source_target_pairs={{0,3},{1,0},{2,1},{3,2},{8,11},{9,8},{10,9},{11,10},{4,7},{5,4},{6... | collective-permute-start | bytes 786440 | tf_op jit(solution)/shard_map/ppermute | solution.py:53
  42.2 21.8 %all-to-all-start.1 = ((bf16[4,2,512,128]{3,2,1,0:T(8,128)(2,1)}), bf16[4,2,512,128]{3,2,1,0:T(8,128)(2,1)S(1)}, u32[]{:S(2)}, u32[]{:S(2)}) async-start(bf16[4,2,512,128]{3,2,1,0:T(8,128)(2,1)} %broadcast_in_dim.43), calls=%async_computation.1 | async-start | bytes 2097152 | tf_op jit(solution)/shard_map/all_to_all | solution.py:581
  93.2 17.5 %all-to-all-start.3 = ((bf16[4,2,512,128]{3,2,1,0:T(8,128)(2,1)}), bf16[4,2,512,128]{3,2,1,0:T(8,128)(2,1)S(1)}, u32[]{:S(2)}, u32[]{:S(2)}) async-start(bf16[4,2,512,128]{3,2,1,0:T(8,128)(2,1)} %shard_map.257), calls=%async_computation.3 | async-start | bytes 2097152 | tf_op jit(solution)/shard_map/all_to_all | solution.py:581
  124.4 17.0 %all-to-all-start.4 = ((bf16[4,2,512,128]{3,2,1,0:T(8,128)(2,1)}), bf16[4,2,512,128]{3,2,1,0:T(8,128)(2,1)S(1)}, u32[]{:S(2)}, u32[]{:S(2)}) async-start(bf16[4,2,512,128]{3,2,1,0:T(8,128)(2,1)} %get-tuple-element.86), calls=%async_computation.4 | async-start | bytes 2097152 | tf_op jit(solution)/shard_map/all_to_all | solution.py:581
  142.6 19.5 %all-to-all-start.5 = ((bf16[4,2,512,128]{3,2,1,0:T(8,128)(2,1)}), bf16[4,2,512,128]{3,2,1,0:T(8,128)(2,1)S(1)}, u32[]{:S(2)}, u32[]{:S(2)}) async-start(bf16[4,2,512,128]{3,2,1,0:T(8,128)(2,1)} %shard_map.260), calls=%async_computation.5 | async-start | bytes 2097152 | tf_op jit(solution)/shard_map/all_to_all | solution.py:581
  147.6 67.4 %reduce-scatter.2.cloned.1.call-start = ((), (), s32[]{:S(2)}) async-start(), calls=%async_computation.8 | async-start | bytes 1310720 | tf_op jit(solution)/shard_map/reduce_scatter | solution.py:756
  151.4 28.0 %collective-permute-start.4 = (bf16[4,64,1152]{2,1,0:T(8,128)(2,1)}, bf16[4,64,1152]{2,1,0:T(8,128)(2,1)}, u32[]{:S(2)}, u32[]{:S(2)}) collective-permute-start(bf16[4,64,1152]{2,1,0:T(8,128)(2,1)} %get-tuple-element.146), channel_id=1, source_target_pairs={{0,32},{1,33},{2,34},{3,35},{8,40},{9,41},{10,42},{11,43},{4,36},{... | collective-permute-start | bytes 1769480 | tf_op jit(solution)/shard_map/ppermute | solution.py:53
  152.5 29.1 %collective-permute-start.5 = (bf16[4,64,1152]{2,1,0:T(8,128)(2,1)S(1)}, bf16[4,64,1152]{2,1,0:T(8,128)(2,1)}, u32[]{:S(2)}, u32[]{:S(2)}) collective-permute-start(bf16[4,64,1152]{2,1,0:T(8,128)(2,1)S(1)} %get-tuple-element.145), channel_id=1, source_target_pairs={{0,64},{1,65},{2,66},{3,67},{8,72},{9,73},{10,74},{11,75},{4,68},{... | collective-permute-start | bytes 1769480 | tf_op jit(solution)/shard_map/ppermute | solution.py:53
  155.2 26.4 %collective-permute-start.6 = (bf16[4,64,1152]{2,1,0:T(8,128)(2,1)S(1)}, bf16[4,64,1152]{2,1,0:T(8,128)(2,1)}, u32[]{:S(2)}, u32[]{:S(2)}) collective-permute-start(bf16[4,64,1152]{2,1,0:T(8,128)(2,1)S(1)} %get-tuple-element.144), channel_id=1, source_target_pairs={{0,96},{1,97},{2,98},{3,99},{8,104},{9,105},{10,106},{11,107},{4,1... | collective-permute-start | bytes 1769480 | tf_op jit(solution)/shard_map/ppermute | solution.py:53
  188.0 14.0 %collective-permute-start.10 = (bf16[2,512,128]{2,1,0:T(8,128)(2,1)S(1)}, bf16[2,512,128]{2,1,0:T(8,128)(2,1)S(1)}, u32[]{:S(2)}, u32[]{:S(2)}) collective-permute-start(bf16[2,512,128]{2,1,0:T(8,128)(2,1)S(1)} %copy-done.19), channel_id=1, source_target_pairs={{0,3},{1,0},{2,1},{3,2},{8,11},{9,8},{10,9},{11,10},{4,7},{5,4},{6... | collective-permute-start | bytes 786440 | tf_op jit(solution)/shard_map/ppermute | solution.py:53
  188.4 15.6 %collective-permute-start.8 = (bf16[2,512,128]{2,1,0:T(8,128)(2,1)}, bf16[2,512,128]{2,1,0:T(8,128)(2,1)S(1)}, u32[]{:S(2)}, u32[]{:S(2)}) collective-permute-start(bf16[2,512,128]{2,1,0:T(8,128)(2,1)} %get-tuple-element.119), channel_id=1, source_target_pairs={{0,1},{1,2},{2,3},{3,0},{8,9},{9,10},{10,11},{11,8},{4,5},{5,6},{6... | collective-permute-start | bytes 786440 | tf_op jit(solution)/shard_map/ppermute | solution.py:53
  190.1 21.3 %collective-permute-start.9 = (bf16[2,512,128]{2,1,0:T(8,128)(2,1)}, bf16[2,512,128]{2,1,0:T(8,128)(2,1)S(1)}, u32[]{:S(2)}, u32[]{:S(2)}) collective-permute-start(bf16[2,512,128]{2,1,0:T(8,128)(2,1)} %get-tuple-element.120), channel_id=1, source_target_pairs={{0,2},{1,3},{2,0},{3,1},{8,10},{9,11},{10,8},{11,9},{4,6},{5,7},{6... | collective-permute-start | bytes 786440 | tf_op jit(solution)/shard_map/ppermute | solution.py:53
  195.1 26.5 %collective-permute-start.11 = (bf16[4,72,768]{2,1,0:T(8,128)(2,1)}, bf16[4,72,768]{2,1,0:T(8,128)(2,1)}, u32[]{:S(2)}, u32[]{:S(2)}) collective-permute-start(bf16[4,72,768]{2,1,0:T(8,128)(2,1)} %get-tuple-element.125), channel_id=1, source_target_pairs={{0,32},{1,33},{2,34},{3,35},{8,40},{9,41},{10,42},{11,43},{4,36},{... | collective-permute-start | bytes 1327112 | tf_op jit(solution)/shard_map/ppermute | solution.py:53
  200.5 21.1 %collective-permute-start.12 = (bf16[4,72,768]{2,1,0:T(8,128)(2,1)S(1)}, bf16[4,72,768]{2,1,0:T(8,128)(2,1)}, u32[]{:S(2)}, u32[]{:S(2)}) collective-permute-start(bf16[4,72,768]{2,1,0:T(8,128)(2,1)S(1)} %get-tuple-element.126), channel_id=1, source_target_pairs={{0,64},{1,65},{2,66},{3,67},{8,72},{9,73},{10,74},{11,75},{4,68},{... | collective-permute-start | bytes 1327112 | tf_op jit(solution)/shard_map/ppermute | solution.py:53
  202.0 19.5 %collective-permute-start.13 = (bf16[4,72,768]{2,1,0:T(8,128)(2,1)S(1)}, bf16[4,72,768]{2,1,0:T(8,128)(2,1)}, u32[]{:S(2)}, u32[]{:S(2)}) collective-permute-start(bf16[4,72,768]{2,1,0:T(8,128)(2,1)S(1)} %get-tuple-element.127), channel_id=1, source_target_pairs={{0,96},{1,97},{2,98},{3,99},{8,104},{9,105},{10,106},{11,107},{4,1... | collective-permute-start | bytes 1327112 | tf_op jit(solution)/shard_map/ppermute | solution.py:53
  204.1 17.5 %collective-permute-start.15 = (bf16[64,1152]{1,0:T(8,128)(2,1)}, bf16[64,1152]{1,0:T(8,128)(2,1)}, u32[]{:S(2)}, u32[]{:S(2)}) collective-permute-start(bf16[64,1152]{1,0:T(8,128)(2,1)} %get-tuple-element.151), channel_id=1, source_target_pairs={{0,16},{1,17},{2,18},{3,19},{8,24},{9,25},{10,26},{11,27},{4,20},{... | collective-permute-start | bytes 442376 | tf_op jit(solution)/shard_map/ppermute | solution.py:53
  216.8 29.9 %all-to-all-start.6 = ((bf16[32,64,128]{2,1,0:T(8,128)(2,1)}), bf16[32,64,128]{2,1,0:T(8,128)(2,1)S(1)}, u32[]{:S(2)}, u32[]{:S(2)}) async-start(bf16[32,64,128]{2,1,0:T(8,128)(2,1)} %pad_maximum_fusion.1), calls=%async_computation.7 | async-start | bytes 1048576 | tf_op jit(solution)/shard_map/all_to_all | solution.py:581
  223.5 10.3 %collective-permute-start.17 = (bf16[72,768]{1,0:T(8,128)(2,1)S(1)}, bf16[72,768]{1,0:T(8,128)(2,1)S(1)}, u32[]{:S(2)}, u32[]{:S(2)}) collective-permute-start(bf16[72,768]{1,0:T(8,128)(2,1)S(1)} %get-tuple-element.153), channel_id=1, source_target_pairs={{0,4},{1,5},{2,6},{3,7},{8,12},{9,13},{10,14},{11,15},{4,16},{5,17... | collective-permute-start | bytes 331784 | tf_op jit(solution)/shard_map/ppermute | solution.py:53
  225.3 10.9 %collective-permute-start.18 = (bf16[72,768]{1,0:T(8,128)(2,1)S(1)}, bf16[72,768]{1,0:T(8,128)(2,1)S(1)}, u32[]{:S(2)}, u32[]{:S(2)}) collective-permute-start(bf16[72,768]{1,0:T(8,128)(2,1)S(1)} %get-tuple-element.155), channel_id=1, source_target_pairs={{0,16},{1,17},{2,18},{3,19},{8,24},{9,25},{10,26},{11,27},{4,20},{... | collective-permute-start | bytes 331784 | tf_op jit(solution)/shard_map/ppermute | solution.py:53
  (29 other events, 249.6 us)
Sparse Core Ops, SparseCore 0:
  10.9 50.4 all-gather.4
  63.6 46.2 all-gather.6
  181.7 27.0 reduce-scatter.1

commit v2 on v1

--- a/solution.py
+++ b/solution.py
@@ -420,10 +420,10 @@
 
 def attend_back_body(
     where_ref, d_hbm, w_hbm, proj_hbm, q_hbm, k_hbm, v_hbm, lse_hbm, table_hbm,
-    rope_hbm, gain_hbm, full_hbm, n_hbm, a_hbm, mlp_sum_hbm,
-    own_hbm, send1, send2, send3, keep_hbm, give_hbm,
+    rope_hbm, gain_hbm, full_hbm, n_hbm, a_hbm, mlp_sum_hbm, out_hbm,
+    back_hbm, keep_hbm, give_hbm, gains_hbm,
     delta_ref, w_ref, proj_ref, q_ref, k_ref, v_ref, lse_ref, table_ref, rope_ref, gain_ref, bias_ref, dk_ref, dv_ref,
-    da_ref, dproj_ref, full_ref, part_ref, own_ref, back_ref, n_ref, a_ref, wide_ref, thin_ref, keep_ref, give_ref,
+    da_ref, dproj_ref, full_ref, part_ref, back_ref, n_ref, a_ref, wide_ref, thin_ref, keep_ref, give_ref,
     head_ref, sum_ref, mlp_sum_ref, rows_ref, sems,
 ):
     x, core = where_ref[0], where_ref[3]
@@ -448,6 +448,7 @@
         mover.start(full_hbm, full_ref),
     ]
     much = [mover.start(n_hbm, n_ref), mover.start(a_hbm, a_ref)]
+    last = mover.start(out_hbm, back_ref.at[:, :, :, 1])
     head_ref[...] = jnp.zeros_like(head_ref)
     sum_ref[...] = jnp.zeros_like(sum_ref)
     dk_ref[...] = jnp.zeros_like(dk_ref)
@@ -507,8 +508,8 @@
             thin_ref[...] = nn(delta, a_ref[y]).astype(BF)
             store_grad(thin_ref, core, j, y, slice(512, 768), keep_ref, give_ref)
         done = pl.ds(j * 4, 4)
-        stores.append(mover.start(give_ref.at[done], give_hbm.at[done, pl.ds(0, 64)]))
-        stores.append(mover.start(keep_ref.at[done], keep_hbm.at[done, pl.ds(0, 64)]))
+        stores.append(mover.start(give_ref.at[done], give_hbm.at[done]))
+        stores.append(mover.start(keep_ref.at[done], keep_hbm.at[done]))
     wait(more)
     for i in range(TOK // TILE):
         rows = pl.ds(i * TILE, TILE)
@@ -524,26 +525,23 @@
         part_ref[...] = inv * (scaled - hat * inner)
         for y in range(2):
             part_ref[:, mine(x, y)] += delta_ref[rows, mine(x, y)].astype(F32)
-        for y in range(2):
-            own_ref[y, rows, :] = part_ref[:, mine(x, y)]
-            for k in range(3):
-                back_ref[k, y, rows, :] = part_ref[:, mine(lax.rem(x + k + 1, 4), y)].astype(BF)
-        stores.append(mover.start(own_ref.at[:, rows], own_hbm.at[:, rows]))
-        for k, send in enumerate((send1, send2, send3)):
-            stores.append(mover.start(back_ref.at[k, :, rows], send.at[:, rows]))
+        places = pl.ds(i * (TILE // 32), TILE // 32)
+        for k in range(4):
+            for y in range(2):
+                lanes = slice(y * 512 + k * 128, y * 512 + k * 128 + 128)
+                back_ref[k, y, places, 0] = part_ref[:, lanes].astype(BF).reshape(TILE // 32, 32, 128)
+        if i == 0:
+            last.wait()
+        stores.append(mover.start(back_ref.at[:, :, places], back_hbm.at[:, :, places]))
     attn_sum, mlp_sum = sum_ref[0:1, :], mlp_sum_ref[0:1, :]
-    gains = jnp.concatenate(
-        [
-            attn_sum[:, 0:768],
-            jnp.concatenate([attn_sum[:, 768:1024], mlp_sum[:, 0:512]], axis=1),
-            jnp.concatenate([mlp_sum[:, 512:1024], head_ref[0:1, :], head_ref[1:2, :]], axis=1),
-            jnp.zeros((5, 768), F32),
-        ],
-        axis=0,
-    )
-    rows_ref[...] = jnp.broadcast_to(gains[None], (16, 8, 768)).astype(BF)
-    stores.append(mover.start(rows_ref, keep_hbm.at[:, pl.ds(64, 8)]))
-    stores.append(mover.start(rows_ref, give_hbm.at[:, pl.ds(64, 8)]))
+    rows_ref[0:1, :] = attn_sum[:, 0:768]
+    rows_ref[1:2, 0:256] = attn_sum[:, 768:1024]
+    rows_ref[1:2, 256:768] = mlp_sum[:, 0:512]
+    rows_ref[2:3, 0:512] = mlp_sum[:, 512:1024]
+    rows_ref[2:3, 512:640] = head_ref[0:1, :]
+    rows_ref[2:3, 640:768] = head_ref[1:2, :]
+    rows_ref[3:8, :] = jnp.zeros((5, 768), F32)
+    stores.append(mover.start(rows_ref, gains_hbm))
     wait(stores)
 
 
@@ -656,7 +654,9 @@
     arrived = exchange(sorted_rows.reshape(32, 72, 128), TEAM).reshape(2, ROWS, 72, 128)
     my_input = arrived[:, :, 0:32, :].reshape(FEATURES)
     inputs = exchange(repeat(my_input), SAME_X)
-    grads = spread(arrived[:, :, 32:64, :].reshape(FEATURES))
+    my_grad = arrived[:, :, 32:64, :].reshape(FEATURES)
+    inputs, my_grad = fence((inputs, my_grad))
+    grads = spread(my_grad)
     codes = arrived[0, :, 64, 0:64].astype(F32)
     slots = (codes[:, 0:32] * 16 + codes[:, 32:64]).astype(jnp.int32).reshape(TOK)
 
@@ -731,41 +731,41 @@
     late_parts = [shift(late_sends[k - 1], dz=k) for k in (1, 2, 3)]
     wide, _ = fence((wide, late_sends))
 
-    mine_delta, *delta_sends, keep, give = call(
+    back, keep, give, gains = call(
         attend_back_body,
-        "s" + "h" * 14,
-        [("h", FEATURES, F32)] + [("h", FEATURES, BF)] * 3 + [("h", (16, 72, 768), BF)] * 2,
+        "s" + "h" * 15,
+        [("h", (4, 2, ROWS, 2, 32, 128), BF)] + [("h", (16, 64, 768), BF)] * 2 + [("h", (8, 768), F32)],
         [((TOK, D), BF), (EARLY + (768,), BF), ((2, TOK, 384), F32), ((2, TOK, 256), BF), (FEATURES, BF), (FEATURES, BF),
          ((TOK, 128), F32), ((8, TOK), F32), ((TOK, 256), F32), ((8, D), F32), ((TOK, TOK), F32), ((2, 128, TOK), F32),
          ((2, 128, TOK), F32), ((TILE, 256), BF), ((2, TOK, 512), BF), ((TOK, D), BF), ((TILE, D), F32),
-         (FEATURES, F32), ((3,) + FEATURES, BF), ((TOK, D), BF), ((2, TOK, 256), BF), ((256, 512), BF), ((256, 256), BF)]
+         ((4, 2, ROWS, 2, 32, 128), BF), ((TOK, D), BF), ((2, TOK, 256), BF), ((256, 512), BF), ((256, 256), BF)]
         + [((16, 64, 768), BF)] * 2
-        + [((8, 128), F32), ((8, D), F32), ((8, D), F32), ((16, 8, 768), BF)],
+        + [((8, 128), F32), ((8, D), F32), ((8, D), F32), ((8, 768), F32)],
         52,
         7 << 30,
         32 << 20,
         where, wide, early, proj, q_rows, k_rows, v_rows, lse, table, rope, all_gains, full, normed_one, attended, mlp_sum,
-    )
-    mine_delta, delta_sends, keep, give, late_parts = fence(
-        (mine_delta, delta_sends, keep, give, late_parts)
-    )
+        out_home.reshape(4, 2, ROWS, 32, 128),
+    )
+    back, keep, give, gains, late_parts = fence((back, keep, give, gains, late_parts))
+    gains = add_up(gains, [shift(gains, dx=k) for k in (1, 2, 3)])
+    gains = (gains + shift(gains, dcore=1)).astype(BF)
     own, sends = blocks_z(where, keep, shift(give, dcore=1))
-    sends, delta_sends = fence((sends, delta_sends))
+    gains = jnp.broadcast_to(gains[None], (4, 8, 768))
+    own, *sends = [jnp.concatenate([rows, gains.astype(rows.dtype)], axis=1) for rows in [own] + sends]
+    back = lax.psum_scatter(
+        back, BOTH, scatter_dimension=0, tiled=True, axis_index_groups=SAME_X
+    )
+    home = exchange(back.reshape(32, 64, 128), TEAM).reshape(2, ROWS, 64, 128)
+    sends, late_own, late_parts = fence((sends, late_own, late_parts))
     early_parts = [shift(sends[k - 1], dz=k) for k in (1, 2, 3)]
-    delta_mine = add_up(mine_delta, collect(delta_sends)).astype(BF)
-    output_mine = lax.psum_scatter(
-        out_home, BOTH, scatter_dimension=0, tiled=True, axis_index_groups=SAME_X
-    )
-    back = jnp.concatenate(
-        [delta_mine.reshape(2, ROWS, 32, 128), output_mine.reshape(2, ROWS, 32, 128)], axis=2
-    )
-    home = exchange(back.reshape(32, 64, 128), TEAM).reshape(2, ROWS, 64, 128)
-    late_own, late_parts = fence((late_own, late_parts))
     late_total = add_up(late_own, late_parts)
     late_parts = [shift(take(late_total, where[2] + k).astype(BF), dy=k) for k in (1, 2, 3)]
     early_parts, late_parts = fence((early_parts, late_parts))
     late_total = add_up(take(late_total, where[2]), late_parts)
-    early_total = reduce_y(where, add_up(own, early_parts))
+    early_parts, home = fence((early_parts, home))
+    early_total = add_up(own, early_parts)
+    early_total = reduce_y(where, early_total)
     layer_output, input_grad = call(
         unsort_body,
         "vh",
@@ -778,8 +778,7 @@
         home,
         limit=60,
     )
-    gains = early_total[64:72]
-    gains = add_up(gains, [shift(gains, dx=k) for k in (1, 2, 3)])[0:3].reshape(3 * 768)
+    gains = early_total[64:67].reshape(3 * 768)
     early_total = early_total[0:64]
     return (
         layer_output,

time: 258 us -> 252 us (0.977)
  local copies, waits for them, and re-layouts: 10.7 us -> 6.55 us
  starting transfers between devices: 67.4 us -> 63.5 us
  other arithmetic: 21.9 us -> 18.2 us
    ppermute x23 -> x21, waiting for transfers between devices: 22.3 us -> 10 us  [shift(): return lax.ppermute(value, BOTH, moves(**step))]
    all_to_all x6, waiting for transfers between devices: 45.1 us -> 57 us  [exchange(): lax.all_to_all(blocks, BOTH, 0, 0, axis_index_groups=groups, tiled=True)]
    ppermute x23 -> x21, starting transfers between devices: 34.5 us -> 28.1 us  [shift(): return lax.ppermute(value, BOTH, moves(**step))]
    convert_element_type x2 -> x1, other arithmetic: 3.5 us -> 0.01 us  [body(): gains = (gains + shift(gains, dcore=1)).astype(BF)]
    unnamed x42 -> x34, local copies, waits for them, and re-layouts: 4.59 us -> 1.15 us
    add x1 -> x2, other arithmetic: 3.76 us -> 5.57 us  [block(): take(keep, where[1] + k).astype(F32) + take(other, where[1] + k).astype(F32)]
  transfers between devices with their start and end apart: 32 -> 30, of which waited for: 13 -> 15; matrix products, arithmetic and copies ran while one was open for 10% -> 7% of each run, Pallas kernels for 16% -> 18%
where the time goes in v2:
time: 252 us; the launch traced here: 249 us
  waiting for transfers between devices  69.5 us (28%)
  starting transfers between devices  63.5 us (25%)
  Pallas kernels  56.8 us (23%)
  other arithmetic  18.2 us (7%)
  blocking collectives  18.2 us (7%)
  between operations  16.3 us (6%)
  local copies, waits for them, and re-layouts  6.55 us (3%)
    all_to_all x6, waiting for transfers between devices, exchange(): lax.all_to_all(blocks, BOTH, 0, 0, axis_index_groups=groups, tiled=True)  57 us
    pallas_call x8, Pallas kernels, call(): pl.pallas_call(body, out_shape=[jax.ShapeDtypeStruct(s, t) for _, s, t in...  56.8 us
    all_to_all x6, starting transfers between devices, exchange(): lax.all_to_all(blocks, BOTH, 0, 0, axis_index_groups=groups, tiled=True)  35.3 us
    ppermute x21, starting transfers between devices, shift(): return lax.ppermute(value, BOTH, moves(**step))  28.1 us
    all_to_all x1, blocking collectives, exchange(): lax.all_to_all(blocks, BOTH, 0, 0, axis_index_groups=groups, tiled=True)  18.2 us
    ppermute x21, waiting for transfers between devices, shift(): return lax.ppermute(value, BOTH, moves(**step))  10 us
    add x2, other arithmetic, block(): take(keep, where[1] + k).astype(F32) + take(other, where[1] + k).astype(F32)  5.57 us
  transfers between devices with their start and end apart: 30, of which 15 were waited for; matrix products, arithmetic and copies ran while one was open for 7% of the time, Pallas kernels for 18%

profile of v2, /device:TPU:2, one launch (start us, length us, event | category | flops | bytes accessed | tf_op | source)
XLA Modules:
  0.0 249.2 jit_solution(11239856337159273640)
XLA Ops:
  10.4 3.7 %shard_map.255 = bf16[2,16,72,128]{3,2,1,0:T(8,128)(2,1)} custom-call(s32[2,512]{1,0:T(2,128)} %route_ref.3, bf16[2,512,128]{2,1,0:T(8,128)(2,1)} %x_hbm.1, bf16[2,512,128]{2,1,0:T(8,128)(2,1)} %g_hbm.1), custom_call_target="tpu_custom_call" | custom-call | flops 4194304 | bytes 65536 | tf_op jit(solution)/shard_map/pallas_call | solution.py:74
  14.1 8.3 %all-to-all-start = ((bf16[32,72,128]{2,1,0:T(8,128)(2,1)}), bf16[32,72,128]{2,1,0:T(8,128)(2,1)S(1)}, u32[]{:S(2)}, u32[]{:S(2)}) async-start(bf16[32,72,128]{2,1,0:T(8,128)(2,1)} %bitcast.71), calls=%async_computation | async-start | bytes 1179648 | tf_op jit(solution)/shard_map/all_to_all | solution.py:579
  25.9 9.9 %all-to-all-done = bf16[32,72,128]{2,1,0:T(8,128)(2,1)S(1)} async-done(((bf16[32,72,128]{2,1,0:T(8,128)(2,1)}), bf16[32,72,128]{2,1,0:T(8,128)(2,1)S(1)}, u32[]{:S(2)}, u32[]{:S(2)}) %all-to-all-start) | async-done | bytes 589856 | tf_op jit(solution)/shard_map/all_to_all | solution.py:579
  37.0 4.8 %all-to-all-start.1 = ((bf16[4,2,512,128]{3,2,1,0:T(8,128)(2,1)}), bf16[4,2,512,128]{3,2,1,0:T(8,128)(2,1)S(1)}, u32[]{:S(2)}, u32[]{:S(2)}) async-start(bf16[4,2,512,128]{3,2,1,0:T(8,128)(2,1)} %broadcast_in_dim.51), calls=%async_computation.1 | async-start | bytes 2097152 | tf_op jit(solution)/shard_map/all_to_all | solution.py:579
  43.9 12.0 %all-to-all-done.1.x_hbm = bf16[4,2,512,128]{3,2,1,0:T(8,128)(2,1)S(1)} async-done(((bf16[4,2,512,128]{3,2,1,0:T(8,128)(2,1)}), bf16[4,2,512,128]{3,2,1,0:T(8,128)(2,1)S(1)}, u32[]{:S(2)}, u32[]{:S(2)}) %all-to-all-start.1) | async-done | bytes 1048608 | tf_op jit(solution)/shard_map/all_to_all | solution.py:579
  55.9 3.5 %collective-permute-start.1 = (bf16[2,512,128]{2,1,0:T(8,128)(2,1)S(1)}, bf16[2,512,128]{2,1,0:T(8,128)(2,1)S(1)}, u32[]{:S(2)}, u32[]{:S(2)}) collective-permute-start(bf16[2,512,128]{2,1,0:T(8,128)(2,1)S(1)} %bitcast.61), channel_id=1, source_target_pairs={{0,2},{1,3},{2,0},{3,1},{8,10},{9,11},{10,8},{11,9},{4,6},{5,7},{6... | collective-permute-start | bytes 786440 | tf_op jit(solution)/shard_map/ppermute | solution.py:53
  62.0 9.9 %shard_map.256 = (bf16[4,2,512,128]{3,2,1,0:T(8,128)(2,1)}, bf16[512,1024]{1,0:T(8,128)(2,1)}, bf16[512,1024]{1,0:T(8,128)(2,1)}, f32[2,512,384]{2,1,0:T(8,128)}...) custom-call(bf16[4,2,512,128]{3,2,1,0:T(8,128)(2,1)} %copy-done.5, ...), custom_call_target="tpu_custom_call" | custom-call | flops 50331648 | bytes 262144 | tf_op jit(solution)/shard_map/pallas_call | solution.py:74
  72.0 18.2 %all_to_all.35.got_ref = bf16[4,2,512,128]{3,2,1,0:T(8,128)(2,1)S(1)} all-to-all(bf16[4,2,512,128]{3,2,1,0:T(8,128)(2,1)} %get-tuple-element.82), channel_id=1, replica_groups={{0,1,2,3},{4,5,6,7},{8,9,10,11},{12,13,14,15},{16,17,18,19},{20,21,22,2..., dimensions={0} | all-to-all | bytes 2097152 | tf_op jit(solution)/shard_map/all_to_all | solution.py:579
  91.4 5.0 %all-to-all-start.3 = ((bf16[4,2,512,128]{3,2,1,0:T(8,128)(2,1)}), bf16[4,2,512,128]{3,2,1,0:T(8,128)(2,1)S(1)}, u32[]{:S(2)}, u32[]{:S(2)}) async-start(bf16[4,2,512,128]{3,2,1,0:T(8,128)(2,1)} %shard_map.257), calls=%async_computation.3 | async-start | bytes 2097152 | tf_op jit(solution)/shard_map/all_to_all | solution.py:579
  97.0 12.0 %all-to-all-done.3.h_hbm = bf16[4,2,512,128]{3,2,1,0:T(8,128)(2,1)S(1)} async-done(((bf16[4,2,512,128]{3,2,1,0:T(8,128)(2,1)}), bf16[4,2,512,128]{3,2,1,0:T(8,128)(2,1)S(1)}, u32[]{:S(2)}, u32[]{:S(2)}) %all-to-all-start.3) | async-done | bytes 1048608 | tf_op jit(solution)/shard_map/all_to_all | solution.py:579
  109.9 12.8 %shard_map.258 = (bf16[4,2,512,128]{3,2,1,0:T(8,128)(2,1)}, bf16[512,1024]{1,0:T(8,128)(2,1)}, bf16[512,1024]{1,0:T(8,128)(2,1)}, bf16[2,512,384]{2,1,0:T(8,128)...) custom-call(s32[4]{0:T(128)} %pad_add_fusion.where_ref, bf16[4,2,512,128]{3,2,1,0:T(8,128)(2,1)} %copy-done.3, ...), custom_call_target="tpu_custom_call" | custom-call | flops 83886080 | bytes 262144 | tf_op jit(solution)/shard_map/pallas_call | solution.py:74
  122.7 4.9 %all-to-all-start.4 = ((bf16[4,2,512,128]{3,2,1,0:T(8,128)(2,1)}), bf16[4,2,512,128]{3,2,1,0:T(8,128)(2,1)S(1)}, u32[]{:S(2)}, u32[]{:S(2)}) async-start(bf16[4,2,512,128]{3,2,1,0:T(8,128)(2,1)} %get-tuple-element.87), calls=%async_computation.4 | async-start | bytes 2097152 | tf_op jit(solution)/shard_map/all_to_all | solution.py:579
  127.7 8.5 %shard_map.259 = (bf16[4,2,512,128]{3,2,1,0:T(8,128)(2,1)}, bf16[16,64,1152]{2,1,0:T(8,128)(2,1)}, bf16[16,64,1152]{2,1,0:T(8,128)(2,1)}) custom-call(s32[4]{0:T(128)} %pad_add_fusion.where_ref, bf16[2,512,384]{2,1,0:T(8,128)(2,1)} %get-tuple-element.88.hid_hbm, bf16[2,512,768]{2,1,0:T(8,128)(2,1)} %get-tuple-element.89.dgu_hbm, ...), custom_call_target="tpu_custom_call" | custom-call | flops 67108864 | bytes 262144 | tf_op jit(solution)/shard_map/pallas_call | solution.py:74
  136.2 5.4 %all-to-all-done.4.got_ref = bf16[4,2,512,128]{3,2,1,0:T(8,128)(2,1)S(1)} async-done(((bf16[4,2,512,128]{3,2,1,0:T(8,128)(2,1)}), bf16[4,2,512,128]{3,2,1,0:T(8,128)(2,1)S(1)}, u32[]{:S(2)}, u32[]{:S(2)}) %all-to-all-start.4) | async-done | bytes 1048608 | tf_op jit(solution)/shard_map/all_to_all | solution.py:579
  142.7 5.0 %all-to-all-start.5 = ((bf16[4,2,512,128]{3,2,1,0:T(8,128)(2,1)}), bf16[4,2,512,128]{3,2,1,0:T(8,128)(2,1)S(1)}, u32[]{:S(2)}, u32[]{:S(2)}) async-start(bf16[4,2,512,128]{3,2,1,0:T(8,128)(2,1)} %shard_map.260), calls=%async_computation.5 | async-start | bytes 2097152 | tf_op jit(solution)/shard_map/all_to_all | solution.py:579
  147.7 3.8 %add_bitcast_fusion = (f32[4,64,1152]{2,1,0:T(8,128)S(1)}, bf16[4,64,1152]{2,1,0:T(8,128)(2,1)S(1)}, bf16[4,64,1152]{2,1,0:T(8,128)(2,1)S(1)}, bf16[4,64,1152]{2,1,0:T(8,128)(2,1)}) fusion(bf16[4,4,64,1152]{3,2,1,0:T(8,128)(2,1)} %bitcast.18, s32[]{:T(128)S(6)} %select_n.199, bf16[4,4,64,1152]{3,2,1,0:T(8,128)(2,1)} %bitcast.72, s32[]{:T(128)S(6)} %select_n.197, ...), kind=kLoop, calls=%fused_computation.1 | loop fusion | flops 4423680 | bytes 7667728 | tf_op jit(solution)/shard_map/add | solution.py:600
  155.8 6.4 %all-to-all-done.5.d_hbm = bf16[4,2,512,128]{3,2,1,0:T(8,128)(2,1)S(1)} async-done(((bf16[4,2,512,128]{3,2,1,0:T(8,128)(2,1)}), bf16[4,2,512,128]{3,2,1,0:T(8,128)(2,1)S(1)}, u32[]{:S(2)}, u32[]{:S(2)}) %all-to-all-start.5) | async-done | bytes 1048608 | tf_op jit(solution)/shard_map/all_to_all | solution.py:579
  163.3 16.2 %shard_map.261 = (bf16[4,2,16,2,32,128]{5,4,3,2,1,0:T(8,128)(2,1)}, bf16[16,64,768]{2,1,0:T(8,128)(2,1)}, bf16[16,64,768]{2,1,0:T(8,128)(2,1)}, f32[8,768]{1,0:T(8,128)}) custom-call(s32[4]{0:T(128)} %pad_add_fusion.where_ref, bf16[4,2,512,128]{3,2,1,0:T(8,128)(2,1)} %copy-done.4, bf16[8,2,2,64,768]{4,3,2,1,0:T(8,128)(2,1)} %bitcast.70, ...), custom_call_target="tpu_custom_call" | custom-call | flops 117440512 | bytes 524288 | tf_op jit(solution)/shard_map/pallas_call | solution.py:74
  183.9 3.3 %collective-permute-start.9 = (f32[8,768]{1,0:T(8,128)S(1)}, f32[8,768]{1,0:T(8,128)S(1)}, u32[]{:S(2)}, u32[]{:S(2)}) collective-permute-start(f32[8,768]{1,0:T(8,128)S(1)} %copy-done.11), channel_id=1, source_target_pairs={{0,2},{1,3},{2,0},{3,1},{8,10},{9,11},{10,8},{11,9},{4,6},{5,7},{6... | collective-permute-start | bytes 73736 | tf_op jit(solution)/shard_map/ppermute | solution.py:53
  194.6 2.9 %collective-permute-start.13 = (bf16[4,72,768]{2,1,0:T(8,128)(2,1)}, bf16[4,72,768]{2,1,0:T(8,128)(2,1)}, u32[]{:S(2)}, u32[]{:S(2)}) collective-permute-start(bf16[4,72,768]{2,1,0:T(8,128)(2,1)} %get-tuple-element.120), channel_id=1, source_target_pairs={{0,64},{1,65},{2,66},{3,67},{8,72},{9,73},{10,74},{11,75},{4,68},{... | collective-permute-start | bytes 1327112 | tf_op jit(solution)/shard_map/ppermute | solution.py:53
  203.3 3.4 %collective-permute-done.15 = bf16[64,1152]{1,0:T(8,128)(2,1)S(1)} collective-permute-done((bf16[64,1152]{1,0:T(8,128)(2,1)S(1)}, bf16[64,1152]{1,0:T(8,128)(2,1)S(1)}, u32[]{:S(2)}, u32[]{:S(2)}) %collective-permute-start.15) | collective-permute-done | bytes 147488 | tf_op jit(solution)/shard_map/ppermute | solution.py:53
  210.1 7.3 %all-to-all-start.6 = ((bf16[32,64,128]{2,1,0:T(8,128)(2,1)}), bf16[32,64,128]{2,1,0:T(8,128)(2,1)S(1)}, u32[]{:S(2)}, u32[]{:S(2)}) async-start(bf16[32,64,128]{2,1,0:T(8,128)(2,1)} %bitcast.78), calls=%async_computation.7 | async-start | bytes 1048576 | tf_op jit(solution)/shard_map/all_to_all | solution.py:579
  217.6 11.4 %all-to-all-done.6 = bf16[32,64,128]{2,1,0:T(8,128)(2,1)S(1)} async-done(((bf16[32,64,128]{2,1,0:T(8,128)(2,1)}), bf16[32,64,128]{2,1,0:T(8,128)(2,1)S(1)}, u32[]{:S(2)}, u32[]{:S(2)}) %all-to-all-start.6) | async-done | bytes 524320 | tf_op jit(solution)/shard_map/all_to_all | solution.py:579
  235.7 3.4 %shard_map.262 = (bf16[2,512,128]{2,1,0:T(8,128)(2,1)}, bf16[2,512,128]{2,1,0:T(8,128)(2,1)}) custom-call(s32[2,512]{1,0:T(2,128)} %route_ref.3, bf16[2,16,64,128]{3,2,1,0:T(8,128)(2,1)} %bitcast.75), custom_call_target="tpu_custom_call" | custom-call | flops 4194304 | bytes 32768 | tf_op jit(solution)/shard_map/pallas_call | solution.py:74
  (133 shorter events, 50.9 us)
Async XLA Ops:
  7.2 54.8 %all-gather.5.cloned.1.call-start = ((), (), s32[]{:S(2)}) async-start(), calls=%async_computation.9 | async-start | bytes 3244032 | tf_op jit(solution)/shard_map/all_gather | solution.py:562
  8.7 101.2 %all-gather.7.cloned.1.call-start = ((), (), s32[]{:S(2)}) async-start(), calls=%async_computation.10 | async-start | bytes 4866048 | tf_op jit(solution)/shard_map/all_gather | solution.py:562
  14.1 21.7 %all-to-all-start = ((bf16[32,72,128]{2,1,0:T(8,128)(2,1)}), bf16[32,72,128]{2,1,0:T(8,128)(2,1)S(1)}, u32[]{:S(2)}, u32[]{:S(2)}) async-start(bf16[32,72,128]{2,1,0:T(8,128)(2,1)} %bitcast.71), calls=%async_computation | async-start | bytes 1179648 | tf_op jit(solution)/shard_map/all_to_all | solution.py:579
  37.0 18.9 %all-to-all-start.1 = ((bf16[4,2,512,128]{3,2,1,0:T(8,128)(2,1)}), bf16[4,2,512,128]{3,2,1,0:T(8,128)(2,1)S(1)}, u32[]{:S(2)}, u32[]{:S(2)}) async-start(bf16[4,2,512,128]{3,2,1,0:T(8,128)(2,1)} %broadcast_in_dim.51), calls=%async_computation.1 | async-start | bytes 2097152 | tf_op jit(solution)/shard_map/all_to_all | solution.py:579
  55.9 16.0 %collective-permute-start = (bf16[2,512,128]{2,1,0:T(8,128)(2,1)S(1)}, bf16[2,512,128]{2,1,0:T(8,128)(2,1)S(1)}, u32[]{:S(2)}, u32[]{:S(2)}) collective-permute-start(bf16[2,512,128]{2,1,0:T(8,128)(2,1)S(1)} %bitcast.60), channel_id=1, source_target_pairs={{0,1},{1,2},{2,3},{3,0},{8,9},{9,10},{10,11},{11,8},{4,5},{5,6},{6... | collective-permute-start | bytes 786440 | tf_op jit(solution)/shard_map/ppermute | solution.py:53
  55.9 16.0 %collective-permute-start.1 = (bf16[2,512,128]{2,1,0:T(8,128)(2,1)S(1)}, bf16[2,512,128]{2,1,0:T(8,128)(2,1)S(1)}, u32[]{:S(2)}, u32[]{:S(2)}) collective-permute-start(bf16[2,512,128]{2,1,0:T(8,128)(2,1)S(1)} %bitcast.61), channel_id=1, source_target_pairs={{0,2},{1,3},{2,0},{3,1},{8,10},{9,11},{10,8},{11,9},{4,6},{5,7},{6... | collective-permute-start | bytes 786440 | tf_op jit(solution)/shard_map/ppermute | solution.py:53
  59.5 12.5 %collective-permute-start.2 = (bf16[2,512,128]{2,1,0:T(8,128)(2,1)S(1)}, bf16[2,512,128]{2,1,0:T(8,128)(2,1)S(1)}, u32[]{:S(2)}, u32[]{:S(2)}) collective-permute-start(bf16[2,512,128]{2,1,0:T(8,128)(2,1)S(1)} %bitcast.62), channel_id=1, source_target_pairs={{0,3},{1,0},{2,1},{3,2},{8,11},{9,8},{10,9},{11,10},{4,7},{5,4},{6... | collective-permute-start | bytes 786440 | tf_op jit(solution)/shard_map/ppermute | solution.py:53
  91.4 17.5 %all-to-all-start.3 = ((bf16[4,2,512,128]{3,2,1,0:T(8,128)(2,1)}), bf16[4,2,512,128]{3,2,1,0:T(8,128)(2,1)S(1)}, u32[]{:S(2)}, u32[]{:S(2)}) async-start(bf16[4,2,512,128]{3,2,1,0:T(8,128)(2,1)} %shard_map.257), calls=%async_computation.3 | async-start | bytes 2097152 | tf_op jit(solution)/shard_map/all_to_all | solution.py:579
  122.7 18.8 %all-to-all-start.4 = ((bf16[4,2,512,128]{3,2,1,0:T(8,128)(2,1)}), bf16[4,2,512,128]{3,2,1,0:T(8,128)(2,1)S(1)}, u32[]{:S(2)}, u32[]{:S(2)}) async-start(bf16[4,2,512,128]{3,2,1,0:T(8,128)(2,1)} %get-tuple-element.87), calls=%async_computation.4 | async-start | bytes 2097152 | tf_op jit(solution)/shard_map/all_to_all | solution.py:579
  142.7 19.5 %all-to-all-start.5 = ((bf16[4,2,512,128]{3,2,1,0:T(8,128)(2,1)}), bf16[4,2,512,128]{3,2,1,0:T(8,128)(2,1)S(1)}, u32[]{:S(2)}, u32[]{:S(2)}) async-start(bf16[4,2,512,128]{3,2,1,0:T(8,128)(2,1)} %shard_map.260), calls=%async_computation.5 | async-start | bytes 2097152 | tf_op jit(solution)/shard_map/all_to_all | solution.py:579
  147.7 62.5 %reduce-scatter.2.cloned.1.call-start = ((), (), s32[]{:S(2)}) async-start(), calls=%async_computation.8 | async-start | bytes 2621440 | tf_op jit(solution)/shard_map/reduce_scatter | solution.py:756
  151.4 28.0 %collective-permute-start.4 = (bf16[4,64,1152]{2,1,0:T(8,128)(2,1)}, bf16[4,64,1152]{2,1,0:T(8,128)(2,1)}, u32[]{:S(2)}, u32[]{:S(2)}) collective-permute-start(bf16[4,64,1152]{2,1,0:T(8,128)(2,1)} %get-tuple-element.144), channel_id=1, source_target_pairs={{0,32},{1,33},{2,34},{3,35},{8,40},{9,41},{10,42},{11,43},{4,36},{... | collective-permute-start | bytes 1769480 | tf_op jit(solution)/shard_map/ppermute | solution.py:53
  152.6 29.1 %collective-permute-start.5 = (bf16[4,64,1152]{2,1,0:T(8,128)(2,1)S(1)}, bf16[4,64,1152]{2,1,0:T(8,128)(2,1)}, u32[]{:S(2)}, u32[]{:S(2)}) collective-permute-start(bf16[4,64,1152]{2,1,0:T(8,128)(2,1)S(1)} %get-tuple-element.143), channel_id=1, source_target_pairs={{0,64},{1,65},{2,66},{3,67},{8,72},{9,73},{10,74},{11,75},{4,68},{... | collective-permute-start | bytes 1769480 | tf_op jit(solution)/shard_map/ppermute | solution.py:53
  155.3 26.4 %collective-permute-start.6 = (bf16[4,64,1152]{2,1,0:T(8,128)(2,1)S(1)}, bf16[4,64,1152]{2,1,0:T(8,128)(2,1)}, u32[]{:S(2)}, u32[]{:S(2)}) collective-permute-start(bf16[4,64,1152]{2,1,0:T(8,128)(2,1)S(1)} %get-tuple-element.142), channel_id=1, source_target_pairs={{0,96},{1,97},{2,98},{3,99},{8,104},{9,105},{10,106},{11,107},{4,1... | collective-permute-start | bytes 1769480 | tf_op jit(solution)/shard_map/ppermute | solution.py:53
  181.7 8.8 %collective-permute-start.7 = (bf16[16,64,768]{2,1,0:T(8,128)(2,1)}, bf16[16,64,768]{2,1,0:T(8,128)(2,1)}, u32[]{:S(2)}, u32[]{:S(2)}) collective-permute-start(bf16[16,64,768]{2,1,0:T(8,128)(2,1)} %get-tuple-element.114), channel_id=1, source_target_pairs={{0,8},{1,9},{2,10},{3,11},{8,0},{9,1},{10,2},{11,3},{4,12},{5,13},... | collective-permute-start | bytes 4718600 | tf_op jit(solution)/shard_map/ppermute | solution.py:53
  193.5 24.0 %collective-permute-start.12 = (bf16[4,72,768]{2,1,0:T(8,128)(2,1)}, bf16[4,72,768]{2,1,0:T(8,128)(2,1)}, u32[]{:S(2)}, u32[]{:S(2)}) collective-permute-start(bf16[4,72,768]{2,1,0:T(8,128)(2,1)} %get-tuple-element.119), channel_id=1, source_target_pairs={{0,32},{1,33},{2,34},{3,35},{8,40},{9,41},{10,42},{11,43},{4,36},{... | collective-permute-start | bytes 1327112 | tf_op jit(solution)/shard_map/ppermute | solution.py:53
  194.6 22.9 %collective-permute-start.13 = (bf16[4,72,768]{2,1,0:T(8,128)(2,1)}, bf16[4,72,768]{2,1,0:T(8,128)(2,1)}, u32[]{:S(2)}, u32[]{:S(2)}) collective-permute-start(bf16[4,72,768]{2,1,0:T(8,128)(2,1)} %get-tuple-element.120), channel_id=1, source_target_pairs={{0,64},{1,65},{2,66},{3,67},{8,72},{9,73},{10,74},{11,75},{4,68},{... | collective-permute-start | bytes 1327112 | tf_op jit(solution)/shard_map/ppermute | solution.py:53
  197.5 20.0 %collective-permute-start.14 = (bf16[4,72,768]{2,1,0:T(8,128)(2,1)}, bf16[4,72,768]{2,1,0:T(8,128)(2,1)}, u32[]{:S(2)}, u32[]{:S(2)}) collective-permute-start(bf16[4,72,768]{2,1,0:T(8,128)(2,1)} %get-tuple-element.121), channel_id=1, source_target_pairs={{0,96},{1,97},{2,98},{3,99},{8,104},{9,105},{10,106},{11,107},{4,1... | collective-permute-start | bytes 1327112 | tf_op jit(solution)/shard_map/ppermute | solution.py:53
  199.5 7.3 %collective-permute-start.15 = (bf16[64,1152]{1,0:T(8,128)(2,1)S(1)}, bf16[64,1152]{1,0:T(8,128)(2,1)S(1)}, u32[]{:S(2)}, u32[]{:S(2)}) collective-permute-start(bf16[64,1152]{1,0:T(8,128)(2,1)S(1)} %get-tuple-element.151), channel_id=1, source_target_pairs={{0,4},{1,5},{2,6},{3,7},{8,12},{9,13},{10,14},{11,15},{4,16},{5,17... | collective-permute-start | bytes 442376 | tf_op jit(solution)/shard_map/ppermute | solution.py:53
  200.7 16.7 %collective-permute-start.16 = (bf16[64,1152]{1,0:T(8,128)(2,1)S(1)}, bf16[64,1152]{1,0:T(8,128)(2,1)S(1)}, u32[]{:S(2)}, u32[]{:S(2)}) collective-permute-start(bf16[64,1152]{1,0:T(8,128)(2,1)S(1)} %get-tuple-element.150), channel_id=1, source_target_pairs={{0,16},{1,17},{2,18},{3,19},{8,24},{9,25},{10,26},{11,27},{4,20},{... | collective-permute-start | bytes 442376 | tf_op jit(solution)/shard_map/ppermute | solution.py:53
  206.8 10.7 %collective-permute-start.17 = (bf16[64,1152]{1,0:T(8,128)(2,1)S(1)}, bf16[64,1152]{1,0:T(8,128)(2,1)S(1)}, u32[]{:S(2)}, u32[]{:S(2)}) collective-permute-start(bf16[64,1152]{1,0:T(8,128)(2,1)S(1)} %get-tuple-element.149), channel_id=1, source_target_pairs={{0,20},{1,21},{2,22},{3,23},{8,28},{9,29},{10,30},{11,31},{4,0},{5... | collective-permute-start | bytes 442376 | tf_op jit(solution)/shard_map/ppermute | solution.py:53
  210.1 18.9 %all-to-all-start.6 = ((bf16[32,64,128]{2,1,0:T(8,128)(2,1)}), bf16[32,64,128]{2,1,0:T(8,128)(2,1)S(1)}, u32[]{:S(2)}, u32[]{:S(2)}) async-start(bf16[32,64,128]{2,1,0:T(8,128)(2,1)} %bitcast.78), calls=%async_computation.7 | async-start | bytes 1048576 | tf_op jit(solution)/shard_map/all_to_all | solution.py:579
  230.8 8.8 %collective-permute-start.18 = (bf16[72,768]{1,0:T(8,128)(2,1)S(1)}, bf16[72,768]{1,0:T(8,128)(2,1)S(1)}, u32[]{:S(2)}, u32[]{:S(2)}) collective-permute-start(bf16[72,768]{1,0:T(8,128)(2,1)S(1)} %get-tuple-element.152), channel_id=1, source_target_pairs={{0,4},{1,5},{2,6},{3,7},{8,12},{9,13},{10,14},{11,15},{4,16},{5,17... | collective-permute-start | bytes 331784 | tf_op jit(solution)/shard_map/ppermute | solution.py:53
  231.4 8.1 %collective-permute-start.19 = (bf16[72,768]{1,0:T(8,128)(2,1)S(1)}, bf16[72,768]{1,0:T(8,128)(2,1)S(1)}, u32[]{:S(2)}, u32[]{:S(2)}) collective-permute-start(bf16[72,768]{1,0:T(8,128)(2,1)S(1)} %get-tuple-element.154), channel_id=1, source_target_pairs={{0,16},{1,17},{2,18},{3,19},{8,24},{9,25},{10,26},{11,27},{4,20},{... | collective-permute-start | bytes 331784 | tf_op jit(solution)/shard_map/ppermute | solution.py:53
  (23 other events, 226.8 us)
Sparse Core Ops, SparseCore 0:
  10.9 50.4 all-gather.4
  63.6 46.2 all-gather.6
  181.8 28.2 reduce-scatter.1

commit v3 on v2

--- a/solution.py
+++ b/solution.py
@@ -312,12 +312,22 @@
     rest = pl.ds(768, 384)
     loads = features_in_order(mover, h_hbm, full_ref)
     loads.append(mover.start(gain_hbm, gain_ref))
-    loads.append(mover.start(w_hbm.at[:, :, :, :, cut], w_ref.at[:, :, :, :, cut]))
-    later = features_of(mover, (g0, g1, g2, g3), where_ref[0], dy_ref)
+    later = [mover.start(w_hbm.at[:, :, :, :, cut], w_ref.at[:, :, :, :, cut])]
+    later += features_of(mover, (g0, g1, g2, g3), where_ref[0], dy_ref)
     later.append(mover.start(w_hbm.at[:, :, :, :, rest], w_ref.at[:, :, :, :, rest]))
     sum_ref[...] = jnp.zeros_like(sum_ref)
-    wait(loads + later)
-    stores = [mover.start(dy_ref, dy_hbm)]
+    wait(loads)
+
+    def norm(i, carry):
+        rows = tile(i)
+        value = full_ref[rows, :].astype(F32)
+        inv = lax.rsqrt(jnp.mean(value * value, axis=-1, keepdims=True) + EPSILON)
+        n_ref[rows, :] = (value * inv * gain_ref[1:2, :]).astype(BF)
+        return carry
+
+    lax.fori_loop(0, TOK // TILE, norm, 0)
+    wait(later)
+    stores = [mover.start(dy_ref, dy_hbm), mover.start(n_ref, n_hbm)]
 
     def step(i, carry):
         rows = tile(i)
@@ -325,8 +335,7 @@
         value = full_ref[rows, :].astype(F32)
         inv = lax.rsqrt(jnp.mean(value * value, axis=-1, keepdims=True) + EPSILON)
         hat = value * inv
-        normed = (hat * gain).astype(BF)
-        n_ref[rows, :] = normed
+        normed = n_ref[rows, :]
         delta = dy_ref[rows, :]
         for y in range(2):
             gate = nn(normed, weight(w_ref, y, slice(0, 384)))
@@ -348,7 +357,6 @@
                 part_ref[...] = inv * (scaled - hat * inner)
         split_features(part_ref, rows, send_ref)
         pltpu.make_async_copy(send_ref.at[:, :, rows], send_hbm.at[:, :, rows], sems.at[SENT + i]).start()
-        pltpu.make_async_copy(n_ref.at[rows], n_hbm.at[rows], sems.at[SENT + 2 + i]).start()
         pltpu.make_async_copy(hid_ref.at[:, rows], hid_hbm.at[:, rows], sems.at[SENT + 4 + i]).start()
         pltpu.make_async_copy(dgu_ref.at[:, rows], dgu_hbm.at[:, rows], sems.at[SENT + 6 + i]).start()
         return carry
@@ -356,7 +364,6 @@
     lax.fori_loop(0, TOK // TILE, step, 0)
     for i in range(TOK // TILE):
         rows = pl.ds(i * TILE, TILE)
-        stores.append(pltpu.make_async_copy(n_ref.at[rows], n_hbm.at[rows], sems.at[SENT + 2 + i]))
         stores.append(pltpu.make_async_copy(hid_ref.at[:, rows], hid_hbm.at[:, rows], sems.at[SENT + 4 + i]))
         stores.append(pltpu.make_async_copy(dgu_ref.at[:, rows], dgu_hbm.at[:, rows], sems.at[SENT + 6 + i]))
     wait(stores + sent_tiles(send_ref, send_hbm, sems))
@@ -443,12 +450,6 @@
         mover.start(gain_hbm, gain_ref),
         mover.start(mlp_sum_hbm, mlp_sum_ref),
     ]
-    more = [
-        mover.start(w_hbm.at[:, :, :, :, pl.ds(0, 512)], w_ref.at[:, :, :, :, pl.ds(0, 512)]),
-        mover.start(full_hbm, full_ref),
-    ]
-    much = [mover.start(n_hbm, n_ref), mover.start(a_hbm, a_ref)]
-    last = mover.start(out_hbm, back_ref.at[:, :, :, 1])
     head_ref[...] = jnp.zeros_like(head_ref)
     sum_ref[...] = jnp.zeros_like(sum_ref)
     dk_ref[...] = jnp.zeros_like(dk_ref)
@@ -456,6 +457,12 @@
     loads[0].wait()
     bias_of(table_ref, bias_ref)
     wait(loads[1:])
+    more = [
+        mover.start(w_hbm.at[:, :, :, :, pl.ds(0, 512)], w_ref.at[:, :, :, :, pl.ds(0, 512)]),
+        mover.start(full_hbm, full_ref),
+    ]
+    much = [mover.start(n_hbm, n_ref), mover.start(a_hbm, a_ref)]
+    last = mover.start(out_hbm, back_ref.at[:, :, :, 1])
     stores = []
 
     def back(rotated, proj, gain, rows, at):

time: 252 us -> 251 us (level)
  no operation moved by 1% of the time
where the time goes in v3:
time: 251 us; the launch traced here: 249 us
  waiting for transfers between devices  69.6 us (28%)
  starting transfers between devices  63.5 us (25%)
  Pallas kernels  56.3 us (22%)
  other arithmetic  18.2 us (7%)
  blocking collectives  18.2 us (7%)
  between operations  16.3 us (6%)
  local copies, waits for them, and re-layouts  6.55 us (3%)
    all_to_all x6, waiting for transfers between devices, exchange(): lax.all_to_all(blocks, BOTH, 0, 0, axis_index_groups=groups, tiled=True)  57 us
    pallas_call x8, Pallas kernels, call(): pl.pallas_call(body, out_shape=[jax.ShapeDtypeStruct(s, t) for _, s, t in...  56.3 us
    all_to_all x6, starting transfers between devices, exchange(): lax.all_to_all(blocks, BOTH, 0, 0, axis_index_groups=groups, tiled=True)  35.3 us
    ppermute x21, starting transfers between devices, shift(): return lax.ppermute(value, BOTH, moves(**step))  28.1 us
    all_to_all x1, blocking collectives, exchange(): lax.all_to_all(blocks, BOTH, 0, 0, axis_index_groups=groups, tiled=True)  18.2 us
    ppermute x21, waiting for transfers between devices, shift(): return lax.ppermute(value, BOTH, moves(**step))  10.1 us
    add x2, other arithmetic, block(): take(keep, where[1] + k).astype(F32) + take(other, where[1] + k).astype(F32)  5.57 us
  transfers between devices with their start and end apart: 30, of which 15 were waited for; matrix products, arithmetic and copies ran while one was open for 7% of the time, Pallas kernels for 18%

profile of v3, /device:TPU:2, one launch (start us, length us, event | category | flops | bytes accessed | tf_op | source)
XLA Modules:
  0.0 248.7 jit_solution(15676854624795002753)
XLA Ops:
  10.4 3.7 %shard_map.255 = bf16[2,16,72,128]{3,2,1,0:T(8,128)(2,1)} custom-call(s32[2,512]{1,0:T(2,128)} %route_ref.3, bf16[2,512,128]{2,1,0:T(8,128)(2,1)} %x_hbm.1, bf16[2,512,128]{2,1,0:T(8,128)(2,1)} %g_hbm.1), custom_call_target="tpu_custom_call" | custom-call | flops 4194304 | bytes 65536 | tf_op jit(solution)/shard_map/pallas_call | solution.py:74
  14.1 8.3 %all-to-all-start = ((bf16[32,72,128]{2,1,0:T(8,128)(2,1)}), bf16[32,72,128]{2,1,0:T(8,128)(2,1)S(1)}, u32[]{:S(2)}, u32[]{:S(2)}) async-start(bf16[32,72,128]{2,1,0:T(8,128)(2,1)} %bitcast.71), calls=%async_computation | async-start | bytes 1179648 | tf_op jit(solution)/shard_map/all_to_all | solution.py:586
  25.9 9.9 %all-to-all-done = bf16[32,72,128]{2,1,0:T(8,128)(2,1)S(1)} async-done(((bf16[32,72,128]{2,1,0:T(8,128)(2,1)}), bf16[32,72,128]{2,1,0:T(8,128)(2,1)S(1)}, u32[]{:S(2)}, u32[]{:S(2)}) %all-to-all-start) | async-done | bytes 589856 | tf_op jit(solution)/shard_map/all_to_all | solution.py:586
  37.0 4.8 %all-to-all-start.1 = ((bf16[4,2,512,128]{3,2,1,0:T(8,128)(2,1)}), bf16[4,2,512,128]{3,2,1,0:T(8,128)(2,1)S(1)}, u32[]{:S(2)}, u32[]{:S(2)}) async-start(bf16[4,2,512,128]{3,2,1,0:T(8,128)(2,1)} %broadcast_in_dim.51), calls=%async_computation.1 | async-start | bytes 2097152 | tf_op jit(solution)/shard_map/all_to_all | solution.py:586
  43.9 12.0 %all-to-all-done.1.x_hbm = bf16[4,2,512,128]{3,2,1,0:T(8,128)(2,1)S(1)} async-done(((bf16[4,2,512,128]{3,2,1,0:T(8,128)(2,1)}), bf16[4,2,512,128]{3,2,1,0:T(8,128)(2,1)S(1)}, u32[]{:S(2)}, u32[]{:S(2)}) %all-to-all-start.1) | async-done | bytes 1048608 | tf_op jit(solution)/shard_map/all_to_all | solution.py:586
  55.9 3.5 %collective-permute-start.1 = (bf16[2,512,128]{2,1,0:T(8,128)(2,1)S(1)}, bf16[2,512,128]{2,1,0:T(8,128)(2,1)S(1)}, u32[]{:S(2)}, u32[]{:S(2)}) collective-permute-start(bf16[2,512,128]{2,1,0:T(8,128)(2,1)S(1)} %bitcast.61), channel_id=1, source_target_pairs={{0,2},{1,3},{2,0},{3,1},{8,10},{9,11},{10,8},{11,9},{4,6},{5,7},{6... | collective-permute-start | bytes 786440 | tf_op jit(solution)/shard_map/ppermute | solution.py:53
  62.0 9.9 %shard_map.256 = (bf16[4,2,512,128]{3,2,1,0:T(8,128)(2,1)}, bf16[512,1024]{1,0:T(8,128)(2,1)}, bf16[512,1024]{1,0:T(8,128)(2,1)}, f32[2,512,384]{2,1,0:T(8,128)}...) custom-call(bf16[4,2,512,128]{3,2,1,0:T(8,128)(2,1)} %copy-done.5, ...), custom_call_target="tpu_custom_call" | custom-call | flops 50331648 | bytes 262144 | tf_op jit(solution)/shard_map/pallas_call | solution.py:74
  72.0 18.2 %all_to_all.35.got_ref = bf16[4,2,512,128]{3,2,1,0:T(8,128)(2,1)S(1)} all-to-all(bf16[4,2,512,128]{3,2,1,0:T(8,128)(2,1)} %get-tuple-element.82), channel_id=1, replica_groups={{0,1,2,3},{4,5,6,7},{8,9,10,11},{12,13,14,15},{16,17,18,19},{20,21,22,2..., dimensions={0} | all-to-all | bytes 2097152 | tf_op jit(solution)/shard_map/all_to_all | solution.py:586
  91.4 5.0 %all-to-all-start.3 = ((bf16[4,2,512,128]{3,2,1,0:T(8,128)(2,1)}), bf16[4,2,512,128]{3,2,1,0:T(8,128)(2,1)S(1)}, u32[]{:S(2)}, u32[]{:S(2)}) async-start(bf16[4,2,512,128]{3,2,1,0:T(8,128)(2,1)} %shard_map.257), calls=%async_computation.3 | async-start | bytes 2097152 | tf_op jit(solution)/shard_map/all_to_all | solution.py:586
  97.0 12.0 %all-to-all-done.3.h_hbm = bf16[4,2,512,128]{3,2,1,0:T(8,128)(2,1)S(1)} async-done(((bf16[4,2,512,128]{3,2,1,0:T(8,128)(2,1)}), bf16[4,2,512,128]{3,2,1,0:T(8,128)(2,1)S(1)}, u32[]{:S(2)}, u32[]{:S(2)}) %all-to-all-start.3) | async-done | bytes 1048608 | tf_op jit(solution)/shard_map/all_to_all | solution.py:586
  109.9 12.3 %shard_map.258 = (bf16[4,2,512,128]{3,2,1,0:T(8,128)(2,1)}, bf16[512,1024]{1,0:T(8,128)(2,1)}, bf16[512,1024]{1,0:T(8,128)(2,1)}, bf16[2,512,384]{2,1,0:T(8,128)...) custom-call(s32[4]{0:T(128)} %pad_add_fusion.where_ref, bf16[4,2,512,128]{3,2,1,0:T(8,128)(2,1)} %copy-done.3, ...), custom_call_target="tpu_custom_call" | custom-call | flops 83886080 | bytes 262144 | tf_op jit(solution)/shard_map/pallas_call | solution.py:74
  122.3 5.0 %all-to-all-start.4 = ((bf16[4,2,512,128]{3,2,1,0:T(8,128)(2,1)}), bf16[4,2,512,128]{3,2,1,0:T(8,128)(2,1)S(1)}, u32[]{:S(2)}, u32[]{:S(2)}) async-start(bf16[4,2,512,128]{3,2,1,0:T(8,128)(2,1)} %get-tuple-element.87), calls=%async_computation.4 | async-start | bytes 2097152 | tf_op jit(solution)/shard_map/all_to_all | solution.py:586
  127.3 8.5 %shard_map.259 = (bf16[4,2,512,128]{3,2,1,0:T(8,128)(2,1)}, bf16[16,64,1152]{2,1,0:T(8,128)(2,1)}, bf16[16,64,1152]{2,1,0:T(8,128)(2,1)}) custom-call(s32[4]{0:T(128)} %pad_add_fusion.where_ref, bf16[2,512,384]{2,1,0:T(8,128)(2,1)} %get-tuple-element.88.hid_hbm, bf16[2,512,768]{2,1,0:T(8,128)(2,1)} %get-tuple-element.89.dgu_hbm, ...), custom_call_target="tpu_custom_call" | custom-call | flops 67108864 | bytes 262144 | tf_op jit(solution)/shard_map/pallas_call | solution.py:74
  135.7 5.4 %all-to-all-done.4.got_ref = bf16[4,2,512,128]{3,2,1,0:T(8,128)(2,1)S(1)} async-done(((bf16[4,2,512,128]{3,2,1,0:T(8,128)(2,1)}), bf16[4,2,512,128]{3,2,1,0:T(8,128)(2,1)S(1)}, u32[]{:S(2)}, u32[]{:S(2)}) %all-to-all-start.4) | async-done | bytes 1048608 | tf_op jit(solution)/shard_map/all_to_all | solution.py:586
  142.3 5.0 %all-to-all-start.5 = ((bf16[4,2,512,128]{3,2,1,0:T(8,128)(2,1)}), bf16[4,2,512,128]{3,2,1,0:T(8,128)(2,1)S(1)}, u32[]{:S(2)}, u32[]{:S(2)}) async-start(bf16[4,2,512,128]{3,2,1,0:T(8,128)(2,1)} %shard_map.260), calls=%async_computation.5 | async-start | bytes 2097152 | tf_op jit(solution)/shard_map/all_to_all | solution.py:586
  147.2 3.8 %add_bitcast_fusion = (f32[4,64,1152]{2,1,0:T(8,128)S(1)}, bf16[4,64,1152]{2,1,0:T(8,128)(2,1)S(1)}, bf16[4,64,1152]{2,1,0:T(8,128)(2,1)S(1)}, bf16[4,64,1152]{2,1,0:T(8,128)(2,1)}) fusion(bf16[4,4,64,1152]{3,2,1,0:T(8,128)(2,1)} %bitcast.18, s32[]{:T(128)S(6)} %select_n.199, bf16[4,4,64,1152]{3,2,1,0:T(8,128)(2,1)} %bitcast.72, s32[]{:T(128)S(6)} %select_n.197, ...), kind=kLoop, calls=%fused_computation.1 | loop fusion | flops 4423680 | bytes 7667728 | tf_op jit(solution)/shard_map/add | solution.py:607
  155.4 6.4 %all-to-all-done.5.d_hbm = bf16[4,2,512,128]{3,2,1,0:T(8,128)(2,1)S(1)} async-done(((bf16[4,2,512,128]{3,2,1,0:T(8,128)(2,1)}), bf16[4,2,512,128]{3,2,1,0:T(8,128)(2,1)S(1)}, u32[]{:S(2)}, u32[]{:S(2)}) %all-to-all-start.5) | async-done | bytes 1048608 | tf_op jit(solution)/shard_map/all_to_all | solution.py:586
  162.8 16.2 %shard_map.261 = (bf16[4,2,16,2,32,128]{5,4,3,2,1,0:T(8,128)(2,1)}, bf16[16,64,768]{2,1,0:T(8,128)(2,1)}, bf16[16,64,768]{2,1,0:T(8,128)(2,1)}, f32[8,768]{1,0:T(8,128)}) custom-call(s32[4]{0:T(128)} %pad_add_fusion.where_ref, bf16[4,2,512,128]{3,2,1,0:T(8,128)(2,1)} %copy-done.4, bf16[8,2,2,64,768]{4,3,2,1,0:T(8,128)(2,1)} %bitcast.70, ...), custom_call_target="tpu_custom_call" | custom-call | flops 117440512 | bytes 524288 | tf_op jit(solution)/shard_map/pallas_call | solution.py:74
  183.5 3.3 %collective-permute-start.9 = (f32[8,768]{1,0:T(8,128)S(1)}, f32[8,768]{1,0:T(8,128)S(1)}, u32[]{:S(2)}, u32[]{:S(2)}) collective-permute-start(f32[8,768]{1,0:T(8,128)S(1)} %copy-done.11), channel_id=1, source_target_pairs={{0,2},{1,3},{2,0},{3,1},{8,10},{9,11},{10,8},{11,9},{4,6},{5,7},{6... | collective-permute-start | bytes 73736 | tf_op jit(solution)/shard_map/ppermute | solution.py:53
  194.2 2.9 %collective-permute-start.13 = (bf16[4,72,768]{2,1,0:T(8,128)(2,1)}, bf16[4,72,768]{2,1,0:T(8,128)(2,1)}, u32[]{:S(2)}, u32[]{:S(2)}) collective-permute-start(bf16[4,72,768]{2,1,0:T(8,128)(2,1)} %get-tuple-element.120), channel_id=1, source_target_pairs={{0,64},{1,65},{2,66},{3,67},{8,72},{9,73},{10,74},{11,75},{4,68},{... | collective-permute-start | bytes 1327112 | tf_op jit(solution)/shard_map/ppermute | solution.py:53
  202.9 3.4 %collective-permute-done.15 = bf16[64,1152]{1,0:T(8,128)(2,1)S(1)} collective-permute-done((bf16[64,1152]{1,0:T(8,128)(2,1)S(1)}, bf16[64,1152]{1,0:T(8,128)(2,1)S(1)}, u32[]{:S(2)}, u32[]{:S(2)}) %collective-permute-start.15) | collective-permute-done | bytes 147488 | tf_op jit(solution)/shard_map/ppermute | solution.py:53
  209.7 7.3 %all-to-all-start.6 = ((bf16[32,64,128]{2,1,0:T(8,128)(2,1)}), bf16[32,64,128]{2,1,0:T(8,128)(2,1)S(1)}, u32[]{:S(2)}, u32[]{:S(2)}) async-start(bf16[32,64,128]{2,1,0:T(8,128)(2,1)} %bitcast.78), calls=%async_computation.7 | async-start | bytes 1048576 | tf_op jit(solution)/shard_map/all_to_all | solution.py:586
  217.2 11.4 %all-to-all-done.6 = bf16[32,64,128]{2,1,0:T(8,128)(2,1)S(1)} async-done(((bf16[32,64,128]{2,1,0:T(8,128)(2,1)}), bf16[32,64,128]{2,1,0:T(8,128)(2,1)S(1)}, u32[]{:S(2)}, u32[]{:S(2)}) %all-to-all-start.6) | async-done | bytes 524320 | tf_op jit(solution)/shard_map/all_to_all | solution.py:586
  235.2 3.4 %shard_map.262 = (bf16[2,512,128]{2,1,0:T(8,128)(2,1)}, bf16[2,512,128]{2,1,0:T(8,128)(2,1)}) custom-call(s32[2,512]{1,0:T(2,128)} %route_ref.3, bf16[2,16,64,128]{3,2,1,0:T(8,128)(2,1)} %bitcast.75), custom_call_target="tpu_custom_call" | custom-call | flops 4194304 | bytes 32768 | tf_op jit(solution)/shard_map/pallas_call | solution.py:74
  (133 shorter events, 50.9 us)
Async XLA Ops:
  7.2 54.8 %all-gather.5.cloned.1.call-start = ((), (), s32[]{:S(2)}) async-start(), calls=%async_computation.9 | async-start | bytes 3244032 | tf_op jit(solution)/shard_map/all_gather | solution.py:569
  8.7 101.2 %all-gather.7.cloned.1.call-start = ((), (), s32[]{:S(2)}) async-start(), calls=%async_computation.10 | async-start | bytes 4866048 | tf_op jit(solution)/shard_map/all_gather | solution.py:569
  14.1 21.7 %all-to-all-start = ((bf16[32,72,128]{2,1,0:T(8,128)(2,1)}), bf16[32,72,128]{2,1,0:T(8,128)(2,1)S(1)}, u32[]{:S(2)}, u32[]{:S(2)}) async-start(bf16[32,72,128]{2,1,0:T(8,128)(2,1)} %bitcast.71), calls=%async_computation | async-start | bytes 1179648 | tf_op jit(solution)/shard_map/all_to_all | solution.py:586
  37.0 18.9 %all-to-all-start.1 = ((bf16[4,2,512,128]{3,2,1,0:T(8,128)(2,1)}), bf16[4,2,512,128]{3,2,1,0:T(8,128)(2,1)S(1)}, u32[]{:S(2)}, u32[]{:S(2)}) async-start(bf16[4,2,512,128]{3,2,1,0:T(8,128)(2,1)} %broadcast_in_dim.51), calls=%async_computation.1 | async-start | bytes 2097152 | tf_op jit(solution)/shard_map/all_to_all | solution.py:586
  55.9 16.0 %collective-permute-start = (bf16[2,512,128]{2,1,0:T(8,128)(2,1)S(1)}, bf16[2,512,128]{2,1,0:T(8,128)(2,1)S(1)}, u32[]{:S(2)}, u32[]{:S(2)}) collective-permute-start(bf16[2,512,128]{2,1,0:T(8,128)(2,1)S(1)} %bitcast.60), channel_id=1, source_target_pairs={{0,1},{1,2},{2,3},{3,0},{8,9},{9,10},{10,11},{11,8},{4,5},{5,6},{6... | collective-permute-start | bytes 786440 | tf_op jit(solution)/shard_map/ppermute | solution.py:53
  55.9 16.0 %collective-permute-start.1 = (bf16[2,512,128]{2,1,0:T(8,128)(2,1)S(1)}, bf16[2,512,128]{2,1,0:T(8,128)(2,1)S(1)}, u32[]{:S(2)}, u32[]{:S(2)}) collective-permute-start(bf16[2,512,128]{2,1,0:T(8,128)(2,1)S(1)} %bitcast.61), channel_id=1, source_target_pairs={{0,2},{1,3},{2,0},{3,1},{8,10},{9,11},{10,8},{11,9},{4,6},{5,7},{6... | collective-permute-start | bytes 786440 | tf_op jit(solution)/shard_map/ppermute | solution.py:53
  59.5 12.5 %collective-permute-start.2 = (bf16[2,512,128]{2,1,0:T(8,128)(2,1)S(1)}, bf16[2,512,128]{2,1,0:T(8,128)(2,1)S(1)}, u32[]{:S(2)}, u32[]{:S(2)}) collective-permute-start(bf16[2,512,128]{2,1,0:T(8,128)(2,1)S(1)} %bitcast.62), channel_id=1, source_target_pairs={{0,3},{1,0},{2,1},{3,2},{8,11},{9,8},{10,9},{11,10},{4,7},{5,4},{6... | collective-permute-start | bytes 786440 | tf_op jit(solution)/shard_map/ppermute | solution.py:53
  91.4 17.5 %all-to-all-start.3 = ((bf16[4,2,512,128]{3,2,1,0:T(8,128)(2,1)}), bf16[4,2,512,128]{3,2,1,0:T(8,128)(2,1)S(1)}, u32[]{:S(2)}, u32[]{:S(2)}) async-start(bf16[4,2,512,128]{3,2,1,0:T(8,128)(2,1)} %shard_map.257), calls=%async_computation.3 | async-start | bytes 2097152 | tf_op jit(solution)/shard_map/all_to_all | solution.py:586
  122.3 18.8 %all-to-all-start.4 = ((bf16[4,2,512,128]{3,2,1,0:T(8,128)(2,1)}), bf16[4,2,512,128]{3,2,1,0:T(8,128)(2,1)S(1)}, u32[]{:S(2)}, u32[]{:S(2)}) async-start(bf16[4,2,512,128]{3,2,1,0:T(8,128)(2,1)} %get-tuple-element.87), calls=%async_computation.4 | async-start | bytes 2097152 | tf_op jit(solution)/shard_map/all_to_all | solution.py:586
  142.3 19.5 %all-to-all-start.5 = ((bf16[4,2,512,128]{3,2,1,0:T(8,128)(2,1)}), bf16[4,2,512,128]{3,2,1,0:T(8,128)(2,1)S(1)}, u32[]{:S(2)}, u32[]{:S(2)}) async-start(bf16[4,2,512,128]{3,2,1,0:T(8,128)(2,1)} %shard_map.260), calls=%async_computation.5 | async-start | bytes 2097152 | tf_op jit(solution)/shard_map/all_to_all | solution.py:586
  147.2 62.5 %reduce-scatter.2.cloned.1.call-start = ((), (), s32[]{:S(2)}) async-start(), calls=%async_computation.8 | async-start | bytes 2621440 | tf_op jit(solution)/shard_map/reduce_scatter | solution.py:763
  151.0 28.0 %collective-permute-start.4 = (bf16[4,64,1152]{2,1,0:T(8,128)(2,1)}, bf16[4,64,1152]{2,1,0:T(8,128)(2,1)}, u32[]{:S(2)}, u32[]{:S(2)}) collective-permute-start(bf16[4,64,1152]{2,1,0:T(8,128)(2,1)} %get-tuple-element.144), channel_id=1, source_target_pairs={{0,32},{1,33},{2,34},{3,35},{8,40},{9,41},{10,42},{11,43},{4,36},{... | collective-permute-start | bytes 1769480 | tf_op jit(solution)/shard_map/ppermute | solution.py:53
  152.2 29.1 %collective-permute-start.5 = (bf16[4,64,1152]{2,1,0:T(8,128)(2,1)S(1)}, bf16[4,64,1152]{2,1,0:T(8,128)(2,1)}, u32[]{:S(2)}, u32[]{:S(2)}) collective-permute-start(bf16[4,64,1152]{2,1,0:T(8,128)(2,1)S(1)} %get-tuple-element.143), channel_id=1, source_target_pairs={{0,64},{1,65},{2,66},{3,67},{8,72},{9,73},{10,74},{11,75},{4,68},{... | collective-permute-start | bytes 1769480 | tf_op jit(solution)/shard_map/ppermute | solution.py:53
  154.9 26.4 %collective-permute-start.6 = (bf16[4,64,1152]{2,1,0:T(8,128)(2,1)S(1)}, bf16[4,64,1152]{2,1,0:T(8,128)(2,1)}, u32[]{:S(2)}, u32[]{:S(2)}) collective-permute-start(bf16[4,64,1152]{2,1,0:T(8,128)(2,1)S(1)} %get-tuple-element.142), channel_id=1, source_target_pairs={{0,96},{1,97},{2,98},{3,99},{8,104},{9,105},{10,106},{11,107},{4,1... | collective-permute-start | bytes 1769480 | tf_op jit(solution)/shard_map/ppermute | solution.py:53
  181.3 8.8 %collective-permute-start.7 = (bf16[16,64,768]{2,1,0:T(8,128)(2,1)}, bf16[16,64,768]{2,1,0:T(8,128)(2,1)}, u32[]{:S(2)}, u32[]{:S(2)}) collective-permute-start(bf16[16,64,768]{2,1,0:T(8,128)(2,1)} %get-tuple-element.114), channel_id=1, source_target_pairs={{0,8},{1,9},{2,10},{3,11},{8,0},{9,1},{10,2},{11,3},{4,12},{5,13},... | collective-permute-start | bytes 4718600 | tf_op jit(solution)/shard_map/ppermute | solution.py:53
  193.1 24.0 %collective-permute-start.12 = (bf16[4,72,768]{2,1,0:T(8,128)(2,1)}, bf16[4,72,768]{2,1,0:T(8,128)(2,1)}, u32[]{:S(2)}, u32[]{:S(2)}) collective-permute-start(bf16[4,72,768]{2,1,0:T(8,128)(2,1)} %get-tuple-element.119), channel_id=1, source_target_pairs={{0,32},{1,33},{2,34},{3,35},{8,40},{9,41},{10,42},{11,43},{4,36},{... | collective-permute-start | bytes 1327112 | tf_op jit(solution)/shard_map/ppermute | solution.py:53
  194.2 22.9 %collective-permute-start.13 = (bf16[4,72,768]{2,1,0:T(8,128)(2,1)}, bf16[4,72,768]{2,1,0:T(8,128)(2,1)}, u32[]{:S(2)}, u32[]{:S(2)}) collective-permute-start(bf16[4,72,768]{2,1,0:T(8,128)(2,1)} %get-tuple-element.120), channel_id=1, source_target_pairs={{0,64},{1,65},{2,66},{3,67},{8,72},{9,73},{10,74},{11,75},{4,68},{... | collective-permute-start | bytes 1327112 | tf_op jit(solution)/shard_map/ppermute | solution.py:53
  197.1 20.0 %collective-permute-start.14 = (bf16[4,72,768]{2,1,0:T(8,128)(2,1)}, bf16[4,72,768]{2,1,0:T(8,128)(2,1)}, u32[]{:S(2)}, u32[]{:S(2)}) collective-permute-start(bf16[4,72,768]{2,1,0:T(8,128)(2,1)} %get-tuple-element.121), channel_id=1, source_target_pairs={{0,96},{1,97},{2,98},{3,99},{8,104},{9,105},{10,106},{11,107},{4,1... | collective-permute-start | bytes 1327112 | tf_op jit(solution)/shard_map/ppermute | solution.py:53
  199.0 7.3 %collective-permute-start.15 = (bf16[64,1152]{1,0:T(8,128)(2,1)S(1)}, bf16[64,1152]{1,0:T(8,128)(2,1)S(1)}, u32[]{:S(2)}, u32[]{:S(2)}) collective-permute-start(bf16[64,1152]{1,0:T(8,128)(2,1)S(1)} %get-tuple-element.151), channel_id=1, source_target_pairs={{0,4},{1,5},{2,6},{3,7},{8,12},{9,13},{10,14},{11,15},{4,16},{5,17... | collective-permute-start | bytes 442376 | tf_op jit(solution)/shard_map/ppermute | solution.py:53
  200.3 16.7 %collective-permute-start.16 = (bf16[64,1152]{1,0:T(8,128)(2,1)S(1)}, bf16[64,1152]{1,0:T(8,128)(2,1)S(1)}, u32[]{:S(2)}, u32[]{:S(2)}) collective-permute-start(bf16[64,1152]{1,0:T(8,128)(2,1)S(1)} %get-tuple-element.150), channel_id=1, source_target_pairs={{0,16},{1,17},{2,18},{3,19},{8,24},{9,25},{10,26},{11,27},{4,20},{... | collective-permute-start | bytes 442376 | tf_op jit(solution)/shard_map/ppermute | solution.py:53
  206.4 10.7 %collective-permute-start.17 = (bf16[64,1152]{1,0:T(8,128)(2,1)S(1)}, bf16[64,1152]{1,0:T(8,128)(2,1)S(1)}, u32[]{:S(2)}, u32[]{:S(2)}) collective-permute-start(bf16[64,1152]{1,0:T(8,128)(2,1)S(1)} %get-tuple-element.149), channel_id=1, source_target_pairs={{0,20},{1,21},{2,22},{3,23},{8,28},{9,29},{10,30},{11,31},{4,0},{5... | collective-permute-start | bytes 442376 | tf_op jit(solution)/shard_map/ppermute | solution.py:53
  209.7 18.9 %all-to-all-start.6 = ((bf16[32,64,128]{2,1,0:T(8,128)(2,1)}), bf16[32,64,128]{2,1,0:T(8,128)(2,1)S(1)}, u32[]{:S(2)}, u32[]{:S(2)}) async-start(bf16[32,64,128]{2,1,0:T(8,128)(2,1)} %bitcast.78), calls=%async_computation.7 | async-start | bytes 1048576 | tf_op jit(solution)/shard_map/all_to_all | solution.py:586
  230.4 8.8 %collective-permute-start.18 = (bf16[72,768]{1,0:T(8,128)(2,1)S(1)}, bf16[72,768]{1,0:T(8,128)(2,1)S(1)}, u32[]{:S(2)}, u32[]{:S(2)}) collective-permute-start(bf16[72,768]{1,0:T(8,128)(2,1)S(1)} %get-tuple-element.152), channel_id=1, source_target_pairs={{0,4},{1,5},{2,6},{3,7},{8,12},{9,13},{10,14},{11,15},{4,16},{5,17... | collective-permute-start | bytes 331784 | tf_op jit(solution)/shard_map/ppermute | solution.py:53
  231.0 8.1 %collective-permute-start.19 = (bf16[72,768]{1,0:T(8,128)(2,1)S(1)}, bf16[72,768]{1,0:T(8,128)(2,1)S(1)}, u32[]{:S(2)}, u32[]{:S(2)}) collective-permute-start(bf16[72,768]{1,0:T(8,128)(2,1)S(1)} %get-tuple-element.154), channel_id=1, source_target_pairs={{0,16},{1,17},{2,18},{3,19},{8,24},{9,25},{10,26},{11,27},{4,20},{... | collective-permute-start | bytes 331784 | tf_op jit(solution)/shard_map/ppermute | solution.py:53
  (23 other events, 226.8 us)
Sparse Core Ops, SparseCore 0:
  10.9 50.4 all-gather.4
  63.6 46.2 all-gather.6
  181.4 28.2 reduce-scatter.1

commit v4 on v3

--- a/solution.py
+++ b/solution.py
@@ -662,8 +662,6 @@
     my_input = arrived[:, :, 0:32, :].reshape(FEATURES)
     inputs = exchange(repeat(my_input), SAME_X)
     my_grad = arrived[:, :, 32:64, :].reshape(FEATURES)
-    inputs, my_grad = fence((inputs, my_grad))
-    grads = spread(my_grad)
     codes = arrived[0, :, 64, 0:64].astype(F32)
     slots = (codes[:, 0:32] * 16 + codes[:, 32:64]).astype(jnp.int32).reshape(TOK)
 
@@ -687,7 +685,8 @@
     cosine = jnp.cos(angles)
     sine = jnp.sin(angles)
     rope = jnp.concatenate([cosine, cosine, -sine, sine], axis=-1)
-    inputs, table, rope = fence((inputs, table, rope))
+    inputs, my_grad, table, rope = fence((inputs, my_grad, table, rope))
+    grads = spread(my_grad)
 
     sent = [("h", WIDE, BF)]
     send, full, normed_one, proj, q_rows, k_rows, v_rows, attended, lse = call(

time: 251 us -> 251 us (level)
  transfers between devices with their start and end apart: 30 -> 30, of which waited for: 15 -> 16; matrix products, arithmetic and copies ran while one was open for 7% -> 7% of each run, Pallas kernels for 18% -> 18%
where the time goes in v4:
time: 251 us; the launch traced here: 249 us
  waiting for transfers between devices  68.6 us (27%)
  starting transfers between devices  63.5 us (25%)
  Pallas kernels  56.3 us (22%)
  blocking collectives  18.9 us (8%)
  other arithmetic  18.3 us (7%)
  between operations  16.3 us (6%)
  local copies, waits for them, and re-layouts  6.81 us (3%)
    pallas_call x8, Pallas kernels, call(): pl.pallas_call(body, out_shape=[jax.ShapeDtypeStruct(s, t) for _, s, t in...  56.3 us
    all_to_all x6, waiting for transfers between devices, exchange(): lax.all_to_all(blocks, BOTH, 0, 0, axis_index_groups=groups, tiled=True)  56.2 us
    all_to_all x6, starting transfers between devices, exchange(): lax.all_to_all(blocks, BOTH, 0, 0, axis_index_groups=groups, tiled=True)  35.3 us
    ppermute x21, starting transfers between devices, shift(): return lax.ppermute(value, BOTH, moves(**step))  28.1 us
    all_to_all x1, blocking collectives, exchange(): lax.all_to_all(blocks, BOTH, 0, 0, axis_index_groups=groups, tiled=True)  18.9 us
    ppermute x21, waiting for transfers between devices, shift(): return lax.ppermute(value, BOTH, moves(**step))  10 us
    add x2, other arithmetic, block(): take(keep, where[1] + k).astype(F32) + take(other, where[1] + k).astype(F32)  5.57 us
  transfers between devices with their start and end apart: 30, of which 16 were waited for; matrix products, arithmetic and copies ran while one was open for 7% of the time, Pallas kernels for 18%

profile of v4, /device:TPU:2, one launch (start us, length us, event | category | flops | bytes accessed | tf_op | source)
XLA Modules:
  0.0 248.7 jit_solution(9297584928959970349)
XLA Ops:
  10.3 3.7 %shard_map.255 = bf16[2,16,72,128]{3,2,1,0:T(8,128)(2,1)} custom-call(s32[2,512]{1,0:T(2,128)} %route_ref.3, bf16[2,512,128]{2,1,0:T(8,128)(2,1)} %x_hbm.1, bf16[2,512,128]{2,1,0:T(8,128)(2,1)} %g_hbm.1), custom_call_target="tpu_custom_call" | custom-call | flops 4194304 | bytes 65536 | tf_op jit(solution)/shard_map/pallas_call | solution.py:74
  14.0 8.3 %all-to-all-start = ((bf16[32,72,128]{2,1,0:T(8,128)(2,1)}), bf16[32,72,128]{2,1,0:T(8,128)(2,1)S(1)}, u32[]{:S(2)}, u32[]{:S(2)}) async-start(bf16[32,72,128]{2,1,0:T(8,128)(2,1)} %bitcast.71), calls=%async_computation | async-start | bytes 1179648 | tf_op jit(solution)/shard_map/all_to_all | solution.py:586
  25.1 10.7 %all-to-all-done = bf16[32,72,128]{2,1,0:T(8,128)(2,1)S(1)} async-done(((bf16[32,72,128]{2,1,0:T(8,128)(2,1)}), bf16[32,72,128]{2,1,0:T(8,128)(2,1)S(1)}, u32[]{:S(2)}, u32[]{:S(2)}) %all-to-all-start) | async-done | bytes 589856 | tf_op jit(solution)/shard_map/all_to_all | solution.py:586
  37.4 4.8 %all-to-all-start.1 = ((bf16[4,2,512,128]{3,2,1,0:T(8,128)(2,1)}), bf16[4,2,512,128]{3,2,1,0:T(8,128)(2,1)S(1)}, u32[]{:S(2)}, u32[]{:S(2)}) async-start(bf16[4,2,512,128]{3,2,1,0:T(8,128)(2,1)} %broadcast_in_dim.51), calls=%async_computation.1 | async-start | bytes 2097152 | tf_op jit(solution)/shard_map/all_to_all | solution.py:586
  45.9 10.4 %all-to-all-done.1.x_hbm = bf16[4,2,512,128]{3,2,1,0:T(8,128)(2,1)S(1)} async-done(((bf16[4,2,512,128]{3,2,1,0:T(8,128)(2,1)}), bf16[4,2,512,128]{3,2,1,0:T(8,128)(2,1)S(1)}, u32[]{:S(2)}, u32[]{:S(2)}) %all-to-all-start.1) | async-done | bytes 1048608 | tf_op jit(solution)/shard_map/all_to_all | solution.py:586
  56.3 3.5 %collective-permute-start.1 = (bf16[2,512,128]{2,1,0:T(8,128)(2,1)S(1)}, bf16[2,512,128]{2,1,0:T(8,128)(2,1)S(1)}, u32[]{:S(2)}, u32[]{:S(2)}) collective-permute-start(bf16[2,512,128]{2,1,0:T(8,128)(2,1)S(1)} %bitcast.61), channel_id=1, source_target_pairs={{0,2},{1,3},{2,0},{3,1},{8,10},{9,11},{10,8},{11,9},{4,6},{5,7},{6... | collective-permute-start | bytes 786440 | tf_op jit(solution)/shard_map/ppermute | solution.py:53
  61.3 9.9 %shard_map.256 = (bf16[4,2,512,128]{3,2,1,0:T(8,128)(2,1)}, bf16[512,1024]{1,0:T(8,128)(2,1)}, bf16[512,1024]{1,0:T(8,128)(2,1)}, f32[2,512,384]{2,1,0:T(8,128)}...) custom-call(bf16[4,2,512,128]{3,2,1,0:T(8,128)(2,1)} %copy-done.5, ...), custom_call_target="tpu_custom_call" | custom-call | flops 50331648 | bytes 262144 | tf_op jit(solution)/shard_map/pallas_call | solution.py:74
  71.4 18.9 %all_to_all.35.got_ref = bf16[4,2,512,128]{3,2,1,0:T(8,128)(2,1)S(1)} all-to-all(bf16[4,2,512,128]{3,2,1,0:T(8,128)(2,1)} %get-tuple-element.80), channel_id=1, replica_groups={{0,1,2,3},{4,5,6,7},{8,9,10,11},{12,13,14,15},{16,17,18,19},{20,21,22,2..., dimensions={0} | all-to-all | bytes 2097152 | tf_op jit(solution)/shard_map/all_to_all | solution.py:586
  91.4 5.0 %all-to-all-start.3 = ((bf16[4,2,512,128]{3,2,1,0:T(8,128)(2,1)}), bf16[4,2,512,128]{3,2,1,0:T(8,128)(2,1)S(1)}, u32[]{:S(2)}, u32[]{:S(2)}) async-start(bf16[4,2,512,128]{3,2,1,0:T(8,128)(2,1)} %shard_map.257), calls=%async_computation.3 | async-start | bytes 2097152 | tf_op jit(solution)/shard_map/all_to_all | solution.py:586
  97.0 12.3 %all-to-all-done.3.h_hbm = bf16[4,2,512,128]{3,2,1,0:T(8,128)(2,1)S(1)} async-done(((bf16[4,2,512,128]{3,2,1,0:T(8,128)(2,1)}), bf16[4,2,512,128]{3,2,1,0:T(8,128)(2,1)S(1)}, u32[]{:S(2)}, u32[]{:S(2)}) %all-to-all-start.3) | async-done | bytes 1048608 | tf_op jit(solution)/shard_map/all_to_all | solution.py:586
  110.2 12.4 %shard_map.258 = (bf16[4,2,512,128]{3,2,1,0:T(8,128)(2,1)}, bf16[512,1024]{1,0:T(8,128)(2,1)}, bf16[512,1024]{1,0:T(8,128)(2,1)}, bf16[2,512,384]{2,1,0:T(8,128)...) custom-call(s32[4]{0:T(128)} %pad_add_fusion.where_ref, bf16[4,2,512,128]{3,2,1,0:T(8,128)(2,1)} %copy-done.3, ...), custom_call_target="tpu_custom_call" | custom-call | flops 83886080 | bytes 262144 | tf_op jit(solution)/shard_map/pallas_call | solution.py:74
  122.6 4.9 %all-to-all-start.4 = ((bf16[4,2,512,128]{3,2,1,0:T(8,128)(2,1)}), bf16[4,2,512,128]{3,2,1,0:T(8,128)(2,1)S(1)}, u32[]{:S(2)}, u32[]{:S(2)}) async-start(bf16[4,2,512,128]{3,2,1,0:T(8,128)(2,1)} %get-tuple-element.85), calls=%async_computation.4 | async-start | bytes 2097152 | tf_op jit(solution)/shard_map/all_to_all | solution.py:586
  127.5 8.5 %shard_map.259 = (bf16[4,2,512,128]{3,2,1,0:T(8,128)(2,1)}, bf16[16,64,1152]{2,1,0:T(8,128)(2,1)}, bf16[16,64,1152]{2,1,0:T(8,128)(2,1)}) custom-call(s32[4]{0:T(128)} %pad_add_fusion.where_ref, bf16[2,512,384]{2,1,0:T(8,128)(2,1)} %get-tuple-element.86.hid_hbm, bf16[2,512,768]{2,1,0:T(8,128)(2,1)} %get-tuple-element.87.dgu_hbm, ...), custom_call_target="tpu_custom_call" | custom-call | flops 67108864 | bytes 262144 | tf_op jit(solution)/shard_map/pallas_call | solution.py:74
  136.0 5.1 %all-to-all-done.4.got_ref = bf16[4,2,512,128]{3,2,1,0:T(8,128)(2,1)S(1)} async-done(((bf16[4,2,512,128]{3,2,1,0:T(8,128)(2,1)}), bf16[4,2,512,128]{3,2,1,0:T(8,128)(2,1)S(1)}, u32[]{:S(2)}, u32[]{:S(2)}) %all-to-all-start.4) | async-done | bytes 1048608 | tf_op jit(solution)/shard_map/all_to_all | solution.py:586
  142.3 5.0 %all-to-all-start.5 = ((bf16[4,2,512,128]{3,2,1,0:T(8,128)(2,1)}), bf16[4,2,512,128]{3,2,1,0:T(8,128)(2,1)S(1)}, u32[]{:S(2)}, u32[]{:S(2)}) async-start(bf16[4,2,512,128]{3,2,1,0:T(8,128)(2,1)} %shard_map.260), calls=%async_computation.5 | async-start | bytes 2097152 | tf_op jit(solution)/shard_map/all_to_all | solution.py:586
  147.3 3.8 %add_bitcast_fusion = (f32[4,64,1152]{2,1,0:T(8,128)S(1)}, bf16[4,64,1152]{2,1,0:T(8,128)(2,1)S(1)}, bf16[4,64,1152]{2,1,0:T(8,128)(2,1)S(1)}, bf16[4,64,1152]{2,1,0:T(8,128)(2,1)}) fusion(bf16[4,4,64,1152]{3,2,1,0:T(8,128)(2,1)} %bitcast.18, s32[]{:T(128)S(6)} %select_n.199, bf16[4,4,64,1152]{3,2,1,0:T(8,128)(2,1)} %bitcast.72, s32[]{:T(128)S(6)} %select_n.197, ...), kind=kLoop, calls=%fused_computation.1 | loop fusion | flops 4423680 | bytes 7667728 | tf_op jit(solution)/shard_map/add | solution.py:607
  155.4 6.4 %all-to-all-done.5.d_hbm = bf16[4,2,512,128]{3,2,1,0:T(8,128)(2,1)S(1)} async-done(((bf16[4,2,512,128]{3,2,1,0:T(8,128)(2,1)}), bf16[4,2,512,128]{3,2,1,0:T(8,128)(2,1)S(1)}, u32[]{:S(2)}, u32[]{:S(2)}) %all-to-all-start.5) | async-done | bytes 1048608 | tf_op jit(solution)/shard_map/all_to_all | solution.py:586
  162.9 16.2 %shard_map.261 = (bf16[4,2,16,2,32,128]{5,4,3,2,1,0:T(8,128)(2,1)}, bf16[16,64,768]{2,1,0:T(8,128)(2,1)}, bf16[16,64,768]{2,1,0:T(8,128)(2,1)}, f32[8,768]{1,0:T(8,128)}) custom-call(s32[4]{0:T(128)} %pad_add_fusion.where_ref, bf16[4,2,512,128]{3,2,1,0:T(8,128)(2,1)} %copy-done.4, bf16[8,2,2,64,768]{4,3,2,1,0:T(8,128)(2,1)} %bitcast.70, ...), custom_call_target="tpu_custom_call" | custom-call | flops 117440512 | bytes 524288 | tf_op jit(solution)/shard_map/pallas_call | solution.py:74
  183.5 3.3 %collective-permute-start.9 = (f32[8,768]{1,0:T(8,128)S(1)}, f32[8,768]{1,0:T(8,128)S(1)}, u32[]{:S(2)}, u32[]{:S(2)}) collective-permute-start(f32[8,768]{1,0:T(8,128)S(1)} %copy-done.11), channel_id=1, source_target_pairs={{0,2},{1,3},{2,0},{3,1},{8,10},{9,11},{10,8},{11,9},{4,6},{5,7},{6... | collective-permute-start | bytes 73736 | tf_op jit(solution)/shard_map/ppermute | solution.py:53
  194.2 2.9 %collective-permute-start.13 = (bf16[4,72,768]{2,1,0:T(8,128)(2,1)}, bf16[4,72,768]{2,1,0:T(8,128)(2,1)}, u32[]{:S(2)}, u32[]{:S(2)}) collective-permute-start(bf16[4,72,768]{2,1,0:T(8,128)(2,1)} %get-tuple-element.118), channel_id=1, source_target_pairs={{0,64},{1,65},{2,66},{3,67},{8,72},{9,73},{10,74},{11,75},{4,68},{... | collective-permute-start | bytes 1327112 | tf_op jit(solution)/shard_map/ppermute | solution.py:53
  202.9 3.4 %collective-permute-done.15 = bf16[64,1152]{1,0:T(8,128)(2,1)S(1)} collective-permute-done((bf16[64,1152]{1,0:T(8,128)(2,1)S(1)}, bf16[64,1152]{1,0:T(8,128)(2,1)S(1)}, u32[]{:S(2)}, u32[]{:S(2)}) %collective-permute-start.15) | collective-permute-done | bytes 147488 | tf_op jit(solution)/shard_map/ppermute | solution.py:53
  209.7 7.3 %all-to-all-start.6 = ((bf16[32,64,128]{2,1,0:T(8,128)(2,1)}), bf16[32,64,128]{2,1,0:T(8,128)(2,1)S(1)}, u32[]{:S(2)}, u32[]{:S(2)}) async-start(bf16[32,64,128]{2,1,0:T(8,128)(2,1)} %bitcast.78), calls=%async_computation.7 | async-start | bytes 1048576 | tf_op jit(solution)/shard_map/all_to_all | solution.py:586
  217.2 11.4 %all-to-all-done.6 = bf16[32,64,128]{2,1,0:T(8,128)(2,1)S(1)} async-done(((bf16[32,64,128]{2,1,0:T(8,128)(2,1)}), bf16[32,64,128]{2,1,0:T(8,128)(2,1)S(1)}, u32[]{:S(2)}, u32[]{:S(2)}) %all-to-all-start.6) | async-done | bytes 524320 | tf_op jit(solution)/shard_map/all_to_all | solution.py:586
  235.2 3.4 %shard_map.262 = (bf16[2,512,128]{2,1,0:T(8,128)(2,1)}, bf16[2,512,128]{2,1,0:T(8,128)(2,1)}) custom-call(s32[2,512]{1,0:T(2,128)} %route_ref.3, bf16[2,16,64,128]{3,2,1,0:T(8,128)(2,1)} %bitcast.75), custom_call_target="tpu_custom_call" | custom-call | flops 4194304 | bytes 32768 | tf_op jit(solution)/shard_map/pallas_call | solution.py:74
  (133 shorter events, 51.1 us)
Async XLA Ops:
  7.2 54.1 %all-gather.5.cloned.1.call-start = ((), (), s32[]{:S(2)}) async-start(), calls=%async_computation.9 | async-start | bytes 3244032 | tf_op jit(solution)/shard_map/all_gather | solution.py:569
  8.7 101.2 %all-gather.7.cloned.1.call-start = ((), (), s32[]{:S(2)}) async-start(), calls=%async_computation.10 | async-start | bytes 4866048 | tf_op jit(solution)/shard_map/all_gather | solution.py:569
  14.0 21.7 %all-to-all-start = ((bf16[32,72,128]{2,1,0:T(8,128)(2,1)}), bf16[32,72,128]{2,1,0:T(8,128)(2,1)S(1)}, u32[]{:S(2)}, u32[]{:S(2)}) async-start(bf16[32,72,128]{2,1,0:T(8,128)(2,1)} %bitcast.71), calls=%async_computation | async-start | bytes 1179648 | tf_op jit(solution)/shard_map/all_to_all | solution.py:586
  37.4 18.9 %all-to-all-start.1 = ((bf16[4,2,512,128]{3,2,1,0:T(8,128)(2,1)}), bf16[4,2,512,128]{3,2,1,0:T(8,128)(2,1)S(1)}, u32[]{:S(2)}, u32[]{:S(2)}) async-start(bf16[4,2,512,128]{3,2,1,0:T(8,128)(2,1)} %broadcast_in_dim.51), calls=%async_computation.1 | async-start | bytes 2097152 | tf_op jit(solution)/shard_map/all_to_all | solution.py:586
  56.3 15.0 %collective-permute-start = (bf16[2,512,128]{2,1,0:T(8,128)(2,1)S(1)}, bf16[2,512,128]{2,1,0:T(8,128)(2,1)S(1)}, u32[]{:S(2)}, u32[]{:S(2)}) collective-permute-start(bf16[2,512,128]{2,1,0:T(8,128)(2,1)S(1)} %bitcast.60), channel_id=1, source_target_pairs={{0,1},{1,2},{2,3},{3,0},{8,9},{9,10},{10,11},{11,8},{4,5},{5,6},{6... | collective-permute-start | bytes 786440 | tf_op jit(solution)/shard_map/ppermute | solution.py:53
  56.3 15.0 %collective-permute-start.1 = (bf16[2,512,128]{2,1,0:T(8,128)(2,1)S(1)}, bf16[2,512,128]{2,1,0:T(8,128)(2,1)S(1)}, u32[]{:S(2)}, u32[]{:S(2)}) collective-permute-start(bf16[2,512,128]{2,1,0:T(8,128)(2,1)S(1)} %bitcast.61), channel_id=1, source_target_pairs={{0,2},{1,3},{2,0},{3,1},{8,10},{9,11},{10,8},{11,9},{4,6},{5,7},{6... | collective-permute-start | bytes 786440 | tf_op jit(solution)/shard_map/ppermute | solution.py:53
  59.8 11.5 %collective-permute-start.2 = (bf16[2,512,128]{2,1,0:T(8,128)(2,1)S(1)}, bf16[2,512,128]{2,1,0:T(8,128)(2,1)S(1)}, u32[]{:S(2)}, u32[]{:S(2)}) collective-permute-start(bf16[2,512,128]{2,1,0:T(8,128)(2,1)S(1)} %bitcast.62), channel_id=1, source_target_pairs={{0,3},{1,0},{2,1},{3,2},{8,11},{9,8},{10,9},{11,10},{4,7},{5,4},{6... | collective-permute-start | bytes 786440 | tf_op jit(solution)/shard_map/ppermute | solution.py:53
  91.4 17.8 %all-to-all-start.3 = ((bf16[4,2,512,128]{3,2,1,0:T(8,128)(2,1)}), bf16[4,2,512,128]{3,2,1,0:T(8,128)(2,1)S(1)}, u32[]{:S(2)}, u32[]{:S(2)}) async-start(bf16[4,2,512,128]{3,2,1,0:T(8,128)(2,1)} %shard_map.257), calls=%async_computation.3 | async-start | bytes 2097152 | tf_op jit(solution)/shard_map/all_to_all | solution.py:586
  122.6 18.6 %all-to-all-start.4 = ((bf16[4,2,512,128]{3,2,1,0:T(8,128)(2,1)}), bf16[4,2,512,128]{3,2,1,0:T(8,128)(2,1)S(1)}, u32[]{:S(2)}, u32[]{:S(2)}) async-start(bf16[4,2,512,128]{3,2,1,0:T(8,128)(2,1)} %get-tuple-element.85), calls=%async_computation.4 | async-start | bytes 2097152 | tf_op jit(solution)/shard_map/all_to_all | solution.py:586
  142.3 19.5 %all-to-all-start.5 = ((bf16[4,2,512,128]{3,2,1,0:T(8,128)(2,1)}), bf16[4,2,512,128]{3,2,1,0:T(8,128)(2,1)S(1)}, u32[]{:S(2)}, u32[]{:S(2)}) async-start(bf16[4,2,512,128]{3,2,1,0:T(8,128)(2,1)} %shard_map.260), calls=%async_computation.5 | async-start | bytes 2097152 | tf_op jit(solution)/shard_map/all_to_all | solution.py:586
  147.2 62.5 %reduce-scatter.2.cloned.1.call-start = ((), (), s32[]{:S(2)}) async-start(), calls=%async_computation.8 | async-start | bytes 2621440 | tf_op jit(solution)/shard_map/reduce_scatter | solution.py:762
  151.0 28.0 %collective-permute-start.4 = (bf16[4,64,1152]{2,1,0:T(8,128)(2,1)}, bf16[4,64,1152]{2,1,0:T(8,128)(2,1)}, u32[]{:S(2)}, u32[]{:S(2)}) collective-permute-start(bf16[4,64,1152]{2,1,0:T(8,128)(2,1)} %get-tuple-element.142), channel_id=1, source_target_pairs={{0,32},{1,33},{2,34},{3,35},{8,40},{9,41},{10,42},{11,43},{4,36},{... | collective-permute-start | bytes 1769480 | tf_op jit(solution)/shard_map/ppermute | solution.py:53
  152.2 29.1 %collective-permute-start.5 = (bf16[4,64,1152]{2,1,0:T(8,128)(2,1)S(1)}, bf16[4,64,1152]{2,1,0:T(8,128)(2,1)}, u32[]{:S(2)}, u32[]{:S(2)}) collective-permute-start(bf16[4,64,1152]{2,1,0:T(8,128)(2,1)S(1)} %get-tuple-element.141), channel_id=1, source_target_pairs={{0,64},{1,65},{2,66},{3,67},{8,72},{9,73},{10,74},{11,75},{4,68},{... | collective-permute-start | bytes 1769480 | tf_op jit(solution)/shard_map/ppermute | solution.py:53
  154.9 26.4 %collective-permute-start.6 = (bf16[4,64,1152]{2,1,0:T(8,128)(2,1)S(1)}, bf16[4,64,1152]{2,1,0:T(8,128)(2,1)}, u32[]{:S(2)}, u32[]{:S(2)}) collective-permute-start(bf16[4,64,1152]{2,1,0:T(8,128)(2,1)S(1)} %get-tuple-element.140), channel_id=1, source_target_pairs={{0,96},{1,97},{2,98},{3,99},{8,104},{9,105},{10,106},{11,107},{4,1... | collective-permute-start | bytes 1769480 | tf_op jit(solution)/shard_map/ppermute | solution.py:53
  181.3 8.8 %collective-permute-start.7 = (bf16[16,64,768]{2,1,0:T(8,128)(2,1)}, bf16[16,64,768]{2,1,0:T(8,128)(2,1)}, u32[]{:S(2)}, u32[]{:S(2)}) collective-permute-start(bf16[16,64,768]{2,1,0:T(8,128)(2,1)} %get-tuple-element.112), channel_id=1, source_target_pairs={{0,8},{1,9},{2,10},{3,11},{8,0},{9,1},{10,2},{11,3},{4,12},{5,13},... | collective-permute-start | bytes 4718600 | tf_op jit(solution)/shard_map/ppermute | solution.py:53
  193.1 24.0 %collective-permute-start.12 = (bf16[4,72,768]{2,1,0:T(8,128)(2,1)}, bf16[4,72,768]{2,1,0:T(8,128)(2,1)}, u32[]{:S(2)}, u32[]{:S(2)}) collective-permute-start(bf16[4,72,768]{2,1,0:T(8,128)(2,1)} %get-tuple-element.117), channel_id=1, source_target_pairs={{0,32},{1,33},{2,34},{3,35},{8,40},{9,41},{10,42},{11,43},{4,36},{... | collective-permute-start | bytes 1327112 | tf_op jit(solution)/shard_map/ppermute | solution.py:53
  194.2 22.9 %collective-permute-start.13 = (bf16[4,72,768]{2,1,0:T(8,128)(2,1)}, bf16[4,72,768]{2,1,0:T(8,128)(2,1)}, u32[]{:S(2)}, u32[]{:S(2)}) collective-permute-start(bf16[4,72,768]{2,1,0:T(8,128)(2,1)} %get-tuple-element.118), channel_id=1, source_target_pairs={{0,64},{1,65},{2,66},{3,67},{8,72},{9,73},{10,74},{11,75},{4,68},{... | collective-permute-start | bytes 1327112 | tf_op jit(solution)/shard_map/ppermute | solution.py:53
  197.1 20.0 %collective-permute-start.14 = (bf16[4,72,768]{2,1,0:T(8,128)(2,1)}, bf16[4,72,768]{2,1,0:T(8,128)(2,1)}, u32[]{:S(2)}, u32[]{:S(2)}) collective-permute-start(bf16[4,72,768]{2,1,0:T(8,128)(2,1)} %get-tuple-element.119), channel_id=1, source_target_pairs={{0,96},{1,97},{2,98},{3,99},{8,104},{9,105},{10,106},{11,107},{4,1... | collective-permute-start | bytes 1327112 | tf_op jit(solution)/shard_map/ppermute | solution.py:53
  199.0 7.3 %collective-permute-start.15 = (bf16[64,1152]{1,0:T(8,128)(2,1)S(1)}, bf16[64,1152]{1,0:T(8,128)(2,1)S(1)}, u32[]{:S(2)}, u32[]{:S(2)}) collective-permute-start(bf16[64,1152]{1,0:T(8,128)(2,1)S(1)} %get-tuple-element.149), channel_id=1, source_target_pairs={{0,4},{1,5},{2,6},{3,7},{8,12},{9,13},{10,14},{11,15},{4,16},{5,17... | collective-permute-start | bytes 442376 | tf_op jit(solution)/shard_map/ppermute | solution.py:53
  200.3 16.7 %collective-permute-start.16 = (bf16[64,1152]{1,0:T(8,128)(2,1)S(1)}, bf16[64,1152]{1,0:T(8,128)(2,1)S(1)}, u32[]{:S(2)}, u32[]{:S(2)}) collective-permute-start(bf16[64,1152]{1,0:T(8,128)(2,1)S(1)} %get-tuple-element.148), channel_id=1, source_target_pairs={{0,16},{1,17},{2,18},{3,19},{8,24},{9,25},{10,26},{11,27},{4,20},{... | collective-permute-start | bytes 442376 | tf_op jit(solution)/shard_map/ppermute | solution.py:53
  206.4 10.7 %collective-permute-start.17 = (bf16[64,1152]{1,0:T(8,128)(2,1)S(1)}, bf16[64,1152]{1,0:T(8,128)(2,1)S(1)}, u32[]{:S(2)}, u32[]{:S(2)}) collective-permute-start(bf16[64,1152]{1,0:T(8,128)(2,1)S(1)} %get-tuple-element.147), channel_id=1, source_target_pairs={{0,20},{1,21},{2,22},{3,23},{8,28},{9,29},{10,30},{11,31},{4,0},{5... | collective-permute-start | bytes 442376 | tf_op jit(solution)/shard_map/ppermute | solution.py:53
  209.7 18.9 %all-to-all-start.6 = ((bf16[32,64,128]{2,1,0:T(8,128)(2,1)}), bf16[32,64,128]{2,1,0:T(8,128)(2,1)S(1)}, u32[]{:S(2)}, u32[]{:S(2)}) async-start(bf16[32,64,128]{2,1,0:T(8,128)(2,1)} %bitcast.78), calls=%async_computation.7 | async-start | bytes 1048576 | tf_op jit(solution)/shard_map/all_to_all | solution.py:586
  230.3 8.8 %collective-permute-start.18 = (bf16[72,768]{1,0:T(8,128)(2,1)S(1)}, bf16[72,768]{1,0:T(8,128)(2,1)S(1)}, u32[]{:S(2)}, u32[]{:S(2)}) collective-permute-start(bf16[72,768]{1,0:T(8,128)(2,1)S(1)} %get-tuple-element.150), channel_id=1, source_target_pairs={{0,4},{1,5},{2,6},{3,7},{8,12},{9,13},{10,14},{11,15},{4,16},{5,17... | collective-permute-start | bytes 331784 | tf_op jit(solution)/shard_map/ppermute | solution.py:53
  231.0 8.1 %collective-permute-start.19 = (bf16[72,768]{1,0:T(8,128)(2,1)S(1)}, bf16[72,768]{1,0:T(8,128)(2,1)S(1)}, u32[]{:S(2)}, u32[]{:S(2)}) collective-permute-start(bf16[72,768]{1,0:T(8,128)(2,1)S(1)} %get-tuple-element.152), channel_id=1, source_target_pairs={{0,16},{1,17},{2,18},{3,19},{8,24},{9,25},{10,26},{11,27},{4,20},{... | collective-permute-start | bytes 331784 | tf_op jit(solution)/shard_map/ppermute | solution.py:53
  (23 other events, 249.9 us)
Sparse Core Ops, SparseCore 0:
  10.9 50.4 all-gather.4
  63.6 46.2 all-gather.6
  181.4 28.2 reduce-scatter.1
